TPU v7x, 512 devices: a whole 4x8x8 slice. The times are simulated.
512 devices in a mesh: seq: 128 (over x, y, z_lo, core), head: 4 (over z_hi).
Axes of the slice: x: 4, y: 8, z: 8 (z_hi: 4, z_lo: 2; z = z_hi * 2 + z_lo), core: 2. Of those that a mesh axis runs over, the one named last changes fastest.
Arguments:
- queries: bfloat16 [128, 8192], P('seq', 'head'), may hold values from -130 to 130
- grad_output: bfloat16 [128, 8192], P('seq', 'head'), may hold values from -384 to 384
- key_cache: bfloat16 [49152, 512], P('seq', 'head'), may hold values from -6 to 6
- saved_value_rows: bfloat16 [49152, 512], P('seq', 'head'), may hold values from -6 to 6
- lengths: int32 [128], P('seq'), may hold values from 1 to 384, 36864 in all
- span_index: int32 [1], replicated, may hold values from 72 to 287
- w_query: bfloat16 [4096, 8192], P('seq', 'head'), may hold values from -0.09375 to 0.09375
- key_projection_weight: bfloat16 [4096, 512], P(None, 'head'), may hold values from -0.09375 to 0.09375
- value_projection_weight: bfloat16 [4096, 512], P(None, 'head'), may hold values from -0.09375 to 0.09375
Outputs:
- saved_key_gradient: bfloat16 [49152, 512], P('seq', 'head')
- saved_value_gradient: bfloat16 [49152, 512], P('seq', 'head')
- cached_input_gradient: bfloat16 [49152, 4096], P('seq', 'head')
- grad_span_input: bfloat16 [128, 4096], P('head', 'seq')
All inputs are finite; a program needn't handle non-finite values. No bound on the sum of `lengths` on one device may be relied on, other than what follows from the above.
Results may differ from a plain program's by a relative error of at most 0.02.
Values may be sent and summed in bfloat16 or wider, within the bound.
No kernel may reach another device: no remote copies, remote signals or barrier semaphores. Data moves between devices by JAX's collectives and lax.ppermute only.
A program may use at most 64 MiB of HBM per device.

v0:
```python
import jax
import jax.numpy as jnp
from jax import lax
from jax.sharding import Mesh
from jax.sharding import PartitionSpec as P

HEAD_WIDTH = 128
SEQ = ("seq_0", "seq_1", "seq_2", "seq_3")


LOWEST_SCORE = -1e30


def filled_with(value, identity):
    return jnp.broadcast_to(jnp.asarray(identity, value.dtype), value.shape)


def prefix_by_axis(value, axes, combine, identity):
    before = start = filled_with(value, identity)
    total = value
    for axis in reversed(axes):
        count, here = (lax.axis_size(axis), lax.axis_index(axis))
        pieces = lax.all_gather(total, axis)
        inside, total = (start, start)
        for k in range(count):
            passed = k < here
            total = combine(total, pieces[k])
            inside = jnp.where(passed, total, inside)
        before = combine(inside, before)
    return before


def side_by_side(arrays, axis, dim, along):
    both = jnp.concatenate(arrays, axis=along)
    whole, at, gathered = (lax.all_gather(both, axis, axis=dim, tiled=True), 0, [])
    for a in arrays:
        gathered.append(lax.slice_in_dim(whole, at, at + a.shape[along], axis=along))
        at += a.shape[along]
    return tuple(gathered)


def collected_together(value, axis):
    leaves = jax.tree.leaves(value)
    turns = sorted(range(len(leaves)), key=lambda k: -leaves[k].size)
    width = (1, *leaves[turns[0]].shape)[-1]
    lines = [
        jnp.pad(leaves[k].reshape(-1), (0, -leaves[k].size % width)).reshape(-1, width)
        for k in turns
    ]
    both, at, found = (lax.all_gather(jnp.concatenate(lines), axis), 0, {})
    for k, line in zip(turns, lines):
        section = both[:, at : at + len(line)].reshape(len(both), -1)
        found[k] = section[:, : leaves[k].size].reshape(-1, *leaves[k].shape)
        at += len(line)
    numbers = iter(range(len(leaves)))
    return jax.tree.map(lambda _: found[next(numbers)], value)


def merged_by_axis(value, axes, combine):
    for axis in axes:
        pieces = collected_together(value, axis)
        value = jax.tree.map(lambda part: part[0], pieces)
        for k in range(1, lax.axis_size(axis)):
            value = combine(value, jax.tree.map(lambda part: part[k], pieces))
    return value


def cut_along(value, dim, count):
    before, after = (value.shape[:dim], value.shape[dim + 1 :])
    return jnp.moveaxis(value.reshape(*before, count, -1, *after), dim, 0)


def summed_on_arrival(value, axis, dim):
    tiles = cut_along(value, dim, lax.axis_size(axis))
    arrived = lax.all_to_all(tiles, axis, split_axis=0, concat_axis=0, tiled=True)
    return arrived.sum(axis=0)


def summed_rows(value, axes, dim):
    far, near = axes
    tiles = cut_along(value, dim, lax.axis_size(far))
    nearer = summed_on_arrival(tiles, near, dim + 1)
    arrived = lax.all_to_all(nearer, far, split_axis=0, concat_axis=0, tiled=True)
    return arrived.sum(axis=0)


def padded_to(lines, count):
    spare = -lines.shape[0] % count
    if not spare:
        return lines
    return jnp.concatenate([lines, jnp.zeros((spare, *lines.shape[1:]), lines.dtype)])


def copy_for_each(value, axis):
    copies = jnp.broadcast_to(value, (lax.axis_size(axis), *value.shape))
    return lax.all_to_all(copies, axis, split_axis=0, concat_axis=0, tiled=True)


def laid_out(tiles, dim):
    tiles = jnp.moveaxis(tiles, 0, dim)
    lengths = tiles.shape
    return tiles.reshape(*lengths[:dim], lengths[dim] * lengths[dim + 1], *lengths[dim + 2 :])


def whole_of(value, axes, dim):
    far, near = axes
    tiles = copy_for_each(copy_for_each(value, far), near)
    return laid_out(tiles.swapaxes(0, 1).reshape(-1, *value.shape), dim)


def sum_by_parts(value, axes):
    lines = value.reshape(-1, value.shape[-1])
    own = summed_rows(padded_to(lines, lax.axis_size(axes[0]) * lax.axis_size(axes[1])), axes, 0)
    whole = whole_of(own, axes, 0)
    return whole[: len(lines)].reshape(value.shape)


def gathered_copies(value, axis, dim):
    return laid_out(copy_for_each(value, axis), dim)


def in_one_piece(arrays, axis, dim, along):
    widths = [a.shape[along] for a in arrays]
    both = jnp.concatenate(arrays, axis=along)
    whole = gathered_copies(both, axis, dim)
    return tuple(jnp.split(whole, [sum(widths[:k]) for k in range(1, len(widths))], axis=along))


def add_counts(earlier, later):
    return earlier + later


def triple_merge(first, second):
    joined_peak = jnp.maximum(first[0], second[0])
    first_factor = jnp.exp(first[0] - joined_peak)
    second_factor = jnp.exp(second[0] - joined_peak)
    return (
        joined_peak,
        first[1] * first_factor + second[1] * second_factor,
        first[2] * first_factor + second[2] * second_factor,
    )


def local(
    queries,
    grad_output,
    key_cache,
    saved_value_rows,
    lengths,
    span_index,
    w_query,
    key_projection_weight,
    value_projection_weight,
):
    score_scale = HEAD_WIDTH ** (-0.5)
    offset = prefix_by_axis(lengths, SEQ, add_counts, jnp.zeros((1,), jnp.int32))
    query_all, grad_all = side_by_side((queries, grad_output), SEQ, 0, 1)
    row_count = query_all.shape[0]
    block_size = key_cache.shape[0]
    heads_per_group = query_all.shape[1] // HEAD_WIDTH
    within = jnp.arange(block_size, dtype=jnp.int32)
    query_positions = span_index[0] * row_count + jnp.arange(row_count, dtype=jnp.int32)
    visible = (within < lengths[0])[None, :] & (
        (offset[0] + within)[None, :] <= query_positions[:, None]
    )
    visible = visible[None, :, :]
    query_heads = query_all.reshape(row_count, heads_per_group, HEAD_WIDTH)
    grad_heads = grad_all.reshape(row_count, heads_per_group, HEAD_WIDTH)
    scores = (
        jnp.einsum("ihd,pd->hip", query_heads, key_cache, preferred_element_type=jnp.float32)
        * score_scale
    )
    weight_grads = jnp.einsum(
        "ihd,pd->hip", grad_heads, saved_value_rows, preferred_element_type=jnp.float32
    )
    local_peak = jnp.max(jnp.where(visible, scores, LOWEST_SCORE), axis=2)
    local_exp = jnp.exp(jnp.where(visible, scores - local_peak[:, :, None], LOWEST_SCORE))
    local_total = jnp.sum(local_exp, axis=2)
    local_weighted = jnp.sum(local_exp * weight_grads, axis=2)
    row_peak, row_total, row_weighted = merged_by_axis(
        (local_peak, local_total, local_weighted), SEQ, triple_merge
    )
    weights = (
        jnp.exp(jnp.where(visible, scores - row_peak[:, :, None], LOWEST_SCORE))
        / row_total[:, :, None]
    )
    row_terms = row_weighted / row_total
    score_grads = weights * (weight_grads - row_terms[:, :, None])
    weights_low = weights.astype(jnp.bfloat16)
    score_low = score_grads.astype(jnp.bfloat16)
    value_grads = jnp.einsum(
        "hip,ihd->pd", weights_low, grad_heads, preferred_element_type=jnp.float32
    )
    key_grads = (
        jnp.einsum("hip,ihd->pd", score_low, query_heads, preferred_element_type=jnp.float32)
        * score_scale
    )
    query_part = (
        jnp.einsum("hip,pd->ihd", score_low, key_cache, preferred_element_type=jnp.float32)
        * score_scale
    )
    query_sum = sum_by_parts(
        query_part.reshape(row_count, heads_per_group * HEAD_WIDTH),
        (("seq_0", "seq_1", "seq_2"), "seq_3"),
    )
    query_low = query_sum.astype(jnp.bfloat16)
    span_part = jnp.dot(query_low, w_query.T, preferred_element_type=jnp.float32)
    grad_span_input = summed_on_arrival(span_part, "head", 0).astype(jnp.bfloat16)
    saved_key_gradient = key_grads.astype(jnp.bfloat16)
    saved_value_gradient = value_grads.astype(jnp.bfloat16)
    key_weights, value_weights = (
        lax.all_to_all(key_projection_weight, "head", split_axis=0, concat_axis=1, tiled=True),
        lax.all_to_all(value_projection_weight, "head", split_axis=0, concat_axis=1, tiled=True),
    )
    key_all, value_all = in_one_piece((saved_key_gradient, saved_value_gradient), "head", 1, 0)
    total = jnp.zeros((block_size, key_weights.shape[0]), jnp.float32)
    for member in range(lax.axis_size("head")):
        first = member * HEAD_WIDTH
        both = jnp.concatenate(
            [key_all[:, first : first + HEAD_WIDTH], value_all[:, first : first + HEAD_WIDTH]],
            axis=1,
        )
        joined = jnp.concatenate(
            [
                key_weights[:, first : first + HEAD_WIDTH],
                value_weights[:, first : first + HEAD_WIDTH],
            ],
            axis=1,
        )
        partial_term = jnp.dot(both, joined.T, preferred_element_type=jnp.float32)
        rounded = lax.optimization_barrier(partial_term.astype(jnp.bfloat16))
        total = total + rounded.astype(jnp.float32)
    cached_input_gradient = total.astype(jnp.bfloat16)
    return (saved_key_gradient, saved_value_gradient, cached_input_gradient, grad_span_input)


def solution(mesh):
    split = Mesh(
        mesh.devices.reshape(4, 8, 2, 2, mesh.shape["head"]),
        ("seq_0", "seq_1", "seq_2", "seq_3", "head"),
    )
    in_specs = (
        P(SEQ, "head"),
        P(SEQ, "head"),
        P(SEQ, "head"),
        P(SEQ, "head"),
        P(SEQ),
        P(),
        P(SEQ, "head"),
        P(None, "head"),
        P(None, "head"),
    )
    out_specs = (P(SEQ, "head"), P(SEQ, "head"), P(SEQ, "head"), P("head", SEQ))
    return jax.shard_map(local, mesh=split, in_specs=in_specs, out_specs=out_specs, check_vma=False)
```

profile of v0, /device:TPU:1, one launch (start us, length us, event | category | flops | bytes accessed | tf_op | source)
XLA Modules:
  0.0 431.1 jit_solution(12880352429960061739)
XLA Ops:
  7.2 1.4 maximum_bitcast_fusion
  9.3 1.3 dynamic-slice
  10.5 0.8 dynamic-update-slice
  11.3 8.3 %all-reduce = s32[2]{0:T(128)S(1)} all-reduce(s32[2]{0:T(128)S(1)} %dynamic-update-slice), channel_id=2, replica_groups=mesh['seq_0'=4,'seq_1'=8,'seq_2'=2,'seq_3'=2,'head'=4] {'seq_3'}, use_global_device_ids=true, to_apply=%add | all-reduce | flops 2 | bytes 16
  19.6 1.3 dynamic-slice.1
  20.9 0.6 fusion.156
  21.5 1.4 dynamic-update-slice.1
  22.9 3.1 all-reduce.1
  26.0 1.3 dynamic-slice.2
  27.2 0.6 fusion.157
  27.9 1.4 dynamic-update-slice.2
  29.3 7.0 %all-reduce.2 = s32[8]{0:T(128)S(1)} all-reduce(s32[8]{0:T(128)S(1)} %dynamic-update-slice.2), channel_id=4, replica_groups=mesh['seq_0'=4,'seq_1'=8,'seq_2'=2,'seq_3'=2,'head'=4] {'seq_1'}, use_global_device_ids=true, to_apply=%add.2 | all-reduce | flops 8 | bytes 64
  36.3 1.3 dynamic-slice.3
  37.5 0.7 slice_add_fusion.3
  38.2 1.2 fusion.158
  39.4 1.3 slice_add_fusion
  40.8 1.4 dynamic-update-slice.3
  42.1 8.8 %all-to-all-start.1 = ((bf16[4,1024,128]{2,1,0:T(8,128)(2,1)}), bf16[4,1024,128]{2,1,0:T(8,128)(2,1)}, u32[]{:S(2)}, u32[]{:S(2)}) async-start(bf16[4,1024,128]{2,1,0:T(8,128)(2,1)} %bitcast.634), calls=%async_computation.1 | async-start | bytes 2097152 | tf_op jit(solution)/shard_map/all_to_all | solution.py:212
  51.0 7.3 %all-reduce.3 = s32[4]{0:T(128)S(1)} all-reduce(s32[4]{0:T(128)S(1)} %dynamic-update-slice.3), channel_id=5, replica_groups=mesh['seq_0'=4,'seq_1'=8,'seq_2'=2,'seq_3'=2,'head'=4] {'seq_0'}, use_global_device_ids=true, to_apply=%add.3 | all-reduce | flops 4 | bytes 32
  58.9 0.7 fusion.159
  70.3 161.3 %all-gather.11.cloned.1.call-done = bf16[128,1,4096]{2,1,0:T(2,128)(2,1)} async-done(((bf16[1,1,4096]{2,1,0:T(2,128)(2,1)}), bf16[128,1,4096]{2,1,0:T(2,128)(2,1)}) %all-gather.11.cloned.1.call-update) | async-done | bytes 1048592 | tf_op jit(solution)/shard_map/all_gather | solution.py:35
  231.6 2.7 copy.61
  234.5 1.0 copy.37
  235.5 1.0 copy.39
  236.5 1.9 fusion.3
  238.4 1.7 fusion.9
  240.1 9.8 %all-gather.4 = f32[192,128]{1,0:T(8,128)S(1)} all-gather(f32[48,128]{1,0:T(8,128)S(1)} %pad_maximum_fusion.1), channel_id=6, replica_groups=mesh['seq_0'=4,'seq_1'=8,'seq_2'=2,'seq_3'=2,'head'=4] {'seq_0'}, dimensions={0}, use_global_device_ids=true | all-gather | bytes 122880 | tf_op jit(solution)/shard_map/all_gather | solution.py:50
  250.0 19.5 %all-gather.5 = f32[384,128]{1,0:T(8,128)S(1)} all-gather(f32[48,128]{1,0:T(8,128)S(1)} %pad_maximum_fusion.2), channel_id=7, replica_groups=mesh['seq_0'=4,'seq_1'=8,'seq_2'=2,'seq_3'=2,'head'=4] {'seq_1'}, dimensions={0}, use_global_device_ids=true | all-gather | bytes 221184 | tf_op jit(solution)/shard_map/all_gather | solution.py:50
  269.6 3.3 all-gather.6
  273.0 12.7 %all-gather.7 = f32[96,128]{1,0:T(8,128)S(1)} all-gather(f32[48,128]{1,0:T(8,128)S(1)} %pad_maximum_fusion.4), channel_id=9, replica_groups=mesh['seq_0'=4,'seq_1'=8,'seq_2'=2,'seq_3'=2,'head'=4] {'seq_3'}, dimensions={0}, use_global_device_ids=true | all-gather | bytes 73728 | tf_op jit(solution)/shard_map/all_gather | solution.py:50
  285.7 1.2 fusion.2
  286.9 1.1 copy-done.1
  288.6 1.6 copy.48
  290.2 2.7 reshape_reshape_reshape.3
  292.9 2.8 copy.49
  295.8 6.6 %all_to_all.71 = f32[2,64,1,2048]{3,1,2,0:T(8,128)} all-to-all(f32[2,64,1,2048]{3,1,2,0:T(8,128)} %copy.49), channel_id=1, replica_groups=mesh['seq_0'=4,'seq_1'=8,'seq_2'=2,'seq_3'=2,'head'=4] {'seq_3'}, dimensions={0} | all-to-all | bytes 2097152 | tf_op jit(solution)/shard_map/all_to_all | solution.py:75
  302.4 6.6 %all-to-all-start.2 = ((bf16[4,1024,128]{2,1,0:T(8,128)(2,1)}), bf16[4,1024,128]{2,1,0:T(8,128)(2,1)}, u32[]{:S(2)}, u32[]{:S(2)}) async-start(bf16[4,1024,128]{2,1,0:T(8,128)(2,1)} %bitcast.635), calls=%async_computation.2 | async-start | bytes 2097152 | tf_op jit(solution)/shard_map/all_to_all | solution.py:213
  308.9 2.2 reduce_sum.49
  311.1 2.2 reduce_sum.50
  313.3 15.3 %all-to-all-done.2 = bf16[4,1024,128]{2,1,0:T(8,128)(2,1)} async-done(((bf16[4,1024,128]{2,1,0:T(8,128)(2,1)}), bf16[4,1024,128]{2,1,0:T(8,128)(2,1)}, u32[]{:S(2)}, u32[]{:S(2)}) %all-to-all-start.2) | async-done | bytes 1048608 | tf_op jit(solution)/shard_map/all_to_all | solution.py:213
  328.6 16.6 %all-to-all-start.4 = ((f32[64,1,2048]{2,1,0:T(1,128)}), f32[64,1,2048]{2,1,0:T(1,128)}, u32[]{:S(2)}, u32[]{:S(2)}) async-start(f32[64,1,2048]{2,1,0:T(1,128)} %reduce_sum.50), calls=%async_computation.4 | async-start | bytes 1048576 | tf_op jit(solution)/shard_map/all_to_all | solution.py:83
  345.3 2.1 fusion.20
  347.4 2.5 fusion.17
  349.9 0.6 copy-done.11
  350.7 9.2 %all-to-all-done.4 = f32[64,1,2048]{2,1,0:T(1,128)} async-done(((f32[64,1,2048]{2,1,0:T(1,128)}), f32[64,1,2048]{2,1,0:T(1,128)}, u32[]{:S(2)}, u32[]{:S(2)}) %all-to-all-start.4) | async-done | bytes 524320 | tf_op jit(solution)/shard_map/all_to_all | solution.py:83
  359.9 0.9 broadcast_in_dim.39
  360.9 3.5 all-to-all-start
  364.4 1.5 copy.46
  365.9 1.5 copy.47
  367.4 1.2 fusion.150
  368.5 1.4 reduce_sum.51
  370.7 2.2 reduce.2
  372.9 0.9 reshape.262
  373.8 8.1 %all-to-all-done = bf16[4,768,128]{1,2,0:T(8,128)(2,1)S(1)} async-done(((bf16[4,768,128]{1,2,0:T(8,128)(2,1)}), bf16[4,768,128]{1,2,0:T(8,128)(2,1)S(1)}, u32[]{:S(2)}, u32[]{:S(2)}) %all-to-all-start) | async-done | bytes 786464 | tf_op jit(solution)/shard_map/all_to_all | solution.py:96
  381.8 11.2 %all-to-all-start.5 = ((bf16[64,2,1024]{2,1,0:T(2,128)(2,1)}), bf16[64,2,1024]{2,1,0:T(2,128)(2,1)S(1)}, u32[]{:S(2)}, u32[]{:S(2)}) async-start(bf16[64,2,1024]{2,1,0:T(2,128)(2,1)} %reshape.262), calls=%async_computation.5 | async-start | bytes 524288 | tf_op jit(solution)/shard_map/all_to_all | solution.py:96
  394.5 1.3 convolution_convert_fusion
  395.8 7.2 %all-to-all-done.5 = bf16[64,2,1024]{2,1,0:T(2,128)(2,1)S(1)} async-done(((bf16[64,2,1024]{2,1,0:T(2,128)(2,1)}), bf16[64,2,1024]{2,1,0:T(2,128)(2,1)S(1)}, u32[]{:S(2)}, u32[]{:S(2)}) %all-to-all-start.5) | async-done | bytes 262176 | tf_op jit(solution)/shard_map/all_to_all | solution.py:96
  403.4 7.3 %all_to_all.72 = bf16[2,64,1,2048]{3,1,2,0:T(8,128)(2,1)S(1)} all-to-all(bf16[2,64,1,2048]{3,1,2,0:T(8,128)(2,1)S(1)} %broadcast_in_dim.41), channel_id=1, replica_groups=mesh['seq_0'=4,'seq_1'=8,'seq_2'=2,'seq_3'=2,'head'=4] {'seq_3'}, dimensions={0} | all-to-all | bytes 1048576 | tf_op jit(solution)/shard_map/all_to_all | solution.py:96
  411.8 0.7 reshape.264
  412.5 3.2 all-to-all-start.7
  415.7 2.6 add_convert_fusion
  418.3 4.0 all-to-all-done.7
  422.8 0.7 reduce.3
  423.6 0.6 reduce_sum.52
  (65 shorter events, 5.4 us)
Async XLA Ops:
  7.2 404.3 %copy-start = (bf16[32,2048]{1,0:T(8,128)(2,1)S(1)}, bf16[32,2048]{1,0:T(8,128)(2,1)}, u32[]{:S(2)}) copy-start(bf16[32,2048]{1,0:T(8,128)(2,1)} %param.15) | copy-start | bytes 393220
  7.2 224.4 %all-gather.11.cloned.1.call-start = ((), (), s32[]{:S(2)}) async-start(), calls=%async_computation.8 | async-start | bytes 2113536 | tf_op jit(solution)/shard_map/all_gather | solution.py:35
  42.1 253.7 %all-to-all-start.1 = ((bf16[4,1024,128]{2,1,0:T(8,128)(2,1)}), bf16[4,1024,128]{2,1,0:T(8,128)(2,1)}, u32[]{:S(2)}, u32[]{:S(2)}) async-start(bf16[4,1024,128]{2,1,0:T(8,128)(2,1)} %bitcast.634), calls=%async_computation.1 | async-start | bytes 2097152 | tf_op jit(solution)/shard_map/all_to_all | solution.py:212
  70.3 166.2 %copy-start.3 = (bf16[384,128]{1,0:T(8,128)(2,1)S(1)}, bf16[384,128]{1,0:T(8,128)(2,1)}, u32[]{:S(2)}) copy-start(bf16[384,128]{1,0:T(8,128)(2,1)} %param.11) | copy-start | bytes 294916
  234.5 4.0 copy-start.12
  236.5 2.0 copy-start.2
  286.9 1.1 copy-start.1
  302.4 26.3 %all-to-all-start.2 = ((bf16[4,1024,128]{2,1,0:T(8,128)(2,1)}), bf16[4,1024,128]{2,1,0:T(8,128)(2,1)}, u32[]{:S(2)}, u32[]{:S(2)}) async-start(bf16[4,1024,128]{2,1,0:T(8,128)(2,1)} %bitcast.635), calls=%async_computation.2 | async-start | bytes 2097152 | tf_op jit(solution)/shard_map/all_to_all | solution.py:213
  328.6 31.3 %all-to-all-start.4 = ((f32[64,1,2048]{2,1,0:T(1,128)}), f32[64,1,2048]{2,1,0:T(1,128)}, u32[]{:S(2)}, u32[]{:S(2)}) async-start(f32[64,1,2048]{2,1,0:T(1,128)} %reduce_sum.50), calls=%async_computation.4 | async-start | bytes 1048576 | tf_op jit(solution)/shard_map/all_to_all | solution.py:83
  347.4 2.5 copy-start.10
  349.9 0.6 copy-start.11
  360.9 21.0 %all-to-all-start = ((bf16[4,768,128]{1,2,0:T(8,128)(2,1)}), bf16[4,768,128]{1,2,0:T(8,128)(2,1)S(1)}, u32[]{:S(2)}, u32[]{:S(2)}) async-start(bf16[4,768,128]{1,2,0:T(8,128)(2,1)} %broadcast_in_dim.39), calls=%async_computation | async-start | bytes 1572864 | tf_op jit(solution)/shard_map/all_to_all | solution.py:96
  368.5 24.8 %copy-start.8 = (bf16[1024,128]{0,1:T(8,128)(2,1)S(1)}, bf16[1024,128]{0,1:T(8,128)(2,1)}, u32[]{:S(2)}) copy-start(bf16[1024,128]{0,1:T(8,128)(2,1)} %get-tuple-element.16) | copy-start | bytes 786436
  372.9 20.4 %copy-start.9 = (bf16[1024,128]{0,1:T(8,128)(2,1)S(1)}, bf16[1024,128]{0,1:T(8,128)(2,1)}, u32[]{:S(2)}) copy-start(bf16[1024,128]{0,1:T(8,128)(2,1)} %get-tuple-element.63) | copy-start | bytes 786436
  381.8 21.1 %all-to-all-start.5 = ((bf16[64,2,1024]{2,1,0:T(2,128)(2,1)}), bf16[64,2,1024]{2,1,0:T(2,128)(2,1)S(1)}, u32[]{:S(2)}, u32[]{:S(2)}) async-start(bf16[64,2,1024]{2,1,0:T(2,128)(2,1)} %reshape.262), calls=%async_computation.5 | async-start | bytes 524288 | tf_op jit(solution)/shard_map/all_to_all | solution.py:96
  393.1 1.0 copy-start.6
  393.1 1.0 copy-start.7
  393.2 1.3 copy-start.4
  393.2 1.3 copy-start.5
  412.5 9.8 %all-to-all-start.7 = ((f32[4,1,1024]{2,1,0:T(1,128)}), f32[4,1,1024]{2,1,0:T(1,128)S(1)}, u32[]{:S(2)}, u32[]{:S(2)}) async-start(f32[4,1,1024]{2,1,0:T(1,128)} %reshape.264), calls=%async_computation.7 | async-start | bytes 32768 | tf_op jit(solution)/shard_map/all_to_all | solution.py:75
Sparse Core Ops, SparseCore 0:
  10.7 220.8 all-gather.10
where the time goes:
time: 433 us; the launch traced here: 431 us
  waiting for transfers between devices  205 us (47%)
  blocking collectives  85 us (20%)
  starting transfers between devices  50 us (12%)
  local copies, waits for them, and re-layouts  36.2 us (8%)
  between operations  26.4 us (6%)
  other arithmetic  17 us (4%)
  matrix products  11.5 us (3%)
    all_gather x1, waiting for transfers between devices, side_by_side(): lax.all_gather(both, axis, axis=dim, tiled=True)  161 us
    all_gather x4, blocking collectives, collected_together(): both, at, found = (lax.all_gather(jnp.concatenate(lines), axis), 0, {})  45.4 us
    unnamed x4, blocking collectives  25.7 us
    all_to_all x1, starting transfers between devices, summed_rows(): lax.all_to_all(nearer, far, split_axis=0, concat_axis=0, tiled=True)  16.6 us
    unnamed x44, local copies, waits for them, and re-layouts  16.6 us
    all_to_all x1, waiting for transfers between devices, local(): lax.all_to_all(value_projection_weight, 'head', split_axis=0, concat_axis...  15.3 us
    all_to_all x2, waiting for transfers between devices, copy_for_each(): return lax.all_to_all(copies, axis, split_axis=0, concat_axis=0, tiled=True)  15.2 us
    all_to_all x2, starting transfers between devices, copy_for_each(): return lax.all_to_all(copies, axis, split_axis=0, concat_axis=0, tiled=True)  14.7 us
  transfers between devices with their start and end apart: 7, of which 6 were waited for; matrix products, arithmetic and copies ran while one was open for 13% of the time, Pallas kernels for 0%

commit v1 on v0

v1 whole, which is shorter than its diff:
```python
import functools

import jax
import jax.numpy as jnp
from jax import lax
from jax.experimental import pallas as pl
from jax.experimental.pallas import tpu as pltpu
from jax.sharding import Mesh
from jax.sharding import PartitionSpec as P

HEAD_WIDTH = 128
SEQ = ("seq_0", "seq_1", "seq_2", "seq_3")
FAR = ("seq_0", "seq_1", "seq_2")
CORE = "seq_3"
LOWEST_SCORE = -1e30
LOWEST_PEAK = -1e29
DEAD = 1e9
SCALE = HEAD_WIDTH ** (-0.5)
F32 = jnp.float32
BF16 = jnp.bfloat16
VMEM = pl.BlockSpec(memory_space=pltpu.VMEM)
SMEM = pl.BlockSpec(memory_space=pltpu.SMEM)


def rows_dot(a, b):
    return lax.dot_general(a, b, (((1,), (1,)), ((), ())), preferred_element_type=F32)


def plain_dot(a, b):
    return lax.dot_general(a, b, (((1,), (0,)), ((), ())), preferred_element_type=F32)


def three_parts(value):
    high = value.astype(BF16)
    rest = value - high.astype(F32)
    middle = rest.astype(BF16)
    low = (rest - middle.astype(F32)).astype(BF16)
    return high, middle, low


def packed_stats(columns, lanes):
    count = len(columns)
    rows = columns[0].shape[0]
    lane = lax.broadcasted_iota(jnp.int32, (rows, 128), 1)
    held = jnp.zeros((rows, 128), F32)
    for k, column in enumerate(columns):
        held = jnp.where(lane == k, column, held)
    return parts_side_by_side(held, count, lanes)


def parts_side_by_side(held, count, lanes):
    parts = [part[:, :count].astype(F32) for part in three_parts(held)]
    joined = jnp.concatenate(parts, axis=1)
    spare = jnp.zeros((held.shape[0], lanes - joined.shape[1]), F32)
    return jnp.concatenate([joined, spare], axis=1).astype(BF16)


def unpacked_stats(block, count):
    wide = block.astype(F32)
    return wide[:, :count] + wide[:, count : 2 * count] + wide[:, 2 * count : 3 * count]


def first_kernel(heads, group, where_ref, x_ref, k_ref, v_ref, y_ref, place_ref):
    rows = x_ref.shape[0]
    slots = k_ref.shape[0]
    half = slots // 2
    width = heads * HEAD_WIDTH
    far, core, span, row_total = (where_ref[0], where_ref[1], where_ref[2], where_ref[3])
    lens = x_ref[:, 2 * width : 2 * width + 128].astype(F32)
    lane = lax.broadcasted_iota(jnp.int32, (rows, 128), 1)
    row = lax.broadcasted_iota(jnp.int32, (rows, 128), 0)
    weight = jnp.where((lane == 0) | (lane == 2), 16.0, jnp.where((lane == 1) | (lane == 3), 1.0, 0.0))
    lens = lens * weight
    base = jnp.sum(jnp.where(row < far, lens, 0.0))
    here = jnp.where(row == far, lens, 0.0)
    own = jnp.sum(jnp.where(lane < 2, here, 0.0))
    other = jnp.sum(jnp.where(lane >= 2, here, 0.0))
    is_second = core.astype(F32)
    own_offset = base + is_second * other
    other_offset = base + (1.0 - is_second) * own
    place_ref[0] = own_offset
    place_ref[1] = other_offset
    place_ref[2] = own
    place_ref[3] = other
    within = lax.broadcasted_iota(jnp.int32, (1, half), 1).astype(F32)
    position = jnp.concatenate(
        [
            jnp.where(within < own, own_offset + within, DEAD),
            jnp.where(within < other, other_offset + within, DEAD),
        ],
        axis=1,
    )
    tall = group * rows
    index = lax.broadcasted_iota(jnp.int32, (tall, 1), 0) % rows
    asked = (span * row_total + 2 * index + core).astype(F32)
    visible = position <= asked
    keys = k_ref[...]
    values = v_ref[...]
    peaks, totals, means = [], [], []
    for first in range(0, heads, group):
        at = [(first + k) * HEAD_WIDTH for k in range(group)]
        q = jnp.concatenate([x_ref[:, a : a + HEAD_WIDTH] for a in at], axis=0)
        g = jnp.concatenate([x_ref[:, width + a : width + a + HEAD_WIDTH] for a in at], axis=0)
        scores = jnp.where(visible, rows_dot(q, keys) * SCALE, LOWEST_SCORE)
        peak = jnp.maximum(jnp.max(scores, axis=1, keepdims=True), LOWEST_PEAK)
        raised = jnp.exp(scores - peak)
        grads = rows_dot(g, values)
        total = jnp.sum(raised, axis=1, keepdims=True)
        mean = jnp.sum(raised * grads, axis=1, keepdims=True) / jnp.maximum(total, 0.5)
        moved = (raised * (grads - mean)).astype(BF16)
        both = plain_dot(jnp.concatenate([moved, raised.astype(BF16)], axis=0), keys)
        for k, a in enumerate(at):
            y_ref[:, a : a + HEAD_WIDTH] = both[k * rows : (k + 1) * rows].astype(BF16)
            y_ref[:, width + a : width + a + HEAD_WIDTH] = both[
                tall + k * rows : tall + (k + 1) * rows
            ].astype(BF16)
            peaks.append(peak[k * rows : (k + 1) * rows])
            totals.append(total[k * rows : (k + 1) * rows])
            means.append(mean[k * rows : (k + 1) * rows])
    y_ref[:, 2 * width :] = packed_stats(peaks + totals + means, 256)


def merge_kernel(heads, z_ref, u_ref):
    width = heads * HEAD_WIDTH
    count = u_ref.shape[0]
    stats = unpacked_stats(z_ref[:, 2 * width :], 3 * heads)
    peak, total, mean = (
        stats[:, :heads],
        stats[:, heads : 2 * heads],
        stats[:, 2 * heads : 3 * heads],
    )
    row_peak = jnp.max(peak, axis=0, keepdims=True)
    share = jnp.exp(peak - row_peak)
    part = share * total
    row_total = jnp.sum(part, axis=0, keepdims=True)
    row_mean = jnp.sum(part * mean, axis=0, keepdims=True) / row_total
    moved_factor = share * (SCALE / row_total)
    plain_factor = moved_factor * (mean - row_mean)
    for h in range(heads):
        a = h * HEAD_WIDTH
        term = z_ref[:, a : a + HEAD_WIDTH].astype(F32) * moved_factor[:, h : h + 1]
        term += z_ref[:, width + a : width + a + HEAD_WIDTH].astype(F32) * plain_factor[:, h : h + 1]
        line = jnp.sum(term, axis=0, keepdims=True)
        u_ref[:, a : a + HEAD_WIDTH] = jnp.broadcast_to(line, (count, HEAD_WIDTH)).astype(BF16)
    found = jnp.concatenate(
        [row_peak, row_total, row_mean, jnp.zeros((1, 128 - 3 * heads), F32)], axis=1
    )
    packed = parts_side_by_side(jnp.broadcast_to(found, (count, 128)), 3 * heads, 256)
    u_ref[:, width:] = packed


def second_kernel(heads, where_ref, place_ref, x_ref, u_ref, k_ref, v_ref, own_ref, other_ref):
    rows = x_ref.shape[0]
    slots = k_ref.shape[0]
    half = slots // 2
    width = heads * HEAD_WIDTH
    core, span, row_total = (where_ref[1], where_ref[2], where_ref[3])
    within = lax.broadcasted_iota(jnp.int32, (half, 1), 0).astype(F32)
    position = jnp.concatenate(
        [
            jnp.where(within < place_ref[2], place_ref[0] + within, DEAD),
            jnp.where(within < place_ref[3], place_ref[1] + within, DEAD),
        ],
        axis=0,
    )
    index = lax.broadcasted_iota(jnp.int32, (1, 2 * rows), 1) % rows
    asked = (span * row_total + 2 * index + core).astype(F32)
    visible = position <= asked
    stats = unpacked_stats(u_ref[:, width:], 3 * heads)
    stats = jnp.concatenate([stats, jnp.zeros((rows, 128 - 3 * heads), F32)], axis=1)
    turned = jnp.transpose(stats)
    keys = k_ref[...]
    values = v_ref[...]
    value_grads = jnp.zeros((slots, HEAD_WIDTH), F32)
    key_grads = jnp.zeros((slots, HEAD_WIDTH), F32)

    def of_pair(kind, h):
        line = kind * heads + h
        return jnp.concatenate([turned[line : line + 1], turned[line + 1 : line + 2]], axis=1)

    for h in range(0, heads, 2):
        a = h * HEAD_WIDTH
        q = jnp.concatenate(
            [x_ref[:, a : a + HEAD_WIDTH], x_ref[:, a + HEAD_WIDTH : a + 2 * HEAD_WIDTH]], axis=0
        )
        a += width
        g = jnp.concatenate(
            [x_ref[:, a : a + HEAD_WIDTH], x_ref[:, a + HEAD_WIDTH : a + 2 * HEAD_WIDTH]], axis=0
        )
        scores = rows_dot(keys, q) * SCALE
        raised = jnp.exp(jnp.where(visible, scores - of_pair(0, h), LOWEST_SCORE))
        weights = raised * (1.0 / of_pair(1, h))
        score_grads = weights * (rows_dot(values, g) - of_pair(2, h))
        value_grads += plain_dot(weights.astype(BF16), g)
        key_grads += plain_dot(score_grads.astype(BF16), q)
    key_grads *= SCALE
    own_ref[:, :HEAD_WIDTH] = key_grads[:half]
    own_ref[:, HEAD_WIDTH:] = value_grads[:half]
    other_ref[:, :HEAD_WIDTH] = key_grads[half:]
    other_ref[:, HEAD_WIDTH:] = value_grads[half:]


def exchanged(value, axes):
    return lax.all_to_all(value, axes, split_axis=0, concat_axis=0, tiled=True)


def shifted(value, axis, by):
    count = lax.axis_size(axis)
    return lax.ppermute(value, axis, [(k, (k + by) % count) for k in range(count)])


def local(
    queries,
    grad_output,
    key_cache,
    saved_value_rows,
    lengths,
    span_index,
    w_query,
    key_projection_weight,
    value_projection_weight,
):
    heads = queries.shape[1] // HEAD_WIDTH
    width = heads * HEAD_WIDTH
    rows = lax.axis_size(FAR)
    block = key_cache.shape[0]
    groups = lax.axis_size("head")
    core = lax.axis_index(CORE)
    far = lax.axis_index(FAR)
    mine = lax.axis_index("head")

    other_length = shifted(lengths, CORE, 1)
    numbers = jnp.stack([lengths // 16, lengths % 16, other_length // 16, other_length % 16], axis=1)
    numbers = jnp.pad(numbers.astype(BF16), ((0, 0), (0, 124)))
    row = jnp.concatenate([queries, grad_output, numbers], axis=1)
    gathered = exchanged(jnp.broadcast_to(row, (rows, 1, row.shape[1])), FAR)
    x = gathered.reshape(rows, row.shape[1])

    cache = jnp.concatenate([key_cache, saved_value_rows], axis=1)
    other_cache = shifted(cache, CORE, 1)
    keys = jnp.concatenate([key_cache, other_cache[:, :HEAD_WIDTH]], axis=0)
    values = jnp.concatenate([saved_value_rows, other_cache[:, HEAD_WIDTH:]], axis=0)

    features = key_projection_weight.shape[0] // groups
    first_is_key = core == 0
    half_weights = jnp.where(first_is_key, key_projection_weight, value_projection_weight)
    half_weights = half_weights.reshape(groups, features, HEAD_WIDTH)
    half_all = exchanged(half_weights, "head")
    other_half = shifted(half_all, CORE, 1)
    key_weights = jnp.where(first_is_key, half_all, other_half)
    value_weights = jnp.where(first_is_key, other_half, half_all)
    joined = jnp.concatenate([key_weights, value_weights], axis=2)

    where = jnp.stack([far, core, span_index[0], jnp.int32(2 * rows)]).astype(jnp.int32)
    y, place = pl.pallas_call(
        functools.partial(first_kernel, heads, min(4, heads)),
        out_shape=(
            jax.ShapeDtypeStruct((rows, 2 * width + 256), BF16),
            jax.ShapeDtypeStruct((4,), F32),
        ),
        in_specs=[SMEM, VMEM, VMEM, VMEM],
        out_specs=(VMEM, SMEM),
        name="row_partials",
    )(where, x, keys, values)
    arrived = exchanged(y.reshape(rows, 1, y.shape[1]), FAR).reshape(y.shape)
    merged = pl.pallas_call(
        functools.partial(merge_kernel, heads),
        out_shape=jax.ShapeDtypeStruct((rows, width + 256), BF16),
        in_specs=[VMEM],
        out_specs=VMEM,
        name="row_merge",
    )(arrived)
    u = exchanged(merged.reshape(rows, 1, merged.shape[1]), FAR).reshape(merged.shape)
    own_part, other_part = pl.pallas_call(
        functools.partial(second_kernel, heads),
        out_shape=(jax.ShapeDtypeStruct((block, 2 * HEAD_WIDTH), F32),) * 2,
        in_specs=[SMEM, SMEM, VMEM, VMEM, VMEM, VMEM],
        out_specs=(VMEM, VMEM),
        name="slot_gradients",
    )(where, place, x, u, keys, values)
    slot_grads = (own_part + shifted(other_part, CORE, 1)).astype(BF16)
    saved_key_gradient = slot_grads[:, :HEAD_WIDTH]
    saved_value_gradient = slot_grads[:, HEAD_WIDTH:]

    pieces = [slot_grads] + [shifted(slot_grads, "head", k) for k in range(1, groups)]
    total = jnp.zeros((block, features), F32)
    for k, piece in enumerate(pieces):
        source = lax.rem(mine - k + groups, groups)
        weights = lax.dynamic_index_in_dim(joined, source, 0, keepdims=False)
        total = total + rows_dot(piece, weights)
    cached_input_gradient = total.astype(BF16)

    query_low = u[:, :width]
    other_low = shifted(query_low, CORE, 1)
    own_rows = rows_dot(query_low, w_query)
    other_rows = rows_dot(other_low, w_query)
    even = jnp.where(first_is_key, own_rows, other_rows)
    odd = jnp.where(first_is_key, other_rows, own_rows)
    span_part = jnp.stack([even, odd], axis=1).reshape(groups, -1, w_query.shape[0])
    grad_span_input = exchanged(span_part, "head").sum(axis=0).astype(BF16)
    return (saved_key_gradient, saved_value_gradient, cached_input_gradient, grad_span_input)


def solution(mesh):
    split = Mesh(
        mesh.devices.reshape(4, 8, 2, 2, mesh.shape["head"]),
        ("seq_0", "seq_1", "seq_2", "seq_3", "head"),
    )
    in_specs = (
        P(SEQ, "head"),
        P(SEQ, "head"),
        P(SEQ, "head"),
        P(SEQ, "head"),
        P(SEQ),
        P(),
        P(SEQ, "head"),
        P(None, "head"),
        P(None, "head"),
    )
    out_specs = (P(SEQ, "head"), P(SEQ, "head"), P(SEQ, "head"), P("head", SEQ))
    return jax.shard_map(local, mesh=split, in_specs=in_specs, out_specs=out_specs, check_vma=False)
```

time: 433 us -> 183 us (0.42)
  waiting for transfers between devices: 205 us -> 68.8 us
  blocking collectives: 85 us -> 0 us
  local copies, waits for them, and re-layouts: 36.2 us -> 9.28 us
  between operations: 26.4 us -> 4.62 us
  starting transfers between devices: 50 us -> 68.3 us
  Pallas kernels: 0 us -> 11.7 us
  matrix products: 11.5 us -> 3.82 us
    all_gather x1 -> x0, waiting for transfers between devices: 161 us -> none  [side_by_side(): lax.all_gather(both, axis, axis=dim, tiled=True)]
    all_gather x4 -> x0, blocking collectives: 45.4 us -> none  [collected_together(): both, at, found = (lax.all_gather(jnp.concatenate(lines), axis), 0, {})]
    ppermute x0 -> x8, starting transfers between devices: none -> 31.2 us  [shifted(): lax.ppermute(value, axis, [(k, (k + by) % count) for k in range(count)])]
    unnamed x4 -> x0, blocking collectives: 25.7 us -> none
    all_to_all x2 -> x0, blocking collectives: 13.9 us -> none  [the longest x1 7.31 us: copy_for_each(): return lax.all_to_all(copies, axis, split_axis=0, concat_axis=0, tiled=True)]
    all_to_all x6 -> x5, waiting for transfers between devices: 43.7 us -> 57.6 us  [exchanged(): return lax.all_to_all(value, axes, split_axis=0, concat_axis=0, tiled=True)]
    all_to_all x6 -> x5, starting transfers between devices: 50 us -> 37.1 us  [exchanged(): return lax.all_to_all(value, axes, split_axis=0, concat_axis=0, tiled=True)]
    pallas_call x0 -> x3, Pallas kernels: none -> 11.7 us  [the longest x1 4.88 us: local(): pl.pallas_call(functools.partial(first_kernel, heads, min(4, heads)), out...]
  transfers between devices with their start and end apart: 7 -> 13, of which waited for: 6 -> 8; matrix products, arithmetic and copies ran while one was open for 13% -> 8% of each run, Pallas kernels for 0% -> 4%
where the time goes in v1:
time: 183 us; the launch traced here: 181 us
  waiting for transfers between devices  68.8 us (38%)
  starting transfers between devices  68.3 us (37%)
  other arithmetic  14.9 us (8%)
  Pallas kernels  11.7 us (6%)
  local copies, waits for them, and re-layouts  9.28 us (5%)
  between operations  4.62 us (3%)
  matrix products  3.82 us (2%)
    all_to_all x5, waiting for transfers between devices, exchanged(): return lax.all_to_all(value, axes, split_axis=0, concat_axis=0, tiled=True)  57.6 us
    all_to_all x5, starting transfers between devices, exchanged(): return lax.all_to_all(value, axes, split_axis=0, concat_axis=0, tiled=True)  37.1 us
    ppermute x8, starting transfers between devices, shifted(): lax.ppermute(value, axis, [(k, (k + by) % count) for k in range(count)])  31.2 us
    ppermute x8, waiting for transfers between devices, shifted(): lax.ppermute(value, axis, [(k, (k + by) % count) for k in range(count)])  11.3 us
    unnamed x23, local copies, waits for them, and re-layouts  6.85 us
    pallas_call x1, Pallas kernels, local(): pl.pallas_call(functools.partial(first_kernel, heads, min(4, heads)), out...  4.88 us
    pallas_call x1, Pallas kernels, local(): pl.pallas_call(functools.partial(second_kernel, heads), out_shape=(jax.Sh...  4.42 us
    broadcast_in_dim x1, other arithmetic, local(): gathered = exchanged(jnp.broadcast_to(row, (rows, 1, row.shape[1])), FAR)  3.89 us
  transfers between devices with their start and end apart: 13, of which 8 were waited for; matrix products, arithmetic and copies ran while one was open for 8% of the time, Pallas kernels for 4%

profile of v1, /device:TPU:1, one launch (start us, length us, event | category | flops | bytes accessed | tf_op | source)
XLA Modules:
  0.0 181.5 jit_solution(7262114282701775657)
XLA Ops:
  0.6 0.0 copy-start
  0.6 8.9 %collective-permute-start = (s32[1]{0:T(128)}, s32[1]{0:T(128)}, u32[]{:S(2)}, u32[]{:S(2)}) collective-permute-start(s32[1]{0:T(128)} %param.13), channel_id=1, source_target_pairs={{0,4},{4,0},{1,5},{5,1},{2,6},{6,2},{3,7},{7,3},{8,12},{12,8},{9,1... | collective-permute-start | bytes 20 | tf_op jit(solution)/shard_map/ppermute | solution.py:209
  10.2 0.4 collective-permute-done
  12.9 0.1 select_maximum_fusion
  13.0 0.8 maximum_reduce_fusion
  13.7 0.6 broadcast_in_dim.3
  14.3 0.5 broadcast.26
  14.8 3.9 %reduce.2 = bf16[64,4224]{1,0:T(8,128)(2,1)S(1)} reduce(bf16[64,1,4224]{2,1,0:T(2,128)(2,1)S(1)} %broadcast_in_dim.3, bf16[]{:T(256)} %broadcast.26), dimensions={1}, to_apply=%broadcast_in_dim.3.reduce_sub_computation | reduce | bytes 1081346 | tf_op jit(solution)/shard_map/broadcast_in_dim | solution.py:236
  18.7 1.2 reshape.118
  19.9 6.8 %all-to-all-start = ((bf16[64,2,2112]{2,1,0:T(2,128)(2,1)}), bf16[64,2,2112]{2,1,0:T(2,128)(2,1)S(1)}, u32[]{:S(2)}, u32[]{:S(2)}) async-start(bf16[64,2,2112]{2,1,0:T(2,128)(2,1)} %reshape.118), calls=%async_computation | async-start | bytes 1114112 | tf_op jit(solution)/shard_map/all_to_all | solution.py:204
  26.7 2.5 %collective-permute-start.1 = (bf16[384,256]{1,0:T(8,128)(2,1)S(1)}, bf16[384,256]{1,0:T(8,128)(2,1)S(1)}, u32[]{:S(2)}, u32[]{:S(2)}) collective-permute-start(bf16[384,256]{1,0:T(8,128)(2,1)S(1)} %pad_maximum_fusion), channel_id=1, source_target_pairs={{0,4},{4,0},{1,5},{5,1},{2,6},{6,2},{3,7},{7,3},{8,12},{12,8},{9,1... | collective-permute-start | bytes 589832 | tf_op jit(solution)/shard_map/ppermute | solution.py:209
  29.9 0.6 pad_add_fusion.where_ref
  30.5 0.0 collective-permute-done.1
  30.6 0.8 pad_maximum_fusion.1
  31.3 12.0 %all-to-all-done = bf16[64,2,2112]{2,1,0:T(2,128)(2,1)S(1)} async-done(((bf16[64,2,2112]{2,1,0:T(2,128)(2,1)}), bf16[64,2,2112]{2,1,0:T(2,128)(2,1)S(1)}, u32[]{:S(2)}, u32[]{:S(2)}) %all-to-all-start) | async-done | bytes 540704 | tf_op jit(solution)/shard_map/all_to_all | solution.py:204
  43.3 0.6 reshape.119
  43.9 0.9 copy.27
  44.8 4.9 %row_partials.1 = (bf16[64,4352]{1,0:T(8,128)(2,1)}, f32[4]{0:T(128)}) custom-call(s32[4]{0:T(128)} %pad_add_fusion.where_ref, bf16[64,4224]{1,0:T(8,128)(2,1)} %bitcast.44, bf16[768,128]{1,0:T(8,128)(2,1)} %get-tuple-element.20.k_ref, bf16[768,128]{1,0:T(8,128)(2,1)} %get-tuple-element.21.v_ref), custom_call_target="tpu_custom_call" | custom-call | tf_op jit(solution)/shard_map/row_partials/pallas_call | solution.py:255
  49.7 0.0 copy-start.2
  49.7 0.0 copy-start.3
  49.7 2.2 %reduce.3 = bf16[64,4352]{1,0:T(8,128)(2,1)S(1)} reduce(bf16[64,1,4352]{2,0,1:T(8,128)(2,1)} %bitcast.51, bf16[]{:T(256)} %broadcast.26), dimensions={1}, to_apply=%copy.17.reduce_sub_computation | reduce | bytes 1114114 | tf_op jit(solution)/shard_map/reshape | solution.py:265
  51.9 0.9 reshape.120
  52.9 7.4 %all-to-all-start.1 = ((bf16[64,2,2176]{2,1,0:T(2,128)(2,1)}), bf16[64,2,2176]{2,1,0:T(2,128)(2,1)S(1)}, u32[]{:S(2)}, u32[]{:S(2)}) async-start(bf16[64,2,2176]{2,1,0:T(2,128)(2,1)} %reshape.120), calls=%async_computation.1 | async-start | bytes 1114112 | tf_op jit(solution)/shard_map/all_to_all | solution.py:204
  60.3 1.1 broadcast_select_fusion
  61.3 15.0 %all-to-all-done.1 = bf16[64,2,2176]{2,1,0:T(2,128)(2,1)S(1)} async-done(((bf16[64,2,2176]{2,1,0:T(2,128)(2,1)}), bf16[64,2,2176]{2,1,0:T(2,128)(2,1)S(1)}, u32[]{:S(2)}, u32[]{:S(2)}) %all-to-all-start.1) | async-done | bytes 557088 | tf_op jit(solution)/shard_map/all_to_all | solution.py:204
  76.4 9.1 %all-to-all-start.3 = ((bf16[4,1024,128]{2,1,0:T(8,128)(2,1)}), bf16[4,1024,128]{2,1,0:T(8,128)(2,1)S(1)}, u32[]{:S(2)}, u32[]{:S(2)}) async-start(bf16[4,1024,128]{2,1,0:T(8,128)(2,1)} %bitcast.8), calls=%async_computation.3 | async-start | bytes 2097152 | tf_op jit(solution)/shard_map/all_to_all | solution.py:204
  85.5 0.5 reshape.121
  86.0 0.9 copy.26
  86.8 2.4 %row_merge.1 = bf16[64,2304]{1,0:T(8,128)(2,1)} custom-call(bf16[64,4352]{1,0:T(8,128)(2,1)} %bitcast.49), custom_call_target="tpu_custom_call" | custom-call | tf_op jit(solution)/shard_map/row_merge/pallas_call | solution.py:266
  89.2 1.7 reduce.4
  90.9 0.8 reshape.122
  91.7 17.8 %all-to-all-done.3 = bf16[4,1024,128]{2,1,0:T(8,128)(2,1)S(1)} async-done(((bf16[4,1024,128]{2,1,0:T(8,128)(2,1)}), bf16[4,1024,128]{2,1,0:T(8,128)(2,1)S(1)}, u32[]{:S(2)}, u32[]{:S(2)}) %all-to-all-start.3) | async-done | bytes 1048608 | tf_op jit(solution)/shard_map/all_to_all | solution.py:204
  109.5 10.6 %all-to-all-start.2 = ((bf16[64,2,1152]{2,1,0:T(2,128)(2,1)}), bf16[64,2,1152]{2,1,0:T(2,128)(2,1)S(1)}, u32[]{:S(2)}, u32[]{:S(2)}) async-start(bf16[64,2,1152]{2,1,0:T(2,128)(2,1)} %reshape.122), calls=%async_computation.2 | async-start | bytes 589824 | tf_op jit(solution)/shard_map/all_to_all | solution.py:204
  120.1 3.3 %collective-permute-start.3 = (bf16[4,1024,128]{2,1,0:T(8,128)(2,1)S(1)}, bf16[4,1024,128]{2,1,0:T(8,128)(2,1)}, u32[]{:S(2)}, u32[]{:S(2)}) collective-permute-start(bf16[4,1024,128]{2,1,0:T(8,128)(2,1)S(1)} %all-to-all-done.3), channel_id=1, source_target_pairs={{0,4},{4,0},{1,5},{5,1},{2,6},{6,2},{3,7},{7,3},{8,12},{12,8},{9,1... | collective-permute-start | bytes 3145736 | tf_op jit(solution)/shard_map/ppermute | solution.py:209
  123.4 7.6 %all-to-all-done.2 = bf16[64,2,1152]{2,1,0:T(2,128)(2,1)S(1)} async-done(((bf16[64,2,1152]{2,1,0:T(2,128)(2,1)}), bf16[64,2,1152]{2,1,0:T(2,128)(2,1)S(1)}, u32[]{:S(2)}, u32[]{:S(2)}) %all-to-all-start.2) | async-done | bytes 294944 | tf_op jit(solution)/shard_map/all_to_all | solution.py:204
  131.0 0.2 reshape.123
  131.3 4.8 %collective-permute-start.7 = (bf16[64,2048]{1,0:T(8,128)(2,1)S(1)}, bf16[64,2048]{1,0:T(8,128)(2,1)S(1)}, u32[]{:S(2)}, u32[]{:S(2)}) collective-permute-start(bf16[64,2048]{1,0:T(8,128)(2,1)S(1)} %slice.24), channel_id=1, source_target_pairs={{0,4},{4,0},{1,5},{5,1},{2,6},{6,2},{3,7},{7,3},{8,12},{12,8},{9,1... | collective-permute-start | bytes 786440 | tf_op jit(solution)/shard_map/ppermute | solution.py:209
  136.1 4.4 %slot_gradients.1 = (f32[384,256]{1,0:T(8,128)}, f32[384,256]{1,0:T(8,128)}) custom-call(s32[4]{0:T(128)} %pad_add_fusion.where_ref, f32[4]{0:T(128)} %get-tuple-element.8.place_ref, bf16[64,4224]{1,0:T(8,128)(2,1)} %bitcast.45, bf16[64,2304]{1,0:T(8,128)(2,1)} %bitcast.47, bf16[768,128]{1,0:T(8,128)(2,1)} %get-tuple-element.20.k_ref, ...), custom_call_target="tpu_custom_call" | custom-call | tf_op jit(solution)/shard_map/slot_gradients/pallas_call | solution.py:274
  140.6 1.9 %collective-permute-start.2 = (f32[384,256]{1,0:T(8,128)}, f32[384,256]{1,0:T(8,128)}, u32[]{:S(2)}, u32[]{:S(2)}) collective-permute-start(f32[384,256]{1,0:T(8,128)} %get-tuple-element.11), channel_id=1, source_target_pairs={{0,4},{4,0},{1,5},{5,1},{2,6},{6,2},{3,7},{7,3},{8,12},{12,8},{9,1... | collective-permute-start | bytes 1179656 | tf_op jit(solution)/shard_map/ppermute | solution.py:209
  142.5 1.1 fusion.26
  143.6 0.0 collective-permute-done.7
  143.6 0.2 select_bitcast_fusion.1
  143.9 0.1 copy.19
  144.0 0.7 reshape.124
  144.7 3.3 %all-to-all-start.4 = ((f32[4,1,1024]{2,1,0:T(1,128)}), f32[4,1,1024]{2,1,0:T(1,128)S(1)}, u32[]{:S(2)}, u32[]{:S(2)}) async-start(f32[4,1,1024]{2,1,0:T(1,128)} %reshape.124), calls=%async_computation.4 | async-start | bytes 32768 | tf_op jit(solution)/shard_map/all_to_all | solution.py:204
  147.9 0.0 collective-permute-done.3
  147.9 1.4 broadcast_select_fusion.1
  149.3 5.2 %all-to-all-done.4 = f32[4,1,1024]{2,1,0:T(1,128)S(1)} async-done(((f32[4,1,1024]{2,1,0:T(1,128)}), f32[4,1,1024]{2,1,0:T(1,128)S(1)}, u32[]{:S(2)}, u32[]{:S(2)}) %all-to-all-start.4) | async-done | bytes 16416 | tf_op jit(solution)/shard_map/all_to_all | solution.py:204
  154.5 0.5 broadcast.29
  155.0 0.7 reduce.5
  155.7 0.1 reshape.125
  155.8 0.6 reduce_sum.9
  156.4 0.0 collective-permute-done.2
  156.4 1.2 add_convert_fusion.1
  157.6 2.4 %collective-permute-start.5 = (bf16[384,256]{1,0:T(8,128)(2,1)S(1)}, bf16[384,256]{1,0:T(8,128)(2,1)S(1)}, u32[]{:S(2)}, u32[]{:S(2)}) collective-permute-start(bf16[384,256]{1,0:T(8,128)(2,1)S(1)} %add_convert_fusion.1), channel_id=1, source_target_pairs={{0,2},{1,3},{2,0},{3,1},{4,6},{5,7},{6,4},{7,5},{8,10},{9,11},{10,... | collective-permute-start | bytes 589832 | tf_op jit(solution)/shard_map/ppermute | solution.py:209
  160.0 4.0 %collective-permute-start.4 = (bf16[384,256]{1,0:T(8,128)(2,1)S(1)}, bf16[384,256]{1,0:T(8,128)(2,1)S(1)}, u32[]{:S(2)}, u32[]{:S(2)}) collective-permute-start(bf16[384,256]{1,0:T(8,128)(2,1)S(1)} %add_convert_fusion.1), channel_id=1, source_target_pairs={{0,1},{1,2},{2,3},{3,0},{4,5},{5,6},{6,7},{7,4},{8,9},{9,10},{10,1... | collective-permute-start | bytes 589832 | tf_op jit(solution)/shard_map/ppermute | solution.py:209
  164.0 3.4 %collective-permute-start.6 = (bf16[384,256]{1,0:T(8,128)(2,1)S(1)}, bf16[384,256]{1,0:T(8,128)(2,1)S(1)}, u32[]{:S(2)}, u32[]{:S(2)}) collective-permute-start(bf16[384,256]{1,0:T(8,128)(2,1)S(1)} %add_convert_fusion.1), channel_id=1, source_target_pairs={{0,3},{1,0},{2,1},{3,2},{4,7},{5,4},{6,5},{7,6},{8,11},{9,8},{10,9... | collective-permute-start | bytes 589832 | tf_op jit(solution)/shard_map/ppermute | solution.py:209
  167.4 0.4 fusion.8
  167.8 0.7 fusion.28
  168.5 5.5 %collective-permute-done.4 = bf16[384,256]{1,0:T(8,128)(2,1)S(1)} collective-permute-done((bf16[384,256]{1,0:T(8,128)(2,1)S(1)}, bf16[384,256]{1,0:T(8,128)(2,1)S(1)}, u32[]{:S(2)}, u32[]{:S(2)}) %collective-permute-start.4) | collective-permute-done | bytes 196640 | tf_op jit(solution)/shard_map/ppermute | solution.py:209
  174.0 0.4 fusion.12
  174.5 0.4 fusion.16
  174.9 5.3 %collective-permute-done.6 = bf16[384,256]{1,0:T(8,128)(2,1)S(1)} collective-permute-done((bf16[384,256]{1,0:T(8,128)(2,1)S(1)}, bf16[384,256]{1,0:T(8,128)(2,1)S(1)}, u32[]{:S(2)}, u32[]{:S(2)}) %collective-permute-start.6) | collective-permute-done | bytes 196640 | tf_op jit(solution)/shard_map/ppermute | solution.py:209
  180.2 1.3 add_convert_fusion
  (15 shorter events, 0.1 us)
Async XLA Ops:
  0.6 141.8 %copy-start = (bf16[32,2048]{1,0:T(8,128)(2,1)S(1)}, bf16[32,2048]{1,0:T(8,128)(2,1)}, u32[]{:S(2)}) copy-start(bf16[32,2048]{1,0:T(8,128)(2,1)} %param.15) | copy-start | bytes 393220
  0.6 9.9 %collective-permute-start = (s32[1]{0:T(128)}, s32[1]{0:T(128)}, u32[]{:S(2)}, u32[]{:S(2)}) collective-permute-start(s32[1]{0:T(128)} %param.13), channel_id=1, source_target_pairs={{0,4},{4,0},{1,5},{5,1},{2,6},{6,2},{3,7},{7,3},{8,12},{12,8},{9,1... | collective-permute-start | bytes 20 | tf_op jit(solution)/shard_map/ppermute | solution.py:209
  14.8 11.9 %copy-start.4 = (bf16[384,128]{1,0:T(8,128)(2,1)S(1)}, bf16[384,128]{1,0:T(8,128)(2,1)}, u32[]{:S(2)}) copy-start(bf16[384,128]{1,0:T(8,128)(2,1)} %param.12) | copy-start | bytes 294916
  14.8 11.9 %copy-start.5 = (bf16[384,128]{1,0:T(8,128)(2,1)S(1)}, bf16[384,128]{1,0:T(8,128)(2,1)}, u32[]{:S(2)}) copy-start(bf16[384,128]{1,0:T(8,128)(2,1)} %param.11) | copy-start | bytes 294916
  19.9 23.4 %all-to-all-start = ((bf16[64,2,2112]{2,1,0:T(2,128)(2,1)}), bf16[64,2,2112]{2,1,0:T(2,128)(2,1)S(1)}, u32[]{:S(2)}, u32[]{:S(2)}) async-start(bf16[64,2,2112]{2,1,0:T(2,128)(2,1)} %reshape.118), calls=%async_computation | async-start | bytes 1114112 | tf_op jit(solution)/shard_map/all_to_all | solution.py:204
  26.7 3.8 %collective-permute-start.1 = (bf16[384,256]{1,0:T(8,128)(2,1)S(1)}, bf16[384,256]{1,0:T(8,128)(2,1)S(1)}, u32[]{:S(2)}, u32[]{:S(2)}) collective-permute-start(bf16[384,256]{1,0:T(8,128)(2,1)S(1)} %pad_maximum_fusion), channel_id=1, source_target_pairs={{0,4},{4,0},{1,5},{5,1},{2,6},{6,2},{3,7},{7,3},{8,12},{12,8},{9,1... | collective-permute-start | bytes 589832 | tf_op jit(solution)/shard_map/ppermute | solution.py:209
  49.7 10.5 %copy-start.2 = (bf16[4096,128]{1,0:T(8,128)(2,1)S(1)}, bf16[4096,128]{1,0:T(8,128)(2,1)}, u32[]{:S(2)}) copy-start(bf16[4096,128]{1,0:T(8,128)(2,1)} %param.16) | copy-start | bytes 3145732
  49.7 10.5 %copy-start.3 = (bf16[4096,128]{1,0:T(8,128)(2,1)S(1)}, bf16[4096,128]{1,0:T(8,128)(2,1)}, u32[]{:S(2)}) copy-start(bf16[4096,128]{1,0:T(8,128)(2,1)} %param.17) | copy-start | bytes 3145732
  52.9 23.5 %all-to-all-start.1 = ((bf16[64,2,2176]{2,1,0:T(2,128)(2,1)}), bf16[64,2,2176]{2,1,0:T(2,128)(2,1)S(1)}, u32[]{:S(2)}, u32[]{:S(2)}) async-start(bf16[64,2,2176]{2,1,0:T(2,128)(2,1)} %reshape.120), calls=%async_computation.1 | async-start | bytes 1114112 | tf_op jit(solution)/shard_map/all_to_all | solution.py:204
  76.4 33.1 %all-to-all-start.3 = ((bf16[4,1024,128]{2,1,0:T(8,128)(2,1)}), bf16[4,1024,128]{2,1,0:T(8,128)(2,1)S(1)}, u32[]{:S(2)}, u32[]{:S(2)}) async-start(bf16[4,1024,128]{2,1,0:T(8,128)(2,1)} %bitcast.8), calls=%async_computation.3 | async-start | bytes 2097152 | tf_op jit(solution)/shard_map/all_to_all | solution.py:204
  109.5 21.5 %all-to-all-start.2 = ((bf16[64,2,1152]{2,1,0:T(2,128)(2,1)}), bf16[64,2,1152]{2,1,0:T(2,128)(2,1)S(1)}, u32[]{:S(2)}, u32[]{:S(2)}) async-start(bf16[64,2,1152]{2,1,0:T(2,128)(2,1)} %reshape.122), calls=%async_computation.2 | async-start | bytes 589824 | tf_op jit(solution)/shard_map/all_to_all | solution.py:204
  120.1 27.8 %collective-permute-start.3 = (bf16[4,1024,128]{2,1,0:T(8,128)(2,1)S(1)}, bf16[4,1024,128]{2,1,0:T(8,128)(2,1)}, u32[]{:S(2)}, u32[]{:S(2)}) collective-permute-start(bf16[4,1024,128]{2,1,0:T(8,128)(2,1)S(1)} %all-to-all-done.3), channel_id=1, source_target_pairs={{0,4},{4,0},{1,5},{5,1},{2,6},{6,2},{3,7},{7,3},{8,12},{12,8},{9,1... | collective-permute-start | bytes 3145736 | tf_op jit(solution)/shard_map/ppermute | solution.py:209
  131.3 4.8 %copy-start.1 = (bf16[64,1,2304]{2,0,1:T(8,128)(2,1)}, bf16[64,1,2304]{2,0,1:T(8,128)(2,1)S(1)}, u32[]{:S(2)}) copy-start(bf16[64,1,2304]{2,0,1:T(8,128)(2,1)S(1)} %copy.28) | copy-start | bytes 884740
  131.3 12.3 %collective-permute-start.7 = (bf16[64,2048]{1,0:T(8,128)(2,1)S(1)}, bf16[64,2048]{1,0:T(8,128)(2,1)S(1)}, u32[]{:S(2)}, u32[]{:S(2)}) collective-permute-start(bf16[64,2048]{1,0:T(8,128)(2,1)S(1)} %slice.24), channel_id=1, source_target_pairs={{0,4},{4,0},{1,5},{5,1},{2,6},{6,2},{3,7},{7,3},{8,12},{12,8},{9,1... | collective-permute-start | bytes 786440 | tf_op jit(solution)/shard_map/ppermute | solution.py:209
  140.6 15.9 %collective-permute-start.2 = (f32[384,256]{1,0:T(8,128)}, f32[384,256]{1,0:T(8,128)}, u32[]{:S(2)}, u32[]{:S(2)}) collective-permute-start(f32[384,256]{1,0:T(8,128)} %get-tuple-element.11), channel_id=1, source_target_pairs={{0,4},{4,0},{1,5},{5,1},{2,6},{6,2},{3,7},{7,3},{8,12},{12,8},{9,1... | collective-permute-start | bytes 1179656 | tf_op jit(solution)/shard_map/ppermute | solution.py:209
  144.7 9.9 %all-to-all-start.4 = ((f32[4,1,1024]{2,1,0:T(1,128)}), f32[4,1,1024]{2,1,0:T(1,128)S(1)}, u32[]{:S(2)}, u32[]{:S(2)}) async-start(f32[4,1,1024]{2,1,0:T(1,128)} %reshape.124), calls=%async_computation.4 | async-start | bytes 32768 | tf_op jit(solution)/shard_map/all_to_all | solution.py:204
  157.6 16.9 %collective-permute-start.5 = (bf16[384,256]{1,0:T(8,128)(2,1)S(1)}, bf16[384,256]{1,0:T(8,128)(2,1)S(1)}, u32[]{:S(2)}, u32[]{:S(2)}) collective-permute-start(bf16[384,256]{1,0:T(8,128)(2,1)S(1)} %add_convert_fusion.1), channel_id=1, source_target_pairs={{0,2},{1,3},{2,0},{3,1},{4,6},{5,7},{6,4},{7,5},{8,10},{9,11},{10,... | collective-permute-start | bytes 589832 | tf_op jit(solution)/shard_map/ppermute | solution.py:209
  160.0 14.0 %collective-permute-start.4 = (bf16[384,256]{1,0:T(8,128)(2,1)S(1)}, bf16[384,256]{1,0:T(8,128)(2,1)S(1)}, u32[]{:S(2)}, u32[]{:S(2)}) collective-permute-start(bf16[384,256]{1,0:T(8,128)(2,1)S(1)} %add_convert_fusion.1), channel_id=1, source_target_pairs={{0,1},{1,2},{2,3},{3,0},{4,5},{5,6},{6,7},{7,4},{8,9},{9,10},{10,1... | collective-permute-start | bytes 589832 | tf_op jit(solution)/shard_map/ppermute | solution.py:209
  164.0 16.2 %collective-permute-start.6 = (bf16[384,256]{1,0:T(8,128)(2,1)S(1)}, bf16[384,256]{1,0:T(8,128)(2,1)S(1)}, u32[]{:S(2)}, u32[]{:S(2)}) collective-permute-start(bf16[384,256]{1,0:T(8,128)(2,1)S(1)} %add_convert_fusion.1), channel_id=1, source_target_pairs={{0,3},{1,0},{2,1},{3,2},{4,7},{5,4},{6,5},{7,6},{8,11},{9,8},{10,9... | collective-permute-start | bytes 589832 | tf_op jit(solution)/shard_map/ppermute | solution.py:209

commit v2 on v1

v2 whole, which is shorter than its diff:
```python
import functools

import jax
import jax.numpy as jnp
from jax import lax
from jax.experimental import pallas as pl
from jax.experimental.pallas import tpu as pltpu
from jax.sharding import Mesh
from jax.sharding import PartitionSpec as P

HEAD_WIDTH = 128
SEQ = ("seq_0", "seq_1", "seq_2", "seq_3")
FAR = ("seq_0", "seq_1", "seq_2")
CORE = "seq_3"
LOWEST_SCORE = -1e30
LOWEST_PEAK = -1e29
DEAD = 1e9
SCALE = HEAD_WIDTH ** (-0.5)
F32 = jnp.float32
BF16 = jnp.bfloat16
VMEM = pl.BlockSpec(memory_space=pltpu.VMEM)
PARAMS = pltpu.CompilerParams(vmem_limit_bytes=32 * 1024 * 1024)
SMEM = pl.BlockSpec(memory_space=pltpu.SMEM)


def rows_dot(a, b):
    return lax.dot_general(a, b, (((1,), (1,)), ((), ())), preferred_element_type=F32)


def plain_dot(a, b):
    return lax.dot_general(a, b, (((1,), (0,)), ((), ())), preferred_element_type=F32)


def three_parts(value):
    high = value.astype(BF16).astype(F32)
    rest = value - high
    middle = rest.astype(BF16).astype(F32)
    low = (rest - middle).astype(BF16).astype(F32)
    return high, middle, low


def spread(held):
    axis = held.ndim - 1
    high, middle, low = three_parts(held)
    return high + pltpu.roll(middle, 16, axis) + pltpu.roll(low, 32, axis)


def gathered_parts(block):
    wide = block.astype(F32)
    axis = wide.ndim - 1
    return wide + pltpu.roll(wide, 112, axis) + pltpu.roll(wide, 96, axis)


def pack_kernel(heads, own_ref, other_ref, q_ref, g_ref, row_ref):
    lane = lax.broadcasted_iota(jnp.int32, (8, 128), 1)
    own, other = own_ref[0], other_ref[0]
    numbers = jnp.where(lane == 0, own // 16, 0) + jnp.where(lane == 1, own % 16, 0)
    numbers += jnp.where(lane == 2, other // 16, 0) + jnp.where(lane == 3, other % 16, 0)
    lines = []
    for ref in (q_ref, g_ref):
        wide = ref[...].astype(F32)
        lines += [wide[:, h * HEAD_WIDTH : (h + 1) * HEAD_WIDTH] for h in range(heads)]
    row = jnp.concatenate([*lines, numbers.astype(F32)], axis=0).astype(BF16)
    for k in range(row_ref.shape[0]):
        row_ref[k] = row


def first_kernel(heads, group, where_ref, x_ref, k_ref, v_ref, y_ref, place_ref):
    rows = x_ref.shape[0]
    half = k_ref.shape[0] // 2
    far, core, span, row_total = (where_ref[0], where_ref[1], where_ref[2], where_ref[3])
    lens = x_ref[:, 2 * heads :, :].astype(F32)
    lane = lax.broadcasted_iota(jnp.int32, lens.shape, 2)
    row = lax.broadcasted_iota(jnp.int32, lens.shape, 0)
    first_line = lax.broadcasted_iota(jnp.int32, lens.shape, 1) == 0
    lens = lens * jnp.where(first_line & (lane < 4), jnp.where(lane % 2 == 0, 16.0, 1.0), 0.0)
    base = jnp.sum(jnp.where(row < far, lens, 0.0))
    here = jnp.where(row == far, lens, 0.0)
    own = jnp.sum(jnp.where(lane < 2, here, 0.0))
    other = jnp.sum(jnp.where(lane >= 2, here, 0.0))
    is_second = core.astype(F32)
    own_offset = base + is_second * other
    other_offset = base + (1.0 - is_second) * own
    place_ref[0] = own_offset
    place_ref[1] = other_offset
    place_ref[2] = own
    place_ref[3] = other
    within = lax.broadcasted_iota(jnp.int32, (1, half), 1).astype(F32)
    position = jnp.concatenate(
        [
            jnp.where(within < own, own_offset + within, DEAD),
            jnp.where(within < other, other_offset + within, DEAD),
        ],
        axis=1,
    )
    tall = group * heads
    index = lax.broadcasted_iota(jnp.int32, (tall, 1), 0) // heads
    lane = lax.broadcasted_iota(jnp.int32, (tall, 128), 1)
    keys = k_ref[...]
    values = v_ref[...]
    for first in range(0, rows, group):
        part = pl.ds(first, group)
        q = x_ref[part, :heads, :].reshape(tall, HEAD_WIDTH)
        g = x_ref[part, heads : 2 * heads, :].reshape(tall, HEAD_WIDTH)
        asked = (span * row_total + 2 * (first + index) + core).astype(F32)
        scores = jnp.where(position <= asked, rows_dot(q, keys) * SCALE, LOWEST_SCORE)
        peak = jnp.maximum(jnp.max(scores, axis=1, keepdims=True), LOWEST_PEAK)
        raised = jnp.exp(scores - peak)
        grads = rows_dot(g, values)
        total = jnp.sum(raised, axis=1, keepdims=True)
        mean = jnp.sum(raised * grads, axis=1, keepdims=True) / jnp.maximum(total, 0.5)
        moved = (raised * (grads - mean)).astype(BF16)
        both = plain_dot(jnp.concatenate([moved, raised.astype(BF16)], axis=0), keys)
        y_ref[part, :heads, :] = both[:tall].astype(BF16).reshape(group, heads, HEAD_WIDTH)
        y_ref[part, heads : 2 * heads, :] = both[tall:].astype(BF16).reshape(group, heads, HEAD_WIDTH)
        held = jnp.where(lane == 0, peak, jnp.where(lane == 1, total, jnp.where(lane == 2, mean, 0.0)))
        held = spread(held).reshape(group, 2, heads // 2, 128)
        held = held[:, 0] + pltpu.roll(held[:, 1], 64, 2)
        y_ref[part, 2 * heads :, :] = held.astype(BF16)


def merge_kernel(heads, z_ref, u_ref):
    stats = gathered_parts(z_ref[:, 2 * heads :, :])
    total = pltpu.roll(stats, 127, 2)
    mean = pltpu.roll(stats, 126, 2)
    row_peak = jnp.max(stats, axis=0, keepdims=True)
    share = jnp.exp(stats - row_peak)
    part = share * total
    row_total = jnp.sum(part, axis=0, keepdims=True)
    row_mean = jnp.sum(part * mean, axis=0, keepdims=True) / row_total
    moved_factor = share * (SCALE / row_total)
    plain_factor = moved_factor * (mean - row_mean)

    def of_heads(factor):
        return jnp.concatenate([factor[:, :, 0:1], factor[:, :, 64:65]], axis=1)

    term = z_ref[:, :heads, :].astype(F32) * of_heads(moved_factor)
    term += z_ref[:, heads : 2 * heads, :].astype(F32) * of_heads(plain_factor)
    query_grads = jnp.sum(term, axis=0).astype(BF16)
    lane = lax.broadcasted_iota(jnp.int32, (heads // 2, 128), 1) % 64
    found = jnp.where(lane == 0, row_peak[0], 0.0)
    found = jnp.where(lane == 1, pltpu.roll(row_total[0], 1, 1), found)
    found = jnp.where(lane == 2, pltpu.roll(row_mean[0], 2, 1), found)
    found = spread(found).astype(BF16)
    for k in range(u_ref.shape[0]):
        u_ref[k, :heads, :] = query_grads
        u_ref[k, heads:, :] = found


def second_kernel(heads, group, where_ref, place_ref, x_ref, u_ref, k_ref, v_ref, own_ref, other_ref):
    rows = x_ref.shape[0]
    slots = k_ref.shape[0]
    half = slots // 2
    core, span, row_total = (where_ref[1], where_ref[2], where_ref[3])
    within = lax.broadcasted_iota(jnp.int32, (half, 1), 0).astype(F32)
    position = jnp.concatenate(
        [
            jnp.where(within < place_ref[2], place_ref[0] + within, DEAD),
            jnp.where(within < place_ref[3], place_ref[1] + within, DEAD),
        ],
        axis=0,
    )
    wide = group * heads
    index = lax.broadcasted_iota(jnp.int32, (1, wide), 1) // heads
    stats = gathered_parts(u_ref[:, heads:, :])
    keys = k_ref[...]
    values = v_ref[...]
    value_grads = jnp.zeros((slots, HEAD_WIDTH), F32)
    key_grads = jnp.zeros((slots, HEAD_WIDTH), F32)
    for first in range(0, rows, group):
        part = pl.ds(first, group)
        q = x_ref[part, :heads, :].reshape(wide, HEAD_WIDTH)
        g = x_ref[part, heads : 2 * heads, :].reshape(wide, HEAD_WIDTH)
        held = stats[first : first + group]
        held = jnp.concatenate([held, pltpu.roll(held, 64, 2)], axis=1).reshape(wide, 128)
        turned = jnp.transpose(held)
        asked = (span * row_total + 2 * (first + index) + core).astype(F32)
        scores = rows_dot(keys, q) * SCALE
        raised = jnp.exp(jnp.where(position <= asked, scores - turned[0:1], LOWEST_SCORE))
        weights = raised * (1.0 / turned[1:2])
        score_grads = weights * (rows_dot(values, g) - turned[2:3])
        value_grads += plain_dot(weights.astype(BF16), g)
        key_grads += plain_dot(score_grads.astype(BF16), q)
    key_grads *= SCALE
    own_ref[:, :HEAD_WIDTH] = key_grads[:half]
    own_ref[:, HEAD_WIDTH:] = value_grads[:half]
    other_ref[:, :HEAD_WIDTH] = key_grads[half:]
    other_ref[:, HEAD_WIDTH:] = value_grads[half:]


def exchanged(value, axes):
    return lax.all_to_all(value, axes, split_axis=0, concat_axis=0, tiled=True)


def shifted(value, axis, by):
    count = lax.axis_size(axis)
    return lax.ppermute(value, axis, [(k, (k + by) % count) for k in range(count)])


def local(
    queries,
    grad_output,
    key_cache,
    saved_value_rows,
    lengths,
    span_index,
    w_query,
    key_projection_weight,
    value_projection_weight,
):
    heads = queries.shape[1] // HEAD_WIDTH
    rows = lax.axis_size(FAR)
    block = key_cache.shape[0]
    groups = lax.axis_size("head")
    core = lax.axis_index(CORE)
    far = lax.axis_index(FAR)
    mine = lax.axis_index("head")
    lines = 2 * heads + 8
    group = min(16, rows)

    other_length = shifted(lengths, CORE, 1)
    row = pl.pallas_call(
        functools.partial(pack_kernel, heads),
        out_shape=jax.ShapeDtypeStruct((rows, lines, HEAD_WIDTH), BF16),
        in_specs=[SMEM, SMEM, VMEM, VMEM],
        out_specs=VMEM,
        name="row_pack",
        compiler_params=PARAMS,
    )(lengths, other_length, queries, grad_output)
    x = exchanged(row, FAR)

    cache = jnp.concatenate([key_cache, saved_value_rows], axis=1)
    other_cache = shifted(cache, CORE, 1)
    keys = jnp.concatenate([key_cache, other_cache[:, :HEAD_WIDTH]], axis=0)
    values = jnp.concatenate([saved_value_rows, other_cache[:, HEAD_WIDTH:]], axis=0)

    features = key_projection_weight.shape[0] // groups
    first_is_key = core == 0
    half_weights = jnp.where(first_is_key, key_projection_weight, value_projection_weight)
    half_weights = half_weights.reshape(groups, features, HEAD_WIDTH)
    arriving = []
    for k in range(1, groups):
        target = lax.rem(mine + k, groups)
        piece = lax.dynamic_index_in_dim(half_weights, target, 0, keepdims=False)
        arriving.append(shifted(piece, "head", k))
    half_all = jnp.concatenate(arriving, axis=0)
    other_half = shifted(half_all, CORE, 1)
    key_weights = jnp.where(first_is_key, half_all, other_half)
    value_weights = jnp.where(first_is_key, other_half, half_all)
    joined = jnp.concatenate([key_weights, value_weights], axis=1)

    where = jnp.stack([far, core, span_index[0], jnp.int32(2 * rows)]).astype(jnp.int32)
    y, place = pl.pallas_call(
        functools.partial(first_kernel, heads, group),
        out_shape=(
            jax.ShapeDtypeStruct((rows, lines, HEAD_WIDTH), BF16),
            jax.ShapeDtypeStruct((4,), F32),
        ),
        in_specs=[SMEM, VMEM, VMEM, VMEM],
        out_specs=(VMEM, SMEM),
        name="row_partials",
        compiler_params=PARAMS,
    )(where, x, keys, values)
    arrived = exchanged(y, FAR)
    merged = pl.pallas_call(
        functools.partial(merge_kernel, heads),
        out_shape=jax.ShapeDtypeStruct((rows, heads + 8, HEAD_WIDTH), BF16),
        in_specs=[VMEM],
        out_specs=VMEM,
        name="row_merge",
        compiler_params=PARAMS,
    )(arrived)
    u = exchanged(merged, FAR)
    own_part, other_part = pl.pallas_call(
        functools.partial(second_kernel, heads, group),
        out_shape=(jax.ShapeDtypeStruct((block, 2 * HEAD_WIDTH), F32),) * 2,
        in_specs=[SMEM, SMEM, VMEM, VMEM, VMEM, VMEM],
        out_specs=(VMEM, VMEM),
        name="slot_gradients",
        compiler_params=PARAMS,
    )(where, place, x, u, keys, values)
    other_sums = shifted(other_part, CORE, 1)
    slot_grads = (own_part + other_sums).astype(BF16)
    saved_key_gradient = slot_grads[:, :HEAD_WIDTH]
    saved_value_gradient = slot_grads[:, HEAD_WIDTH:]

    pieces = [slot_grads]
    for k in range(1, groups):
        pieces.append(shifted(slot_grads, "head", k))
    own_weights = [
        lax.dynamic_slice_in_dim(w, mine * features, features, 0)
        for w in (key_projection_weight, value_projection_weight)
    ]
    total = rows_dot(slot_grads, jnp.concatenate(own_weights, axis=1))
    for k in range(1, groups):
        total = total + rows_dot(pieces[k], joined[(k - 1) * features : k * features])
    cached_input_gradient = total.astype(BF16)

    query_low = u[:, :heads, :]
    other_low = shifted(query_low, CORE, 1)
    own_rows = rows_dot(query_low.reshape(rows, -1), w_query)
    other_rows = rows_dot(other_low.reshape(rows, -1), w_query)
    even = jnp.where(first_is_key, own_rows, other_rows)
    odd = jnp.where(first_is_key, other_rows, own_rows)
    span_part = jnp.stack([even, odd], axis=1).reshape(groups, -1, w_query.shape[0])
    arrived_parts = exchanged(span_part, "head")
    grad_span_input = arrived_parts.sum(axis=0).astype(BF16)
    return (saved_key_gradient, saved_value_gradient, cached_input_gradient, grad_span_input)


def solution(mesh):
    split = Mesh(
        mesh.devices.reshape(4, 8, 2, 2, mesh.shape["head"]),
        ("seq_0", "seq_1", "seq_2", "seq_3", "head"),
    )
    in_specs = (
        P(SEQ, "head"),
        P(SEQ, "head"),
        P(SEQ, "head"),
        P(SEQ, "head"),
        P(SEQ),
        P(),
        P(SEQ, "head"),
        P(None, "head"),
        P(None, "head"),
    )
    out_specs = (P(SEQ, "head"), P(SEQ, "head"), P(SEQ, "head"), P("head", SEQ))
    return jax.shard_map(local, mesh=split, in_specs=in_specs, out_specs=out_specs, check_vma=False)
```

time: 183 us -> 165 us (0.902)
  the two profiles are of different devices: /device:TPU:1 before, /device:TPU:103 now
where the time goes in v2:
time: 165 us; the launch traced here: 164 us
  starting transfers between devices  82.6 us (50%)
  waiting for transfers between devices  53.8 us (33%)
  Pallas kernels  10.4 us (6%)
  local copies, waits for them, and re-layouts  7.32 us (4%)
  other arithmetic  4.38 us (3%)
  matrix products  2.9 us (2%)
  between operations  2.3 us (1%)
    ppermute x11, starting transfers between devices, shifted(): lax.ppermute(value, axis, [(k, (k + by) % count) for k in range(count)])  43.6 us
    all_to_all x4, starting transfers between devices, exchanged(): return lax.all_to_all(value, axes, split_axis=0, concat_axis=0, tiled=True)  39 us
    ppermute x11, waiting for transfers between devices, shifted(): lax.ppermute(value, axis, [(k, (k + by) % count) for k in range(count)])  33 us
    all_to_all x4, waiting for transfers between devices, exchanged(): return lax.all_to_all(value, axes, split_axis=0, concat_axis=0, tiled=True)  20.8 us
    pallas_call x1, Pallas kernels, local(): pl.pallas_call(functools.partial(first_kernel, heads, group), out_shape=(...  4.46 us
  transfers between devices with their start and end apart: 15, of which 8 were waited for; matrix products, arithmetic and copies ran while one was open for 7% of the time, Pallas kernels for 3%

profile of v2, /device:TPU:103, one launch (start us, length us, event | category | flops | bytes accessed | tf_op | source)
XLA Modules:
  0.0 163.7 jit_solution(12187127419989661759)
XLA Ops:
  0.6 0.0 copy-start
  0.6 2.7 %collective-permute-start = (s32[1]{0:T(128)}, s32[1]{0:T(128)}, u32[]{:S(2)}, u32[]{:S(2)}) collective-permute-start(s32[1]{0:T(128)} %param.13), channel_id=1, source_target_pairs={{0,4},{4,0},{1,5},{5,1},{2,6},{6,2},{3,7},{7,3},{8,12},{12,8},{9,1... | collective-permute-start | bytes 20 | tf_op jit(solution)/shard_map/ppermute | solution.py:197
  4.0 0.3 collective-permute-done.other_ref
  4.3 0.7 copy-done.1
  5.0 0.7 copy-done.2
  5.7 1.6 row_pack.1
  7.3 10.7 %all-to-all-start = ((bf16[64,40,128]{2,1,0:T(8,128)(2,1)}), bf16[64,40,128]{2,1,0:T(8,128)(2,1)S(1)}, u32[]{:S(2)}, u32[]{:S(2)}) async-start(bf16[64,40,128]{2,1,0:T(8,128)(2,1)} %row_pack.1), calls=%async_computation | async-start | bytes 1310720 | tf_op jit(solution)/shard_map/all_to_all | solution.py:192
  18.1 2.8 %collective-permute-start.1 = (bf16[384,256]{1,0:T(8,128)(2,1)S(1)}, bf16[384,256]{1,0:T(8,128)(2,1)S(1)}, u32[]{:S(2)}, u32[]{:S(2)}) collective-permute-start(bf16[384,256]{1,0:T(8,128)(2,1)S(1)} %pad_maximum_fusion.4), channel_id=1, source_target_pairs={{0,4},{4,0},{1,5},{5,1},{2,6},{6,2},{3,7},{7,3},{8,12},{12,8},{9,1... | collective-permute-start | bytes 589832 | tf_op jit(solution)/shard_map/ppermute | solution.py:197
  21.6 0.1 pad_add_fusion.where_ref
  21.7 0.3 collective-permute-done.1
  22.0 0.0 copy-start.3
  22.0 10.0 %all-to-all-done.x_ref = bf16[64,40,128]{2,1,0:T(8,128)(2,1)S(1)} async-done(((bf16[64,40,128]{2,1,0:T(8,128)(2,1)}), bf16[64,40,128]{2,1,0:T(8,128)(2,1)S(1)}, u32[]{:S(2)}, u32[]{:S(2)}) %all-to-all-start) | async-done | bytes 655392 | tf_op jit(solution)/shard_map/all_to_all | solution.py:192
  32.1 4.5 %row_partials.1 = (bf16[64,40,128]{2,1,0:T(8,128)(2,1)}, f32[4]{0:T(128)S(1)}) custom-call(s32[4]{0:T(128)S(1)} %pad_add_fusion.where_ref, bf16[64,40,128]{2,1,0:T(8,128)(2,1)S(1)} %all-to-all-done.x_ref, bf16[768,128]{1,0:T(8,128)(2,1)S(1)} %get-tuple-element.23.k_ref, bf16[768,128]{1,0:T(8,128)(2,1)S(1)} %get-tuple-element.24.v_ref), custom_call_target="tpu_custom_call" | custom-call | tf_op jit(solution)/shard_map/row_partials/pallas_call | solution.py:253
  36.6 12.2 %all-to-all-start.1 = ((bf16[64,40,128]{2,1,0:T(8,128)(2,1)}), bf16[64,40,128]{2,1,0:T(8,128)(2,1)S(1)}, u32[]{:S(2)}, u32[]{:S(2)}) async-start(bf16[64,40,128]{2,1,0:T(8,128)(2,1)} %get-tuple-element.9), calls=%async_computation.1 | async-start | bytes 1310720 | tf_op jit(solution)/shard_map/all_to_all | solution.py:192
  48.8 0.0 copy-done.3
  48.8 1.3 broadcast_select_fusion
  50.1 0.9 dynamic-slice_bitcast_fusion
  51.0 5.8 %collective-permute-start.4 = (bf16[1024,128]{1,0:T(8,128)(2,1)S(1)}, bf16[1024,128]{1,0:T(8,128)(2,1)}, u32[]{:S(2)}, u32[]{:S(2)}) collective-permute-start(bf16[1024,128]{1,0:T(8,128)(2,1)S(1)} %get-tuple-element.16), channel_id=1, source_target_pairs={{0,1},{1,2},{2,3},{3,0},{4,5},{5,6},{6,7},{7,4},{8,9},{9,10},{10,1... | collective-permute-start | bytes 786440 | tf_op jit(solution)/shard_map/ppermute | solution.py:197
  56.8 5.7 %all-to-all-done.1.z_ref = bf16[64,40,128]{2,1,0:T(8,128)(2,1)S(1)} async-done(((bf16[64,40,128]{2,1,0:T(8,128)(2,1)}), bf16[64,40,128]{2,1,0:T(8,128)(2,1)S(1)}, u32[]{:S(2)}, u32[]{:S(2)}) %all-to-all-start.1) | async-done | bytes 655392 | tf_op jit(solution)/shard_map/all_to_all | solution.py:192
  62.5 1.6 row_merge.1
  64.0 12.3 %all-to-all-start.2 = ((bf16[64,24,128]{2,1,0:T(8,128)(2,1)}), bf16[64,24,128]{2,1,0:T(8,128)(2,1)S(1)}, u32[]{:S(2)}, u32[]{:S(2)}) async-start(bf16[64,24,128]{2,1,0:T(8,128)(2,1)} %row_merge.1), calls=%async_computation.2 | async-start | bytes 786432 | tf_op jit(solution)/shard_map/all_to_all | solution.py:192
  76.3 10.6 %collective-permute-start.5 = (bf16[1024,128]{1,0:T(8,128)(2,1)}, bf16[1024,128]{1,0:T(8,128)(2,1)S(1)}, u32[]{:S(2)}, u32[]{:S(2)}) collective-permute-start(bf16[1024,128]{1,0:T(8,128)(2,1)} %get-tuple-element.15), channel_id=1, source_target_pairs={{0,2},{1,3},{2,0},{3,1},{4,6},{5,7},{6,4},{7,5},{8,10},{9,11},{10,... | collective-permute-start | bytes 786440 | tf_op jit(solution)/shard_map/ppermute | solution.py:197
  86.9 1.9 %collective-permute-start.6 = (bf16[1024,128]{1,0:T(8,128)(2,1)}, bf16[1024,128]{1,0:T(8,128)(2,1)S(1)}, u32[]{:S(2)}, u32[]{:S(2)}) collective-permute-start(bf16[1024,128]{1,0:T(8,128)(2,1)} %get-tuple-element.14), channel_id=1, source_target_pairs={{0,3},{1,0},{2,1},{3,2},{4,7},{5,4},{6,5},{7,6},{8,11},{9,8},{10,9... | collective-permute-start | bytes 786440 | tf_op jit(solution)/shard_map/ppermute | solution.py:197
  88.9 0.0 collective-permute-done.4
  88.9 1.0 constant_dynamic-update-slice_fusion.2
  89.9 16.0 %collective-permute-done.5 = bf16[1024,128]{1,0:T(8,128)(2,1)S(1)} collective-permute-done((bf16[1024,128]{1,0:T(8,128)(2,1)}, bf16[1024,128]{1,0:T(8,128)(2,1)S(1)}, u32[]{:S(2)}, u32[]{:S(2)}) %collective-permute-start.5) | collective-permute-done | bytes 262176 | tf_op jit(solution)/shard_map/ppermute | solution.py:197
  105.9 2.6 %collective-permute-done.6 = bf16[1024,128]{1,0:T(8,128)(2,1)S(1)} collective-permute-done((bf16[1024,128]{1,0:T(8,128)(2,1)}, bf16[1024,128]{1,0:T(8,128)(2,1)S(1)}, u32[]{:S(2)}, u32[]{:S(2)}) %collective-permute-start.6) | collective-permute-done | bytes 262176 | tf_op jit(solution)/shard_map/ppermute | solution.py:197
  108.5 0.0 copy-start.4
  108.5 5.6 %collective-permute-start.7 = (bf16[3072,128]{1,0:T(8,128)(2,1)S(1)}, bf16[3072,128]{1,0:T(8,128)(2,1)}, u32[]{:S(2)}, u32[]{:S(2)}) collective-permute-start(bf16[3072,128]{1,0:T(8,128)(2,1)S(1)} %constant_dynamic-update-slice_fusion), channel_id=1, source_target_pairs={{0,4},{4,0},{1,5},{5,1},{2,6},{6,2},{3,7},{7,3},{8,12},{12,8},{9,1... | collective-permute-start | bytes 2359304 | tf_op jit(solution)/shard_map/ppermute | solution.py:197
  114.2 0.0 all-to-all-done.2.u_ref
  114.2 1.9 %collective-permute-start.10 = (bf16[64,16,128]{2,1,0:T(8,128)(2,1)S(1)}, bf16[64,16,128]{2,1,0:T(8,128)(2,1)S(1)}, u32[]{:S(2)}, u32[]{:S(2)}) collective-permute-start(bf16[64,16,128]{2,1,0:T(8,128)(2,1)S(1)} %slice.40), channel_id=1, source_target_pairs={{0,4},{4,0},{1,5},{5,1},{2,6},{6,2},{3,7},{7,3},{8,12},{12,8},{9,1... | collective-permute-start | bytes 786440 | tf_op jit(solution)/shard_map/ppermute | solution.py:197
  116.1 1.9 %constant_dynamic-slice_fusion = (bf16[1024,128]{1,0:T(8,128)(2,1)}, bf16[1024,128]{1,0:T(8,128)(2,1)}) fusion(bf16[4096,128]{1,0:T(8,128)(2,1)} %param.17, s32[]{:T(128)S(6)} %select_n.46, bf16[4096,128]{1,0:T(8,128)(2,1)S(1)} %copy-done.3), kind=kLoop, calls=%fused_computation.38 | loop fusion | bytes 1048580 | tf_op jit(solution)/shard_map/dynamic_slice | solution.py:291
  118.0 2.7 %slot_gradients.1 = (f32[384,256]{1,0:T(8,128)S(1)}, f32[384,256]{1,0:T(8,128)S(1)}) custom-call(s32[4]{0:T(128)S(1)} %pad_add_fusion.where_ref, f32[4]{0:T(128)S(1)} %get-tuple-element.8.place_ref, bf16[64,40,128]{2,1,0:T(8,128)(2,1)S(1)} %all-to-all-done.x_ref, bf16[64,24,128]{2,1,0:T(8,128)(2,1)S(1)} %all-to-all-done.2.u_ref, ...), custom_call_target="tpu_custom_call" | custom-call | tf_op jit(solution)/shard_map/slot_gradients/pallas_call | solution.py:274
  120.7 2.4 %collective-permute-start.2 = (f32[384,256]{1,0:T(8,128)S(1)}, f32[384,256]{1,0:T(8,128)S(1)}, u32[]{:S(2)}, u32[]{:S(2)}) collective-permute-start(f32[384,256]{1,0:T(8,128)S(1)} %get-tuple-element.11), channel_id=1, source_target_pairs={{0,4},{4,0},{1,5},{5,1},{2,6},{6,2},{3,7},{7,3},{8,12},{12,8},{9,1... | collective-permute-start | bytes 1179656 | tf_op jit(solution)/shard_map/ppermute | solution.py:197
  123.1 0.0 copy-done
  123.1 0.2 fusion.15
  123.3 0.0 copy-done.4
  123.4 0.0 collective-permute-done.10
  123.4 0.2 select_bitcast_fusion.1
  123.6 0.1 copy.13
  123.7 0.7 reshape.24
  124.4 3.8 %all-to-all-start.3 = ((f32[4,1,1024]{2,1,0:T(1,128)}), f32[4,1,1024]{2,1,0:T(1,128)S(1)}, u32[]{:S(2)}, u32[]{:S(2)}) async-start(f32[4,1,1024]{2,1,0:T(1,128)} %reshape.24), calls=%async_computation.3 | async-start | bytes 32768 | tf_op jit(solution)/shard_map/all_to_all | solution.py:192
  128.2 0.0 collective-permute-done.7
  128.2 1.5 broadcast_select_fusion.1
  129.7 5.1 %all-to-all-done.3 = f32[4,1,1024]{2,1,0:T(1,128)S(1)} async-done(((f32[4,1,1024]{2,1,0:T(1,128)}), f32[4,1,1024]{2,1,0:T(1,128)S(1)}, u32[]{:S(2)}, u32[]{:S(2)}) %all-to-all-start.3) | async-done | bytes 16416 | tf_op jit(solution)/shard_map/all_to_all | solution.py:192
  134.8 0.5 broadcast.3
  135.3 0.7 reduce
  136.0 0.1 reshape.25
  136.1 0.6 reduce_sum.9
  136.7 0.0 collective-permute-done.2
  136.7 0.1 add_convert_fusion.1
  136.8 2.4 %collective-permute-start.8 = (bf16[384,256]{1,0:T(8,128)(2,1)S(1)}, bf16[384,256]{1,0:T(8,128)(2,1)S(1)}, u32[]{:S(2)}, u32[]{:S(2)}) collective-permute-start(bf16[384,256]{1,0:T(8,128)(2,1)S(1)} %add_convert_fusion.1), channel_id=1, source_target_pairs={{0,2},{1,3},{2,0},{3,1},{4,6},{5,7},{6,4},{7,5},{8,10},{9,11},{10,... | collective-permute-start | bytes 589832 | tf_op jit(solution)/shard_map/ppermute | solution.py:197
  139.2 4.0 %collective-permute-start.3 = (bf16[384,256]{1,0:T(8,128)(2,1)S(1)}, bf16[384,256]{1,0:T(8,128)(2,1)S(1)}, u32[]{:S(2)}, u32[]{:S(2)}) collective-permute-start(bf16[384,256]{1,0:T(8,128)(2,1)S(1)} %add_convert_fusion.1), channel_id=1, source_target_pairs={{0,1},{1,2},{2,3},{3,0},{4,5},{5,6},{6,7},{7,4},{8,9},{9,10},{10,1... | collective-permute-start | bytes 589832 | tf_op jit(solution)/shard_map/ppermute | solution.py:197
  143.2 3.4 %collective-permute-start.9 = (bf16[384,256]{1,0:T(8,128)(2,1)S(1)}, bf16[384,256]{1,0:T(8,128)(2,1)S(1)}, u32[]{:S(2)}, u32[]{:S(2)}) collective-permute-start(bf16[384,256]{1,0:T(8,128)(2,1)S(1)} %add_convert_fusion.1), channel_id=1, source_target_pairs={{0,3},{1,0},{2,1},{3,2},{4,7},{5,4},{6,5},{7,6},{8,11},{9,8},{10,9... | collective-permute-start | bytes 589832 | tf_op jit(solution)/shard_map/ppermute | solution.py:197
  146.6 0.0 copy-done.5
  146.7 0.0 copy-done.6
  146.7 0.4 fusion.8
  147.1 0.7 fusion.22
  147.8 13.8 %collective-permute-done.3 = bf16[384,256]{1,0:T(8,128)(2,1)S(1)} collective-permute-done((bf16[384,256]{1,0:T(8,128)(2,1)S(1)}, bf16[384,256]{1,0:T(8,128)(2,1)S(1)}, u32[]{:S(2)}, u32[]{:S(2)}) %collective-permute-start.3) | collective-permute-done | bytes 196640 | tf_op jit(solution)/shard_map/ppermute | solution.py:197
  161.5 0.4 fusion.4
  161.9 0.0 collective-permute-done.8
  161.9 0.4 fusion.1
  162.4 0.0 collective-permute-done.9
  162.4 1.3 add_convert_fusion
  (15 shorter events, 0.2 us)
Async XLA Ops:
  0.6 122.5 %copy-start = (bf16[32,2048]{1,0:T(8,128)(2,1)S(1)}, bf16[32,2048]{1,0:T(8,128)(2,1)}, u32[]{:S(2)}) copy-start(bf16[32,2048]{1,0:T(8,128)(2,1)} %param.15) | copy-start | bytes 393220
  0.6 3.7 %collective-permute-start = (s32[1]{0:T(128)}, s32[1]{0:T(128)}, u32[]{:S(2)}, u32[]{:S(2)}) collective-permute-start(s32[1]{0:T(128)} %param.13), channel_id=1, source_target_pairs={{0,4},{4,0},{1,5},{5,1},{2,6},{6,2},{3,7},{7,3},{8,12},{12,8},{9,1... | collective-permute-start | bytes 20 | tf_op jit(solution)/shard_map/ppermute | solution.py:197
  4.3 0.7 copy-start.1
  5.0 0.7 copy-start.2
  5.7 12.4 %copy-start.7 = (bf16[384,128]{1,0:T(8,128)(2,1)S(1)}, bf16[384,128]{1,0:T(8,128)(2,1)}, u32[]{:S(2)}) copy-start(bf16[384,128]{1,0:T(8,128)(2,1)} %param.12) | copy-start | bytes 294916
  5.7 12.4 %copy-start.8 = (bf16[384,128]{1,0:T(8,128)(2,1)S(1)}, bf16[384,128]{1,0:T(8,128)(2,1)}, u32[]{:S(2)}) copy-start(bf16[384,128]{1,0:T(8,128)(2,1)} %param.11) | copy-start | bytes 294916
  7.3 24.8 %all-to-all-start = ((bf16[64,40,128]{2,1,0:T(8,128)(2,1)}), bf16[64,40,128]{2,1,0:T(8,128)(2,1)S(1)}, u32[]{:S(2)}, u32[]{:S(2)}) async-start(bf16[64,40,128]{2,1,0:T(8,128)(2,1)} %row_pack.1), calls=%async_computation | async-start | bytes 1310720 | tf_op jit(solution)/shard_map/all_to_all | solution.py:192
  18.1 3.8 %collective-permute-start.1 = (bf16[384,256]{1,0:T(8,128)(2,1)S(1)}, bf16[384,256]{1,0:T(8,128)(2,1)S(1)}, u32[]{:S(2)}, u32[]{:S(2)}) collective-permute-start(bf16[384,256]{1,0:T(8,128)(2,1)S(1)} %pad_maximum_fusion.4), channel_id=1, source_target_pairs={{0,4},{4,0},{1,5},{5,1},{2,6},{6,2},{3,7},{7,3},{8,12},{12,8},{9,1... | collective-permute-start | bytes 589832 | tf_op jit(solution)/shard_map/ppermute | solution.py:197
  22.0 26.8 %copy-start.3 = (bf16[4096,128]{1,0:T(8,128)(2,1)S(1)}, bf16[4096,128]{1,0:T(8,128)(2,1)}, u32[]{:S(2)}) copy-start(bf16[4096,128]{1,0:T(8,128)(2,1)} %param.16) | copy-start | bytes 3145732
  36.6 25.9 %all-to-all-start.1 = ((bf16[64,40,128]{2,1,0:T(8,128)(2,1)}), bf16[64,40,128]{2,1,0:T(8,128)(2,1)S(1)}, u32[]{:S(2)}, u32[]{:S(2)}) async-start(bf16[64,40,128]{2,1,0:T(8,128)(2,1)} %get-tuple-element.9), calls=%async_computation.1 | async-start | bytes 1310720 | tf_op jit(solution)/shard_map/all_to_all | solution.py:192
  51.0 37.9 %collective-permute-start.4 = (bf16[1024,128]{1,0:T(8,128)(2,1)S(1)}, bf16[1024,128]{1,0:T(8,128)(2,1)}, u32[]{:S(2)}, u32[]{:S(2)}) collective-permute-start(bf16[1024,128]{1,0:T(8,128)(2,1)S(1)} %get-tuple-element.16), channel_id=1, source_target_pairs={{0,1},{1,2},{2,3},{3,0},{4,5},{5,6},{6,7},{7,4},{8,9},{9,10},{10,1... | collective-permute-start | bytes 786440 | tf_op jit(solution)/shard_map/ppermute | solution.py:197
  64.0 50.1 %all-to-all-start.2 = ((bf16[64,24,128]{2,1,0:T(8,128)(2,1)}), bf16[64,24,128]{2,1,0:T(8,128)(2,1)S(1)}, u32[]{:S(2)}, u32[]{:S(2)}) async-start(bf16[64,24,128]{2,1,0:T(8,128)(2,1)} %row_merge.1), calls=%async_computation.2 | async-start | bytes 786432 | tf_op jit(solution)/shard_map/all_to_all | solution.py:192
  76.3 29.6 %collective-permute-start.5 = (bf16[1024,128]{1,0:T(8,128)(2,1)}, bf16[1024,128]{1,0:T(8,128)(2,1)S(1)}, u32[]{:S(2)}, u32[]{:S(2)}) collective-permute-start(bf16[1024,128]{1,0:T(8,128)(2,1)} %get-tuple-element.15), channel_id=1, source_target_pairs={{0,2},{1,3},{2,0},{3,1},{4,6},{5,7},{6,4},{7,5},{8,10},{9,11},{10,... | collective-permute-start | bytes 786440 | tf_op jit(solution)/shard_map/ppermute | solution.py:197
  86.9 21.6 %collective-permute-start.6 = (bf16[1024,128]{1,0:T(8,128)(2,1)}, bf16[1024,128]{1,0:T(8,128)(2,1)S(1)}, u32[]{:S(2)}, u32[]{:S(2)}) collective-permute-start(bf16[1024,128]{1,0:T(8,128)(2,1)} %get-tuple-element.14), channel_id=1, source_target_pairs={{0,3},{1,0},{2,1},{3,2},{4,7},{5,4},{6,5},{7,6},{8,11},{9,8},{10,9... | collective-permute-start | bytes 786440 | tf_op jit(solution)/shard_map/ppermute | solution.py:197
  108.5 14.8 %copy-start.4 = (bf16[3072,128]{1,0:T(8,128)(2,1)}, bf16[3072,128]{1,0:T(8,128)(2,1)S(1)}, u32[]{:S(2)}) copy-start(bf16[3072,128]{1,0:T(8,128)(2,1)S(1)} %constant_dynamic-update-slice_fusion) | copy-start | bytes 2359300
  108.5 19.7 %collective-permute-start.7 = (bf16[3072,128]{1,0:T(8,128)(2,1)S(1)}, bf16[3072,128]{1,0:T(8,128)(2,1)}, u32[]{:S(2)}, u32[]{:S(2)}) collective-permute-start(bf16[3072,128]{1,0:T(8,128)(2,1)S(1)} %constant_dynamic-update-slice_fusion), channel_id=1, source_target_pairs={{0,4},{4,0},{1,5},{5,1},{2,6},{6,2},{3,7},{7,3},{8,12},{12,8},{9,1... | collective-permute-start | bytes 2359304 | tf_op jit(solution)/shard_map/ppermute | solution.py:197
  114.2 9.2 %collective-permute-start.10 = (bf16[64,16,128]{2,1,0:T(8,128)(2,1)S(1)}, bf16[64,16,128]{2,1,0:T(8,128)(2,1)S(1)}, u32[]{:S(2)}, u32[]{:S(2)}) collective-permute-start(bf16[64,16,128]{2,1,0:T(8,128)(2,1)S(1)} %slice.40), channel_id=1, source_target_pairs={{0,4},{4,0},{1,5},{5,1},{2,6},{6,2},{3,7},{7,3},{8,12},{12,8},{9,1... | collective-permute-start | bytes 786440 | tf_op jit(solution)/shard_map/ppermute | solution.py:197
  120.7 16.0 %collective-permute-start.2 = (f32[384,256]{1,0:T(8,128)S(1)}, f32[384,256]{1,0:T(8,128)S(1)}, u32[]{:S(2)}, u32[]{:S(2)}) collective-permute-start(f32[384,256]{1,0:T(8,128)S(1)} %get-tuple-element.11), channel_id=1, source_target_pairs={{0,4},{4,0},{1,5},{5,1},{2,6},{6,2},{3,7},{7,3},{8,12},{12,8},{9,1... | collective-permute-start | bytes 1179656 | tf_op jit(solution)/shard_map/ppermute | solution.py:197
  124.4 10.4 %all-to-all-start.3 = ((f32[4,1,1024]{2,1,0:T(1,128)}), f32[4,1,1024]{2,1,0:T(1,128)S(1)}, u32[]{:S(2)}, u32[]{:S(2)}) async-start(f32[4,1,1024]{2,1,0:T(1,128)} %reshape.24), calls=%async_computation.3 | async-start | bytes 32768 | tf_op jit(solution)/shard_map/all_to_all | solution.py:192
  128.2 18.4 %copy-start.5 = (bf16[1024,128]{1,0:T(8,128)(2,1)S(1)}, bf16[1024,128]{1,0:T(8,128)(2,1)}, u32[]{:S(2)}) copy-start(bf16[1024,128]{1,0:T(8,128)(2,1)} %get-tuple-element.25) | copy-start | bytes 786436
  128.2 18.5 %copy-start.6 = (bf16[1024,128]{1,0:T(8,128)(2,1)S(1)}, bf16[1024,128]{1,0:T(8,128)(2,1)}, u32[]{:S(2)}) copy-start(bf16[1024,128]{1,0:T(8,128)(2,1)} %get-tuple-element.26) | copy-start | bytes 786436
  136.8 25.1 %collective-permute-start.8 = (bf16[384,256]{1,0:T(8,128)(2,1)S(1)}, bf16[384,256]{1,0:T(8,128)(2,1)S(1)}, u32[]{:S(2)}, u32[]{:S(2)}) collective-permute-start(bf16[384,256]{1,0:T(8,128)(2,1)S(1)} %add_convert_fusion.1), channel_id=1, source_target_pairs={{0,2},{1,3},{2,0},{3,1},{4,6},{5,7},{6,4},{7,5},{8,10},{9,11},{10,... | collective-permute-start | bytes 589832 | tf_op jit(solution)/shard_map/ppermute | solution.py:197
  139.2 22.3 %collective-permute-start.3 = (bf16[384,256]{1,0:T(8,128)(2,1)S(1)}, bf16[384,256]{1,0:T(8,128)(2,1)S(1)}, u32[]{:S(2)}, u32[]{:S(2)}) collective-permute-start(bf16[384,256]{1,0:T(8,128)(2,1)S(1)} %add_convert_fusion.1), channel_id=1, source_target_pairs={{0,1},{1,2},{2,3},{3,0},{4,5},{5,6},{6,7},{7,4},{8,9},{9,10},{10,1... | collective-permute-start | bytes 589832 | tf_op jit(solution)/shard_map/ppermute | solution.py:197
  143.2 19.1 %collective-permute-start.9 = (bf16[384,256]{1,0:T(8,128)(2,1)S(1)}, bf16[384,256]{1,0:T(8,128)(2,1)S(1)}, u32[]{:S(2)}, u32[]{:S(2)}) collective-permute-start(bf16[384,256]{1,0:T(8,128)(2,1)S(1)} %add_convert_fusion.1), channel_id=1, source_target_pairs={{0,3},{1,0},{2,1},{3,2},{4,7},{5,4},{6,5},{7,6},{8,11},{9,8},{10,9... | collective-permute-start | bytes 589832 | tf_op jit(solution)/shard_map/ppermute | solution.py:197

commit v3 on v2

--- a/solution.py
+++ b/solution.py
@@ -147,7 +147,9 @@
         u_ref[k, heads:, :] = found
 
 
-def second_kernel(heads, group, where_ref, place_ref, x_ref, u_ref, k_ref, v_ref, own_ref, other_ref):
+def second_kernel(
+    heads, group, where_ref, place_ref, x_ref, u_ref, k_ref, v_ref, w_ref, own_ref, other_ref
+):
     rows = x_ref.shape[0]
     slots = k_ref.shape[0]
     half = slots // 2
@@ -182,10 +184,71 @@
         value_grads += plain_dot(weights.astype(BF16), g)
         key_grads += plain_dot(score_grads.astype(BF16), q)
     key_grads *= SCALE
-    own_ref[:, :HEAD_WIDTH] = key_grads[:half]
-    own_ref[:, HEAD_WIDTH:] = value_grads[:half]
-    other_ref[:, :HEAD_WIDTH] = key_grads[half:]
-    other_ref[:, HEAD_WIDTH:] = value_grads[half:]
+    low = jnp.concatenate([u_ref[:, h, :] for h in range(heads)], axis=1)
+    features = w_ref.shape[0] // 2
+    both = rows_dot(low, w_ref[...])
+    for ref, first in ((own_ref, 0), (other_ref, 1)):
+        part = slice(first * half, (first + 1) * half)
+        ref[:half, :HEAD_WIDTH] = key_grads[part]
+        ref[:half, HEAD_WIDTH:] = value_grads[part]
+        ref[half:, :] = jnp.zeros((rows, 2 * HEAD_WIDTH), F32)
+        ref[half:, :features] = both[:, first * features : (first + 1) * features]
+
+
+def finish_kernel(groups, features, where_ref, own_ref, other_ref, k_ref, v_ref, span_ref, *out_refs):
+    half = k_ref.shape[0]
+    per = span_ref.shape[0] // 2
+    sums = (own_ref[:half, :] + other_ref[:half, :]).astype(BF16)
+    k_ref[...] = sums[:, :HEAD_WIDTH]
+    v_ref[...] = sums[:, HEAD_WIDTH:]
+    is_first = where_ref[1] == 0
+    lane = lax.broadcasted_iota(jnp.int32, (2 * per, 128), 1)
+
+    def block_rows(target):
+        start = half + per * target
+        if per % 8 == 0:
+            start = pl.multiple_of(start, 8)
+        part = pl.ds(start, per)
+        mine, theirs = own_ref[part, :128], other_ref[part, :128]
+        even = jnp.where(is_first, mine, theirs)
+        odd = jnp.where(is_first, theirs, mine)
+        return jnp.where(lane < features, jnp.concatenate([even, odd], axis=0), 0.0)
+
+    mine = where_ref[4]
+    span_ref[...] = block_rows(mine)
+    for k, ref in enumerate(out_refs, 1):
+        high, middle, low = three_parts(block_rows(lax.rem(mine + k, groups)))
+        wide = high + pltpu.roll(middle, features, 1) + pltpu.roll(low, 2 * features, 1)
+        ref[:half, :] = sums
+        ref[half:, :] = jnp.concatenate([wide, jnp.zeros_like(wide)], axis=1).astype(BF16)
+
+
+def input_kernel(groups, where_ref, own_ref, span_ref, *refs):
+    arrived, refs = refs[: groups - 1], refs[groups - 1 :]
+    own_k_ref, own_v_ref = refs[:2]
+    here, there = refs[2 : 1 + groups], refs[1 + groups : 2 * groups]
+    out_ref, block_ref, turn_ref = refs[2 * groups :]
+    half = out_ref.shape[0]
+    rows, features = block_ref.shape
+    is_first = where_ref[1] == 0
+    left = [own_ref[:half, :]]
+    span = span_ref[...]
+    for ref in arrived:
+        keys, values = ref[:half, :HEAD_WIDTH], ref[:half, HEAD_WIDTH:]
+        left += [jnp.where(is_first, keys, values), jnp.where(is_first, values, keys)]
+        wide = ref[half:, :128].astype(F32)
+        span += wide + pltpu.roll(wide, 128 - features, 1) + pltpu.roll(wide, 128 - 2 * features, 1)
+    left = jnp.concatenate(left, axis=1)
+    step = min(256, out_ref.shape[1])
+    for first in range(0, out_ref.shape[1], step):
+        part = pl.ds(first, step)
+        right = [own_k_ref[part, :], own_v_ref[part, :]]
+        for near_ref, far_ref in zip(here, there):
+            right += [near_ref[part, :], far_ref[part, :]]
+        out_ref[:, part] = rows_dot(left, jnp.concatenate(right, axis=1)).astype(BF16)
+    turn_ref[pl.ds(0, rows // 2, stride=2), :] = span[: rows // 2]
+    turn_ref[pl.ds(1, rows // 2, stride=2), :] = span[rows // 2 :]
+    block_ref[...] = turn_ref[:, :features].astype(BF16)
 
 
 def exchanged(value, axes):
@@ -225,7 +288,6 @@
         in_specs=[SMEM, SMEM, VMEM, VMEM],
         out_specs=VMEM,
         name="row_pack",
-        compiler_params=PARAMS,
     )(lengths, other_length, queries, grad_output)
     x = exchanged(row, FAR)
 
@@ -243,13 +305,19 @@
         target = lax.rem(mine + k, groups)
         piece = lax.dynamic_index_in_dim(half_weights, target, 0, keepdims=False)
         arriving.append(shifted(piece, "head", k))
-    half_all = jnp.concatenate(arriving, axis=0)
-    other_half = shifted(half_all, CORE, 1)
-    key_weights = jnp.where(first_is_key, half_all, other_half)
-    value_weights = jnp.where(first_is_key, other_half, half_all)
-    joined = jnp.concatenate([key_weights, value_weights], axis=1)
-
-    where = jnp.stack([far, core, span_index[0], jnp.int32(2 * rows)]).astype(jnp.int32)
+    other_half = []
+    for k, piece in enumerate(arriving, 1):
+        other_half.append(shifted(piece, CORE, 1))
+    own_weights = [
+        lax.dynamic_slice_in_dim(w, mine * features, features, 0)
+        for w in (key_projection_weight, value_projection_weight)
+    ]
+    other_query = shifted(w_query, CORE, 1)
+    both_query = jnp.concatenate([w_query, other_query], axis=0)
+
+    where = jnp.full((8,), 2 * rows, jnp.int32)
+    for k, number in ((0, far), (1, core), (2, span_index[0]), (4, mine)):
+        where = jnp.where(jnp.arange(8) == k, number, where)
     y, place = pl.pallas_call(
         functools.partial(first_kernel, heads, group),
         out_shape=(
@@ -271,40 +339,54 @@
         compiler_params=PARAMS,
     )(arrived)
     u = exchanged(merged, FAR)
+    width = w_query.shape[0]
     own_part, other_part = pl.pallas_call(
         functools.partial(second_kernel, heads, group),
-        out_shape=(jax.ShapeDtypeStruct((block, 2 * HEAD_WIDTH), F32),) * 2,
-        in_specs=[SMEM, SMEM, VMEM, VMEM, VMEM, VMEM],
+        out_shape=(jax.ShapeDtypeStruct((block + rows, 2 * HEAD_WIDTH), F32),) * 2,
+        in_specs=[SMEM, SMEM, VMEM, VMEM, VMEM, VMEM, VMEM],
         out_specs=(VMEM, VMEM),
         name="slot_gradients",
         compiler_params=PARAMS,
-    )(where, place, x, u, keys, values)
+    )(where, place, x, u, keys, values, both_query)
     other_sums = shifted(other_part, CORE, 1)
-    slot_grads = (own_part + other_sums).astype(BF16)
-    saved_key_gradient = slot_grads[:, :HEAD_WIDTH]
-    saved_value_gradient = slot_grads[:, HEAD_WIDTH:]
-
-    pieces = [slot_grads]
-    for k in range(1, groups):
-        pieces.append(shifted(slot_grads, "head", k))
-    own_weights = [
-        lax.dynamic_slice_in_dim(w, mine * features, features, 0)
-        for w in (key_projection_weight, value_projection_weight)
-    ]
-    total = rows_dot(slot_grads, jnp.concatenate(own_weights, axis=1))
-    for k in range(1, groups):
-        total = total + rows_dot(pieces[k], joined[(k - 1) * features : k * features])
-    cached_input_gradient = total.astype(BF16)
-
-    query_low = u[:, :heads, :]
-    other_low = shifted(query_low, CORE, 1)
-    own_rows = rows_dot(query_low.reshape(rows, -1), w_query)
-    other_rows = rows_dot(other_low.reshape(rows, -1), w_query)
-    even = jnp.where(first_is_key, own_rows, other_rows)
-    odd = jnp.where(first_is_key, other_rows, own_rows)
-    span_part = jnp.stack([even, odd], axis=1).reshape(groups, -1, w_query.shape[0])
-    arrived_parts = exchanged(span_part, "head")
-    grad_span_input = arrived_parts.sum(axis=0).astype(BF16)
+    per = rows // groups
+    saved_key_gradient, saved_value_gradient, own_span, *leaving = pl.pallas_call(
+        functools.partial(finish_kernel, groups, width),
+        out_shape=(
+            jax.ShapeDtypeStruct((block, HEAD_WIDTH), BF16),
+            jax.ShapeDtypeStruct((block, HEAD_WIDTH), BF16),
+            jax.ShapeDtypeStruct((2 * per, 128), F32),
+        )
+        + (jax.ShapeDtypeStruct((block + 2 * per, 2 * HEAD_WIDTH), BF16),) * (groups - 1),
+        in_specs=[SMEM, VMEM, VMEM],
+        out_specs=(VMEM,) * (2 + groups),
+        name="slot_sums",
+        compiler_params=PARAMS,
+    )(where, own_part, other_sums)
+
+    pieces = []
+    for k, piece in enumerate(leaving, 1):
+        pieces.append(shifted(piece, "head", k))
+    cached_input_gradient, grad_span_input = pl.pallas_call(
+        functools.partial(input_kernel, groups),
+        out_shape=(
+            jax.ShapeDtypeStruct((block, features), BF16),
+            jax.ShapeDtypeStruct((2 * per, width), BF16),
+        ),
+        in_specs=[SMEM] + [VMEM] * (1 + 3 * groups),
+        out_specs=(VMEM, VMEM),
+        scratch_shapes=[pltpu.VMEM((2 * per, 128), F32)],
+        name="input_gradient",
+        compiler_params=PARAMS,
+    )(
+        where,
+        leaving[0],
+        own_span,
+        *pieces,
+        *own_weights,
+        *arriving,
+        *other_half,
+    )
     return (saved_key_gradient, saved_value_gradient, cached_input_gradient, grad_span_input)
 
 

time: 165 us -> 164 us (level)
  the two profiles are of different devices: /device:TPU:103 before, /device:TPU:8 now
where the time goes in v3:
time: 164 us; the launch traced here: 163 us
  starting transfers between devices  84.2 us (51%)
  waiting for transfers between devices  58.3 us (36%)
  Pallas kernels  15.2 us (9%)
  other arithmetic  2.39 us (1%)
  between operations  2.21 us (1%)
    ppermute x13, starting transfers between devices, shifted(): lax.ppermute(value, axis, [(k, (k + by) % count) for k in range(count)])  57.5 us
    all_to_all x3, waiting for transfers between devices, exchanged(): return lax.all_to_all(value, axes, split_axis=0, concat_axis=0, tiled=True)  34.7 us
    all_to_all x3, starting transfers between devices, exchanged(): return lax.all_to_all(value, axes, split_axis=0, concat_axis=0, tiled=True)  26.7 us
    ppermute x13, waiting for transfers between devices, shifted(): lax.ppermute(value, axis, [(k, (k + by) % count) for k in range(count)])  23.7 us
    pallas_call x1, Pallas kernels, local(): pl.pallas_call(functools.partial(first_kernel, heads, group), out_shape=(...  4.52 us
  transfers between devices with their start and end apart: 16, of which 10 were waited for; matrix products, arithmetic and copies ran while one was open for 2% of the time, Pallas kernels for 4%

profile of v3, /device:TPU:8, one launch (start us, length us, event | category | flops | bytes accessed | tf_op | source)
XLA Modules:
  0.0 163.5 jit_solution(15616665634734736334)
XLA Ops:
  0.6 1.9 %collective-permute-start = (s32[1]{0:T(128)}, s32[1]{0:T(128)}, u32[]{:S(2)}, u32[]{:S(2)}) collective-permute-start(s32[1]{0:T(128)} %param.13), channel_id=1, source_target_pairs={{0,4},{4,0},{1,5},{5,1},{2,6},{6,2},{3,7},{7,3},{8,12},{12,8},{9,1... | collective-permute-start | bytes 20 | tf_op jit(solution)/shard_map/ppermute | solution.py:260
  3.2 0.6 collective-permute-done.other_ref
  3.8 2.3 %row_pack.1 = bf16[64,40,128]{2,1,0:T(8,128)(2,1)} custom-call(s32[1]{0:T(128)S(6)} %copy.13.own_ref, s32[1]{0:T(128)} %collective-permute-done.other_ref, bf16[1,2048]{1,0:T(2,128)(2,1)} %q_ref.1, bf16[1,2048]{1,0:T(2,128)(2,1)} %g_ref.1), custom_call_target="tpu_custom_call" | custom-call | tf_op jit(solution)/shard_map/row_pack/pallas_call | solution.py:285
  6.1 0.0 copy-start
  6.1 0.0 copy-start.1
  6.1 12.5 %all-to-all-start = ((bf16[64,40,128]{2,1,0:T(8,128)(2,1)}), bf16[64,40,128]{2,1,0:T(8,128)(2,1)S(1)}, u32[]{:S(2)}, u32[]{:S(2)}) async-start(bf16[64,40,128]{2,1,0:T(8,128)(2,1)} %row_pack.1), calls=%async_computation | async-start | bytes 1310720 | tf_op jit(solution)/shard_map/all_to_all | solution.py:255
  18.6 0.0 copy-done
  18.6 0.0 copy-done.1
  18.7 1.9 %collective-permute-start.1 = (bf16[384,256]{1,0:T(8,128)(2,1)S(1)}, bf16[384,256]{1,0:T(8,128)(2,1)S(1)}, u32[]{:S(2)}, u32[]{:S(2)}) collective-permute-start(bf16[384,256]{1,0:T(8,128)(2,1)S(1)} %pad_maximum_fusion.1), channel_id=1, source_target_pairs={{0,4},{4,0},{1,5},{5,1},{2,6},{6,2},{3,7},{7,3},{8,12},{12,8},{9,1... | collective-permute-start | bytes 589832 | tf_op jit(solution)/shard_map/ppermute | solution.py:260
  21.3 0.7 collective-permute-done.1
  22.0 16.4 %all-to-all-done.x_ref = bf16[64,40,128]{2,1,0:T(8,128)(2,1)S(1)} async-done(((bf16[64,40,128]{2,1,0:T(8,128)(2,1)}), bf16[64,40,128]{2,1,0:T(8,128)(2,1)S(1)}, u32[]{:S(2)}, u32[]{:S(2)}) %all-to-all-start) | async-done | bytes 655392 | tf_op jit(solution)/shard_map/all_to_all | solution.py:255
  38.4 4.5 %row_partials.1 = (bf16[64,40,128]{2,1,0:T(8,128)(2,1)}, f32[4]{0:T(128)S(1)}) custom-call(s32[8]{0:T(128)S(1)} %compare_select_fusion.3.where_ref, bf16[64,40,128]{2,1,0:T(8,128)(2,1)S(1)} %all-to-all-done.x_ref, bf16[768,128]{1,0:T(8,128)(2,1)S(1)} %get-tuple-element.33.k_ref, bf16[768,128]{1,0:T(8,128)(2,1)S(1)} %get-tuple-element.34.v_ref), custom_call_target="tpu_custom_call" | custom-call | tf_op jit(solution)/shard_map/row_partials/pallas_call | solution.py:321
  42.9 7.0 %all-to-all-start.1 = ((bf16[64,40,128]{2,1,0:T(8,128)(2,1)}), bf16[64,40,128]{2,1,0:T(8,128)(2,1)S(1)}, u32[]{:S(2)}, u32[]{:S(2)}) async-start(bf16[64,40,128]{2,1,0:T(8,128)(2,1)} %get-tuple-element.17), calls=%async_computation.1 | async-start | bytes 1310720 | tf_op jit(solution)/shard_map/all_to_all | solution.py:255
  50.0 1.9 %collective-permute-start.2 = (bf16[32,2048]{1,0:T(8,128)(2,1)}, bf16[32,2048]{1,0:T(8,128)(2,1)}, u32[]{:S(2)}, u32[]{:S(2)}) collective-permute-start(bf16[32,2048]{1,0:T(8,128)(2,1)} %param.15), channel_id=1, source_target_pairs={{0,4},{4,0},{1,5},{5,1},{2,6},{6,2},{3,7},{7,3},{8,12},{12,8},{9,1... | collective-permute-start | bytes 393224 | tf_op jit(solution)/shard_map/ppermute | solution.py:260
  51.9 17.0 %all-to-all-done.1.z_ref = bf16[64,40,128]{2,1,0:T(8,128)(2,1)S(1)} async-done(((bf16[64,40,128]{2,1,0:T(8,128)(2,1)}), bf16[64,40,128]{2,1,0:T(8,128)(2,1)S(1)}, u32[]{:S(2)}, u32[]{:S(2)}) %all-to-all-start.1) | async-done | bytes 655392 | tf_op jit(solution)/shard_map/all_to_all | solution.py:255
  68.9 1.5 row_merge.1
  70.4 7.2 %all-to-all-start.2 = ((bf16[64,24,128]{2,1,0:T(8,128)(2,1)}), bf16[64,24,128]{2,1,0:T(8,128)(2,1)S(1)}, u32[]{:S(2)}, u32[]{:S(2)}) async-start(bf16[64,24,128]{2,1,0:T(8,128)(2,1)} %row_merge.1), calls=%async_computation.2 | async-start | bytes 786432 | tf_op jit(solution)/shard_map/all_to_all | solution.py:255
  77.7 1.3 broadcast_select_fusion
  79.0 0.1 dynamic-slice_bitcast_fusion
  79.1 10.0 %collective-permute-start.9 = (bf16[1024,128]{1,0:T(8,128)(2,1)S(1)}, bf16[1024,128]{1,0:T(8,128)(2,1)S(1)}, u32[]{:S(2)}, u32[]{:S(2)}) collective-permute-start(bf16[1024,128]{1,0:T(8,128)(2,1)S(1)} %get-tuple-element.28), channel_id=1, source_target_pairs={{0,3},{1,0},{2,1},{3,2},{4,7},{5,4},{6,5},{7,6},{8,11},{9,8},{10,9... | collective-permute-start | bytes 786440 | tf_op jit(solution)/shard_map/ppermute | solution.py:260
  89.1 0.0 collective-permute-done.2
  89.2 1.0 pad_maximum_fusion.w_ref
  90.1 1.3 all-to-all-done.2.u_ref
  91.5 3.1 %slot_gradients.1 = (f32[448,256]{1,0:T(8,128)S(1)}, f32[448,256]{1,0:T(8,128)S(1)}) custom-call(s32[8]{0:T(128)S(1)} %compare_select_fusion.3.where_ref, f32[4]{0:T(128)S(1)} %get-tuple-element.16.place_ref, bf16[64,40,128]{2,1,0:T(8,128)(2,1)S(1)} %all-to-all-done.x_ref, bf16[64,24,128]{2,1,0:T(8,128)(2,1)S(1)} %all-to-all-done.2.u_ref, ...), custom_call_target="tpu_custom_call" | custom-call | tf_op jit(solution)/shard_map/slot_gradients/pallas_call | solution.py:343
  94.6 1.9 %collective-permute-start.3 = (f32[448,256]{1,0:T(8,128)S(1)}, f32[448,256]{1,0:T(8,128)S(1)}, u32[]{:S(2)}, u32[]{:S(2)}) collective-permute-start(f32[448,256]{1,0:T(8,128)S(1)} %get-tuple-element.19), channel_id=1, source_target_pairs={{0,4},{4,0},{1,5},{5,1},{2,6},{6,2},{3,7},{7,3},{8,12},{12,8},{9,1... | collective-permute-start | bytes 1376264 | tf_op jit(solution)/shard_map/ppermute | solution.py:260
  96.5 10.2 %collective-permute-start.8 = (bf16[1024,128]{1,0:T(8,128)(2,1)S(1)}, bf16[1024,128]{1,0:T(8,128)(2,1)S(1)}, u32[]{:S(2)}, u32[]{:S(2)}) collective-permute-start(bf16[1024,128]{1,0:T(8,128)(2,1)S(1)} %get-tuple-element.29), channel_id=1, source_target_pairs={{0,2},{1,3},{2,0},{3,1},{4,6},{5,7},{6,4},{7,5},{8,10},{9,11},{10,... | collective-permute-start | bytes 786440 | tf_op jit(solution)/shard_map/ppermute | solution.py:260
  106.8 4.1 %collective-permute-start.7 = (bf16[1024,128]{1,0:T(8,128)(2,1)S(1)}, bf16[1024,128]{1,0:T(8,128)(2,1)S(1)}, u32[]{:S(2)}, u32[]{:S(2)}) collective-permute-start(bf16[1024,128]{1,0:T(8,128)(2,1)S(1)} %get-tuple-element.30), channel_id=1, source_target_pairs={{0,1},{1,2},{2,3},{3,0},{4,5},{5,6},{6,7},{7,4},{8,9},{9,10},{10,1... | collective-permute-start | bytes 786440 | tf_op jit(solution)/shard_map/ppermute | solution.py:260
  110.8 0.0 collective-permute-done.9.refs_7_
  110.9 1.9 %collective-permute-start.12 = (bf16[1024,128]{1,0:T(8,128)(2,1)S(1)}, bf16[1024,128]{1,0:T(8,128)(2,1)S(1)}, u32[]{:S(2)}, u32[]{:S(2)}) collective-permute-start(bf16[1024,128]{1,0:T(8,128)(2,1)S(1)} %collective-permute-done.9.refs_7_), channel_id=1, source_target_pairs={{0,4},{4,0},{1,5},{5,1},{2,6},{6,2},{3,7},{7,3},{8,12},{12,8},{9,1... | collective-permute-start | bytes 786440 | tf_op jit(solution)/shard_map/ppermute | solution.py:260
  112.8 6.0 %collective-permute-done.8.refs_6_ = bf16[1024,128]{1,0:T(8,128)(2,1)S(1)} collective-permute-done((bf16[1024,128]{1,0:T(8,128)(2,1)S(1)}, bf16[1024,128]{1,0:T(8,128)(2,1)S(1)}, u32[]{:S(2)}, u32[]{:S(2)}) %collective-permute-start.8) | collective-permute-done | bytes 262176 | tf_op jit(solution)/shard_map/ppermute | solution.py:260
  118.8 1.9 %collective-permute-start.11 = (bf16[1024,128]{1,0:T(8,128)(2,1)S(1)}, bf16[1024,128]{1,0:T(8,128)(2,1)S(1)}, u32[]{:S(2)}, u32[]{:S(2)}) collective-permute-start(bf16[1024,128]{1,0:T(8,128)(2,1)S(1)} %collective-permute-done.8.refs_6_), channel_id=1, source_target_pairs={{0,4},{4,0},{1,5},{5,1},{2,6},{6,2},{3,7},{7,3},{8,12},{12,8},{9,1... | collective-permute-start | bytes 786440 | tf_op jit(solution)/shard_map/ppermute | solution.py:260
  120.7 4.3 %collective-permute-done.7.refs_5_ = bf16[1024,128]{1,0:T(8,128)(2,1)S(1)} collective-permute-done((bf16[1024,128]{1,0:T(8,128)(2,1)S(1)}, bf16[1024,128]{1,0:T(8,128)(2,1)S(1)}, u32[]{:S(2)}, u32[]{:S(2)}) %collective-permute-start.7) | collective-permute-done | bytes 262176 | tf_op jit(solution)/shard_map/ppermute | solution.py:260
  125.0 1.9 %collective-permute-start.10 = (bf16[1024,128]{1,0:T(8,128)(2,1)S(1)}, bf16[1024,128]{1,0:T(8,128)(2,1)S(1)}, u32[]{:S(2)}, u32[]{:S(2)}) collective-permute-start(bf16[1024,128]{1,0:T(8,128)(2,1)S(1)} %collective-permute-done.7.refs_5_), channel_id=1, source_target_pairs={{0,4},{4,0},{1,5},{5,1},{2,6},{6,2},{3,7},{7,3},{8,12},{12,8},{9,1... | collective-permute-start | bytes 786440 | tf_op jit(solution)/shard_map/ppermute | solution.py:260
  126.9 0.0 collective-permute-done.3.other_ref
  126.9 1.3 slot_sums.1
  128.2 13.0 %collective-permute-start.5 = (bf16[416,256]{1,0:T(8,128)(2,1)S(1)}, bf16[416,256]{1,0:T(8,128)(2,1)S(1)}, u32[]{:S(2)}, u32[]{:S(2)}) collective-permute-start(bf16[416,256]{1,0:T(8,128)(2,1)S(1)} %get-tuple-element.24), channel_id=1, source_target_pairs={{0,2},{1,3},{2,0},{3,1},{4,6},{5,7},{6,4},{7,5},{8,10},{9,11},{10,... | collective-permute-start | bytes 638984 | tf_op jit(solution)/shard_map/ppermute | solution.py:260
  141.2 2.4 %collective-permute-start.6 = (bf16[416,256]{1,0:T(8,128)(2,1)S(1)}, bf16[416,256]{1,0:T(8,128)(2,1)S(1)}, u32[]{:S(2)}, u32[]{:S(2)}) collective-permute-start(bf16[416,256]{1,0:T(8,128)(2,1)S(1)} %get-tuple-element.25), channel_id=1, source_target_pairs={{0,3},{1,0},{2,1},{3,2},{4,7},{5,4},{6,5},{7,6},{8,11},{9,8},{10,9... | collective-permute-start | bytes 638984 | tf_op jit(solution)/shard_map/ppermute | solution.py:260
  143.6 0.0 collective-permute-done.12.refs_10_
  143.6 4.3 %collective-permute-start.4 = (bf16[416,256]{1,0:T(8,128)(2,1)S(1)}, bf16[416,256]{1,0:T(8,128)(2,1)S(1)}, u32[]{:S(2)}, u32[]{:S(2)}) collective-permute-start(bf16[416,256]{1,0:T(8,128)(2,1)S(1)} %get-tuple-element.22.own_ref), channel_id=1, source_target_pairs={{0,1},{1,2},{2,3},{3,0},{4,5},{5,6},{6,7},{7,4},{8,9},{9,10},{10,1... | collective-permute-start | bytes 638984 | tf_op jit(solution)/shard_map/ppermute | solution.py:260
  147.9 1.1 constant_dynamic-slice_fusion
  149.0 0.0 collective-permute-done.11.refs_9_
  149.0 0.0 collective-permute-done.10.refs_8_
  149.0 2.8 %collective-permute-done.5.refs_1_ = bf16[416,256]{1,0:T(8,128)(2,1)S(1)} collective-permute-done((bf16[416,256]{1,0:T(8,128)(2,1)S(1)}, bf16[416,256]{1,0:T(8,128)(2,1)S(1)}, u32[]{:S(2)}, u32[]{:S(2)}) %collective-permute-start.5) | collective-permute-done | bytes 213024 | tf_op jit(solution)/shard_map/ppermute | solution.py:260
  151.9 7.1 %collective-permute-done.6.refs_2_ = bf16[416,256]{1,0:T(8,128)(2,1)S(1)} collective-permute-done((bf16[416,256]{1,0:T(8,128)(2,1)S(1)}, bf16[416,256]{1,0:T(8,128)(2,1)S(1)}, u32[]{:S(2)}, u32[]{:S(2)}) %collective-permute-start.6) | collective-permute-done | bytes 213024 | tf_op jit(solution)/shard_map/ppermute | solution.py:260
  159.0 2.1 %collective-permute-done.4.refs_0_ = bf16[416,256]{1,0:T(8,128)(2,1)S(1)} collective-permute-done((bf16[416,256]{1,0:T(8,128)(2,1)S(1)}, bf16[416,256]{1,0:T(8,128)(2,1)S(1)}, u32[]{:S(2)}, u32[]{:S(2)}) %collective-permute-start.4) | collective-permute-done | bytes 213024 | tf_op jit(solution)/shard_map/ppermute | solution.py:260
  161.0 2.4 %input_gradient.1 = (bf16[384,1024]{1,0:T(8,128)(2,1)}, bf16[32,32]{1,0:T(8,128)(2,1)}) custom-call(s32[8]{0:T(128)S(1)} %compare_select_fusion.3.where_ref, bf16[416,256]{1,0:T(8,128)(2,1)S(1)} %get-tuple-element.22.own_ref, f32[32,128]{1,0:T(8,128)S(1)} %get-tuple-element.23.span_ref, bf16[416,256]{1,0:T(8,128)(2,1)S(1)} %collective-permute-done.4.refs_0_, ...), custom_call_target="tpu_custom_call" | custom-call | tf_op jit(solution)/shard_map/input_gradient/pallas_call | solution.py:370
  (4 shorter events, 0.1 us)
Async XLA Ops:
  0.6 3.2 %collective-permute-start = (s32[1]{0:T(128)}, s32[1]{0:T(128)}, u32[]{:S(2)}, u32[]{:S(2)}) collective-permute-start(s32[1]{0:T(128)} %param.13), channel_id=1, source_target_pairs={{0,4},{4,0},{1,5},{5,1},{2,6},{6,2},{3,7},{7,3},{8,12},{12,8},{9,1... | collective-permute-start | bytes 20 | tf_op jit(solution)/shard_map/ppermute | solution.py:260
  6.1 12.5 %copy-start = (bf16[384,128]{1,0:T(8,128)(2,1)S(1)}, bf16[384,128]{1,0:T(8,128)(2,1)}, u32[]{:S(2)}) copy-start(bf16[384,128]{1,0:T(8,128)(2,1)} %param.12) | copy-start | bytes 294916
  6.1 12.5 %copy-start.1 = (bf16[384,128]{1,0:T(8,128)(2,1)S(1)}, bf16[384,128]{1,0:T(8,128)(2,1)}, u32[]{:S(2)}) copy-start(bf16[384,128]{1,0:T(8,128)(2,1)} %param.11) | copy-start | bytes 294916
  6.1 32.3 %all-to-all-start = ((bf16[64,40,128]{2,1,0:T(8,128)(2,1)}), bf16[64,40,128]{2,1,0:T(8,128)(2,1)S(1)}, u32[]{:S(2)}, u32[]{:S(2)}) async-start(bf16[64,40,128]{2,1,0:T(8,128)(2,1)} %row_pack.1), calls=%async_computation | async-start | bytes 1310720 | tf_op jit(solution)/shard_map/all_to_all | solution.py:255
  18.7 3.3 %collective-permute-start.1 = (bf16[384,256]{1,0:T(8,128)(2,1)S(1)}, bf16[384,256]{1,0:T(8,128)(2,1)S(1)}, u32[]{:S(2)}, u32[]{:S(2)}) collective-permute-start(bf16[384,256]{1,0:T(8,128)(2,1)S(1)} %pad_maximum_fusion.1), channel_id=1, source_target_pairs={{0,4},{4,0},{1,5},{5,1},{2,6},{6,2},{3,7},{7,3},{8,12},{12,8},{9,1... | collective-permute-start | bytes 589832 | tf_op jit(solution)/shard_map/ppermute | solution.py:260
  42.9 25.9 %all-to-all-start.1 = ((bf16[64,40,128]{2,1,0:T(8,128)(2,1)}), bf16[64,40,128]{2,1,0:T(8,128)(2,1)S(1)}, u32[]{:S(2)}, u32[]{:S(2)}) async-start(bf16[64,40,128]{2,1,0:T(8,128)(2,1)} %get-tuple-element.17), calls=%async_computation.1 | async-start | bytes 1310720 | tf_op jit(solution)/shard_map/all_to_all | solution.py:255
  50.0 39.2 %collective-permute-start.2 = (bf16[32,2048]{1,0:T(8,128)(2,1)}, bf16[32,2048]{1,0:T(8,128)(2,1)}, u32[]{:S(2)}, u32[]{:S(2)}) collective-permute-start(bf16[32,2048]{1,0:T(8,128)(2,1)} %param.15), channel_id=1, source_target_pairs={{0,4},{4,0},{1,5},{5,1},{2,6},{6,2},{3,7},{7,3},{8,12},{12,8},{9,1... | collective-permute-start | bytes 393224 | tf_op jit(solution)/shard_map/ppermute | solution.py:260
  70.4 21.0 %all-to-all-start.2 = ((bf16[64,24,128]{2,1,0:T(8,128)(2,1)}), bf16[64,24,128]{2,1,0:T(8,128)(2,1)S(1)}, u32[]{:S(2)}, u32[]{:S(2)}) async-start(bf16[64,24,128]{2,1,0:T(8,128)(2,1)} %row_merge.1), calls=%async_computation.2 | async-start | bytes 786432 | tf_op jit(solution)/shard_map/all_to_all | solution.py:255
  79.1 31.8 %collective-permute-start.9 = (bf16[1024,128]{1,0:T(8,128)(2,1)S(1)}, bf16[1024,128]{1,0:T(8,128)(2,1)S(1)}, u32[]{:S(2)}, u32[]{:S(2)}) collective-permute-start(bf16[1024,128]{1,0:T(8,128)(2,1)S(1)} %get-tuple-element.28), channel_id=1, source_target_pairs={{0,3},{1,0},{2,1},{3,2},{4,7},{5,4},{6,5},{7,6},{8,11},{9,8},{10,9... | collective-permute-start | bytes 786440 | tf_op jit(solution)/shard_map/ppermute | solution.py:260
  94.6 32.3 %collective-permute-start.3 = (f32[448,256]{1,0:T(8,128)S(1)}, f32[448,256]{1,0:T(8,128)S(1)}, u32[]{:S(2)}, u32[]{:S(2)}) collective-permute-start(f32[448,256]{1,0:T(8,128)S(1)} %get-tuple-element.19), channel_id=1, source_target_pairs={{0,4},{4,0},{1,5},{5,1},{2,6},{6,2},{3,7},{7,3},{8,12},{12,8},{9,1... | collective-permute-start | bytes 1376264 | tf_op jit(solution)/shard_map/ppermute | solution.py:260
  96.5 22.3 %collective-permute-start.8 = (bf16[1024,128]{1,0:T(8,128)(2,1)S(1)}, bf16[1024,128]{1,0:T(8,128)(2,1)S(1)}, u32[]{:S(2)}, u32[]{:S(2)}) collective-permute-start(bf16[1024,128]{1,0:T(8,128)(2,1)S(1)} %get-tuple-element.29), channel_id=1, source_target_pairs={{0,2},{1,3},{2,0},{3,1},{4,6},{5,7},{6,4},{7,5},{8,10},{9,11},{10,... | collective-permute-start | bytes 786440 | tf_op jit(solution)/shard_map/ppermute | solution.py:260
  106.8 18.2 %collective-permute-start.7 = (bf16[1024,128]{1,0:T(8,128)(2,1)S(1)}, bf16[1024,128]{1,0:T(8,128)(2,1)S(1)}, u32[]{:S(2)}, u32[]{:S(2)}) collective-permute-start(bf16[1024,128]{1,0:T(8,128)(2,1)S(1)} %get-tuple-element.30), channel_id=1, source_target_pairs={{0,1},{1,2},{2,3},{3,0},{4,5},{5,6},{6,7},{7,4},{8,9},{9,10},{10,1... | collective-permute-start | bytes 786440 | tf_op jit(solution)/shard_map/ppermute | solution.py:260
  110.9 32.7 %collective-permute-start.12 = (bf16[1024,128]{1,0:T(8,128)(2,1)S(1)}, bf16[1024,128]{1,0:T(8,128)(2,1)S(1)}, u32[]{:S(2)}, u32[]{:S(2)}) collective-permute-start(bf16[1024,128]{1,0:T(8,128)(2,1)S(1)} %collective-permute-done.9.refs_7_), channel_id=1, source_target_pairs={{0,4},{4,0},{1,5},{5,1},{2,6},{6,2},{3,7},{7,3},{8,12},{12,8},{9,1... | collective-permute-start | bytes 786440 | tf_op jit(solution)/shard_map/ppermute | solution.py:260
  118.8 30.2 %collective-permute-start.11 = (bf16[1024,128]{1,0:T(8,128)(2,1)S(1)}, bf16[1024,128]{1,0:T(8,128)(2,1)S(1)}, u32[]{:S(2)}, u32[]{:S(2)}) collective-permute-start(bf16[1024,128]{1,0:T(8,128)(2,1)S(1)} %collective-permute-done.8.refs_6_), channel_id=1, source_target_pairs={{0,4},{4,0},{1,5},{5,1},{2,6},{6,2},{3,7},{7,3},{8,12},{12,8},{9,1... | collective-permute-start | bytes 786440 | tf_op jit(solution)/shard_map/ppermute | solution.py:260
  125.0 24.0 %collective-permute-start.10 = (bf16[1024,128]{1,0:T(8,128)(2,1)S(1)}, bf16[1024,128]{1,0:T(8,128)(2,1)S(1)}, u32[]{:S(2)}, u32[]{:S(2)}) collective-permute-start(bf16[1024,128]{1,0:T(8,128)(2,1)S(1)} %collective-permute-done.7.refs_5_), channel_id=1, source_target_pairs={{0,4},{4,0},{1,5},{5,1},{2,6},{6,2},{3,7},{7,3},{8,12},{12,8},{9,1... | collective-permute-start | bytes 786440 | tf_op jit(solution)/shard_map/ppermute | solution.py:260
  128.2 23.7 %collective-permute-start.5 = (bf16[416,256]{1,0:T(8,128)(2,1)S(1)}, bf16[416,256]{1,0:T(8,128)(2,1)S(1)}, u32[]{:S(2)}, u32[]{:S(2)}) collective-permute-start(bf16[416,256]{1,0:T(8,128)(2,1)S(1)} %get-tuple-element.24), channel_id=1, source_target_pairs={{0,2},{1,3},{2,0},{3,1},{4,6},{5,7},{6,4},{7,5},{8,10},{9,11},{10,... | collective-permute-start | bytes 638984 | tf_op jit(solution)/shard_map/ppermute | solution.py:260
  141.2 17.8 %collective-permute-start.6 = (bf16[416,256]{1,0:T(8,128)(2,1)S(1)}, bf16[416,256]{1,0:T(8,128)(2,1)S(1)}, u32[]{:S(2)}, u32[]{:S(2)}) collective-permute-start(bf16[416,256]{1,0:T(8,128)(2,1)S(1)} %get-tuple-element.25), channel_id=1, source_target_pairs={{0,3},{1,0},{2,1},{3,2},{4,7},{5,4},{6,5},{7,6},{8,11},{9,8},{10,9... | collective-permute-start | bytes 638984 | tf_op jit(solution)/shard_map/ppermute | solution.py:260
  143.6 17.5 %collective-permute-start.4 = (bf16[416,256]{1,0:T(8,128)(2,1)S(1)}, bf16[416,256]{1,0:T(8,128)(2,1)S(1)}, u32[]{:S(2)}, u32[]{:S(2)}) collective-permute-start(bf16[416,256]{1,0:T(8,128)(2,1)S(1)} %get-tuple-element.22.own_ref), channel_id=1, source_target_pairs={{0,1},{1,2},{2,3},{3,0},{4,5},{5,6},{6,7},{7,4},{8,9},{9,10},{10,1... | collective-permute-start | bytes 638984 | tf_op jit(solution)/shard_map/ppermute | solution.py:260

commit v4 on v3

--- a/solution.py
+++ b/solution.py
@@ -216,35 +216,50 @@
 
     mine = where_ref[4]
     span_ref[...] = block_rows(mine)
-    for k, ref in enumerate(out_refs, 1):
-        high, middle, low = three_parts(block_rows(lax.rem(mine + k, groups)))
+
+    def share_of(target):
+        high, middle, low = three_parts(block_rows(target))
         wide = high + pltpu.roll(middle, features, 1) + pltpu.roll(low, 2 * features, 1)
-        ref[:half, :] = sums
-        ref[half:, :] = jnp.concatenate([wide, jnp.zeros_like(wide)], axis=1).astype(BF16)
-
-
-def input_kernel(groups, where_ref, own_ref, span_ref, *refs):
-    arrived, refs = refs[: groups - 1], refs[groups - 1 :]
-    own_k_ref, own_v_ref = refs[:2]
-    here, there = refs[2 : 1 + groups], refs[1 + groups : 2 * groups]
-    out_ref, block_ref, turn_ref = refs[2 * groups :]
-    half = out_ref.shape[0]
+        return jnp.concatenate([wide, jnp.zeros_like(wide)], axis=1).astype(BF16)
+
+    cut = half // 2
+    upper, lower = sums[:cut], sums[cut:]
+    relayed_ref, back_ref, ahead_ref, behind_ref = out_refs
+    relayed_ref[:cut, :] = upper
+    relayed_ref[cut:, :] = share_of(lax.rem(mine + 2, groups))
+    back_ref[...] = lower
+    ahead_ref[:cut, :] = lower
+    ahead_ref[cut:, :] = share_of(lax.rem(mine + 1, groups))
+    behind_ref[:cut, :] = upper
+    behind_ref[cut:, :] = share_of(lax.rem(mine + 3, groups))
+
+
+def input_kernel(groups, sharers, where_ref, *refs):
+    own_upper_ref, own_lower_ref, span_ref = refs[:3]
+    arrived = (refs[3:5], refs[5:7], refs[7:9])
+    own_k_ref, own_v_ref = refs[9:11]
+    here, there = refs[11 : 11 + sharers], refs[11 + sharers : 11 + 2 * sharers]
+    out_ref, block_ref, turn_ref = refs[11 + 2 * sharers :]
+    cut = out_ref.shape[0] // 2
     rows, features = block_ref.shape
     is_first = where_ref[1] == 0
-    left = [own_ref[:half, :]]
+    left = [jnp.concatenate([own_upper_ref[:cut, :], own_lower_ref[:cut, :]], axis=0)]
     span = span_ref[...]
-    for ref in arrived:
-        keys, values = ref[:half, :HEAD_WIDTH], ref[:half, HEAD_WIDTH:]
+    for upper_ref, lower_ref in arrived:
+        both = jnp.concatenate([upper_ref[:cut, :], lower_ref[:cut, :]], axis=0)
+        keys, values = both[:, :HEAD_WIDTH], both[:, HEAD_WIDTH:]
         left += [jnp.where(is_first, keys, values), jnp.where(is_first, values, keys)]
-        wide = ref[half:, :128].astype(F32)
+    for ref in (arrived[0][1], arrived[1][0], arrived[2][0]):
+        wide = ref[cut:, :128].astype(F32)
         span += wide + pltpu.roll(wide, 128 - features, 1) + pltpu.roll(wide, 128 - 2 * features, 1)
     left = jnp.concatenate(left, axis=1)
-    step = min(256, out_ref.shape[1])
-    for first in range(0, out_ref.shape[1], step):
-        part = pl.ds(first, step)
+    share = out_ref.shape[1] // sharers
+    for k, (near_ref, far_ref) in enumerate(zip(here, there)):
+        first = lax.rem(where_ref[5] - k + sharers, sharers) * share
+        part = pl.ds(pl.multiple_of(first, share), share)
         right = [own_k_ref[part, :], own_v_ref[part, :]]
-        for near_ref, far_ref in zip(here, there):
-            right += [near_ref[part, :], far_ref[part, :]]
+        for other in range(groups - 1):
+            right += [ref[other * share : (other + 1) * share, :] for ref in (near_ref, far_ref)]
         out_ref[:, part] = rows_dot(left, jnp.concatenate(right, axis=1)).astype(BF16)
     turn_ref[pl.ds(0, rows // 2, stride=2), :] = span[: rows // 2]
     turn_ref[pl.ds(1, rows // 2, stride=2), :] = span[rows // 2 :]
@@ -297,17 +312,21 @@
     values = jnp.concatenate([saved_value_rows, other_cache[:, HEAD_WIDTH:]], axis=0)
 
     features = key_projection_weight.shape[0] // groups
+    sharers = lax.axis_size("seq_0")
+    share = features // sharers
     first_is_key = core == 0
     half_weights = jnp.where(first_is_key, key_projection_weight, value_projection_weight)
-    half_weights = half_weights.reshape(groups, features, HEAD_WIDTH)
     arriving = []
     for k in range(1, groups):
-        target = lax.rem(mine + k, groups)
-        piece = lax.dynamic_index_in_dim(half_weights, target, 0, keepdims=False)
+        start = lax.rem(mine + k, groups) * features + lax.axis_index("seq_0") * share
+        piece = lax.dynamic_slice_in_dim(half_weights, start, share, 0)
         arriving.append(shifted(piece, "head", k))
-    other_half = []
-    for k, piece in enumerate(arriving, 1):
-        other_half.append(shifted(piece, CORE, 1))
+    near = [jnp.concatenate(arriving, axis=0)]
+    for k in range(1, sharers):
+        near.append(shifted(near[0], "seq_0", k))
+    there = []
+    for piece in near:
+        there.append(shifted(piece, CORE, 1))
     own_weights = [
         lax.dynamic_slice_in_dim(w, mine * features, features, 0)
         for w in (key_projection_weight, value_projection_weight)
@@ -316,7 +335,7 @@
     both_query = jnp.concatenate([w_query, other_query], axis=0)
 
     where = jnp.full((8,), 2 * rows, jnp.int32)
-    for k, number in ((0, far), (1, core), (2, span_index[0]), (4, mine)):
+    for k, number in ((0, far), (1, core), (2, span_index[0]), (4, mine), (5, lax.axis_index("seq_0"))):
         where = jnp.where(jnp.arange(8) == k, number, where)
     y, place = pl.pallas_call(
         functools.partial(first_kernel, heads, group),
@@ -357,35 +376,48 @@
             jax.ShapeDtypeStruct((block, HEAD_WIDTH), BF16),
             jax.ShapeDtypeStruct((2 * per, 128), F32),
         )
-        + (jax.ShapeDtypeStruct((block + 2 * per, 2 * HEAD_WIDTH), BF16),) * (groups - 1),
+        + tuple(
+            jax.ShapeDtypeStruct((block // 2 + more, 2 * HEAD_WIDTH), BF16)
+            for more in (2 * per, 0, 2 * per, 2 * per)
+        ),
         in_specs=[SMEM, VMEM, VMEM],
-        out_specs=(VMEM,) * (2 + groups),
+        out_specs=(VMEM,) * 7,
         name="slot_sums",
         compiler_params=PARAMS,
     )(where, own_part, other_sums)
 
-    pieces = []
-    for k, piece in enumerate(leaving, 1):
-        pieces.append(shifted(piece, "head", k))
+    relayed, back, ahead, behind = leaving
+    upper_1 = shifted(relayed, "head", 1)
+    lower_3 = shifted(back, "head", -1)
+    lower_1 = shifted(ahead, "head", 1)
+    upper_3 = shifted(behind, "head", -1)
+    upper_2 = shifted(upper_1, "head", 1)
+    lower_2 = shifted(lower_3, "head", -1)
     cached_input_gradient, grad_span_input = pl.pallas_call(
-        functools.partial(input_kernel, groups),
+        functools.partial(input_kernel, groups, sharers),
         out_shape=(
             jax.ShapeDtypeStruct((block, features), BF16),
             jax.ShapeDtypeStruct((2 * per, width), BF16),
         ),
-        in_specs=[SMEM] + [VMEM] * (1 + 3 * groups),
+        in_specs=[SMEM] + [VMEM] * (11 + 2 * sharers),
         out_specs=(VMEM, VMEM),
         scratch_shapes=[pltpu.VMEM((2 * per, 128), F32)],
         name="input_gradient",
         compiler_params=PARAMS,
     )(
         where,
-        leaving[0],
+        relayed,
+        back,
         own_span,
-        *pieces,
+        upper_1,
+        lower_1,
+        upper_2,
+        lower_2,
+        upper_3,
+        lower_3,
         *own_weights,
-        *arriving,
-        *other_half,
+        *near,
+        *there,
     )
     return (saved_key_gradient, saved_value_gradient, cached_input_gradient, grad_span_input)
 

time: 164 us -> 160 us (0.976)
  the two profiles are of different devices: /device:TPU:8 before, /device:TPU:1 now
where the time goes in v4:
time: 160 us; the launch traced here: 158 us
  starting transfers between devices  98.7 us (62%)
  waiting for transfers between devices  39.9 us (25%)
  Pallas kernels  15.2 us (10%)
  between operations  2.39 us (1%)
  local copies, waits for them, and re-layouts  1.73 us (1%)
    ppermute x20, starting transfers between devices, shifted(): lax.ppermute(value, axis, [(k, (k + by) % count) for k in range(count)])  76.5 us
    all_to_all x3, waiting for transfers between devices, exchanged(): return lax.all_to_all(value, axes, split_axis=0, concat_axis=0, tiled=True)  33.1 us
    all_to_all x3, starting transfers between devices, exchanged(): return lax.all_to_all(value, axes, split_axis=0, concat_axis=0, tiled=True)  22.2 us
    ppermute x20, waiting for transfers between devices, shifted(): lax.ppermute(value, axis, [(k, (k + by) % count) for k in range(count)])  6.81 us
    pallas_call x1, Pallas kernels, local(): pl.pallas_call(functools.partial(first_kernel, heads, group), out_shape=(...  4.51 us
  transfers between devices with their start and end apart: 23, of which 7 were waited for; matrix products, arithmetic and copies ran while one was open for 1% of the time, Pallas kernels for 3%

profile of v4, /device:TPU:1, one launch (start us, length us, event | category | flops | bytes accessed | tf_op | source)
XLA Modules:
  0.0 158.1 jit_solution(150097237741139915)
XLA Ops:
  0.6 8.7 %collective-permute-start = (s32[1]{0:T(128)}, s32[1]{0:T(128)}, u32[]{:S(2)}, u32[]{:S(2)}) collective-permute-start(s32[1]{0:T(128)} %param.13), channel_id=1, source_target_pairs={{0,4},{4,0},{1,5},{5,1},{2,6},{6,2},{3,7},{7,3},{8,12},{12,8},{9,1... | collective-permute-start | bytes 20 | tf_op jit(solution)/shard_map/ppermute | solution.py:275
  10.0 0.3 collective-permute-done.other_ref
  10.3 2.3 %row_pack.1 = bf16[64,40,128]{2,1,0:T(8,128)(2,1)} custom-call(s32[1]{0:T(128)S(6)} %copy.15.own_ref, s32[1]{0:T(128)} %collective-permute-done.other_ref, bf16[1,2048]{1,0:T(2,128)(2,1)} %q_ref.1, bf16[1,2048]{1,0:T(2,128)(2,1)} %g_ref.1), custom_call_target="tpu_custom_call" | custom-call | tf_op jit(solution)/shard_map/row_pack/pallas_call | solution.py:300
  12.6 0.0 copy-start.1
  12.6 0.0 copy-start.2
  12.6 6.9 %all-to-all-start = ((bf16[64,40,128]{2,1,0:T(8,128)(2,1)}), bf16[64,40,128]{2,1,0:T(8,128)(2,1)S(1)}, u32[]{:S(2)}, u32[]{:S(2)}) async-start(bf16[64,40,128]{2,1,0:T(8,128)(2,1)} %row_pack.1), calls=%async_computation | async-start | bytes 1310720 | tf_op jit(solution)/shard_map/all_to_all | solution.py:270
  19.5 0.0 copy-done.1
  19.5 0.0 copy-done.2
  19.5 2.5 %collective-permute-start.1 = (bf16[384,256]{1,0:T(8,128)(2,1)S(1)}, bf16[384,256]{1,0:T(8,128)(2,1)S(1)}, u32[]{:S(2)}, u32[]{:S(2)}) collective-permute-start(bf16[384,256]{1,0:T(8,128)(2,1)S(1)} %pad_maximum_fusion.1), channel_id=1, source_target_pairs={{0,4},{4,0},{1,5},{5,1},{2,6},{6,2},{3,7},{7,3},{8,12},{12,8},{9,1... | collective-permute-start | bytes 589832 | tf_op jit(solution)/shard_map/ppermute | solution.py:275
  22.7 0.4 collective-permute-done.1
  23.2 14.9 %all-to-all-done.x_ref = bf16[64,40,128]{2,1,0:T(8,128)(2,1)S(1)} async-done(((bf16[64,40,128]{2,1,0:T(8,128)(2,1)}), bf16[64,40,128]{2,1,0:T(8,128)(2,1)S(1)}, u32[]{:S(2)}, u32[]{:S(2)}) %all-to-all-start) | async-done | bytes 655392 | tf_op jit(solution)/shard_map/all_to_all | solution.py:270
  38.1 4.5 %row_partials.1 = (bf16[64,40,128]{2,1,0:T(8,128)(2,1)}, f32[4]{0:T(128)S(1)}) custom-call(s32[8]{0:T(128)S(1)} %compare_select_fusion.4.where_ref, bf16[64,40,128]{2,1,0:T(8,128)(2,1)S(1)} %all-to-all-done.x_ref, bf16[768,128]{1,0:T(8,128)(2,1)S(1)} %get-tuple-element.35.k_ref, bf16[768,128]{1,0:T(8,128)(2,1)S(1)} %get-tuple-element.36.v_ref), custom_call_target="tpu_custom_call" | custom-call | tf_op jit(solution)/shard_map/row_partials/pallas_call | solution.py:340
  42.6 7.6 %all-to-all-start.1 = ((bf16[64,40,128]{2,1,0:T(8,128)(2,1)}), bf16[64,40,128]{2,1,0:T(8,128)(2,1)S(1)}, u32[]{:S(2)}, u32[]{:S(2)}) async-start(bf16[64,40,128]{2,1,0:T(8,128)(2,1)} %get-tuple-element.18), calls=%async_computation.1 | async-start | bytes 1310720 | tf_op jit(solution)/shard_map/all_to_all | solution.py:270
  50.2 0.0 copy-start
  50.2 18.2 %all-to-all-done.1.z_ref = bf16[64,40,128]{2,1,0:T(8,128)(2,1)S(1)} async-done(((bf16[64,40,128]{2,1,0:T(8,128)(2,1)}), bf16[64,40,128]{2,1,0:T(8,128)(2,1)S(1)}, u32[]{:S(2)}, u32[]{:S(2)}) %all-to-all-start.1) | async-done | bytes 655392 | tf_op jit(solution)/shard_map/all_to_all | solution.py:270
  68.4 1.5 row_merge.1
  69.9 7.7 %all-to-all-start.2 = ((bf16[64,24,128]{2,1,0:T(8,128)(2,1)}), bf16[64,24,128]{2,1,0:T(8,128)(2,1)S(1)}, u32[]{:S(2)}, u32[]{:S(2)}) async-start(bf16[64,24,128]{2,1,0:T(8,128)(2,1)} %row_merge.1), calls=%async_computation.2 | async-start | bytes 786432 | tf_op jit(solution)/shard_map/all_to_all | solution.py:270
  77.6 0.0 copy-done
  77.6 0.2 broadcast_select_fusion
  77.8 0.0 copy-start.3
  77.8 0.7 constant_dynamic-slice_fusion
  78.5 5.8 %collective-permute-start.10 = (bf16[256,128]{1,0:T(8,128)(2,1)S(1)}, bf16[256,128]{1,0:T(8,128)(2,1)S(1)}, u32[]{:S(2)}, u32[]{:S(2)}) collective-permute-start(bf16[256,128]{1,0:T(8,128)(2,1)S(1)} %get-tuple-element.32), channel_id=1, source_target_pairs={{0,1},{1,2},{2,3},{3,0},{4,5},{5,6},{6,7},{7,4},{8,9},{9,10},{10,1... | collective-permute-start | bytes 196616 | tf_op jit(solution)/shard_map/ppermute | solution.py:275
  84.3 0.0 copy-done.3
  84.3 4.9 %collective-permute-start.2 = (bf16[32,2048]{1,0:T(8,128)(2,1)S(1)}, bf16[32,2048]{1,0:T(8,128)(2,1)S(1)}, u32[]{:S(2)}, u32[]{:S(2)}) collective-permute-start(bf16[32,2048]{1,0:T(8,128)(2,1)S(1)} %copy-done.3), channel_id=1, source_target_pairs={{0,4},{4,0},{1,5},{5,1},{2,6},{6,2},{3,7},{7,3},{8,12},{12,8},{9,1... | collective-permute-start | bytes 393224 | tf_op jit(solution)/shard_map/ppermute | solution.py:275
  89.3 5.6 %collective-permute-start.12 = (bf16[256,128]{1,0:T(8,128)(2,1)}, bf16[256,128]{1,0:T(8,128)(2,1)S(1)}, u32[]{:S(2)}, u32[]{:S(2)}) collective-permute-start(bf16[256,128]{1,0:T(8,128)(2,1)} %get-tuple-element.30), channel_id=1, source_target_pairs={{0,3},{1,0},{2,1},{3,2},{4,7},{5,4},{6,5},{7,6},{8,11},{9,8},{10,9... | collective-permute-start | bytes 196616 | tf_op jit(solution)/shard_map/ppermute | solution.py:275
  94.9 5.7 %collective-permute-start.11 = (bf16[256,128]{1,0:T(8,128)(2,1)}, bf16[256,128]{1,0:T(8,128)(2,1)S(1)}, u32[]{:S(2)}, u32[]{:S(2)}) collective-permute-start(bf16[256,128]{1,0:T(8,128)(2,1)} %get-tuple-element.31), channel_id=1, source_target_pairs={{0,2},{1,3},{2,0},{3,1},{4,6},{5,7},{6,4},{7,5},{8,10},{9,11},{10,... | collective-permute-start | bytes 196616 | tf_op jit(solution)/shard_map/ppermute | solution.py:275
  100.6 0.0 collective-permute-done.10
  100.6 0.0 collective-permute-done.2
  100.7 0.0 all-to-all-done.2.u_ref
  100.7 3.1 %slot_gradients.1 = (f32[448,256]{1,0:T(8,128)S(1)}, f32[448,256]{1,0:T(8,128)S(1)}) custom-call(s32[8]{0:T(128)S(1)} %compare_select_fusion.4.where_ref, f32[4]{0:T(128)S(1)} %get-tuple-element.17.place_ref, bf16[64,40,128]{2,1,0:T(8,128)(2,1)S(1)} %all-to-all-done.x_ref, bf16[64,24,128]{2,1,0:T(8,128)(2,1)S(1)} %all-to-all-done.2.u_ref, ...), custom_call_target="tpu_custom_call" | custom-call | tf_op jit(solution)/shard_map/slot_gradients/pallas_call | solution.py:362
  103.8 2.5 %collective-permute-start.3 = (f32[448,256]{1,0:T(8,128)S(1)}, f32[448,256]{1,0:T(8,128)S(1)}, u32[]{:S(2)}, u32[]{:S(2)}) collective-permute-start(f32[448,256]{1,0:T(8,128)S(1)} %get-tuple-element.20), channel_id=1, source_target_pairs={{0,4},{4,0},{1,5},{5,1},{2,6},{6,2},{3,7},{7,3},{8,12},{12,8},{9,1... | collective-permute-start | bytes 1376264 | tf_op jit(solution)/shard_map/ppermute | solution.py:275
  106.3 0.0 collective-permute-done.11
  106.4 0.0 collective-permute-done.12
  106.4 4.6 %collective-permute-start.15 = (bf16[768,128]{1,0:T(8,128)(2,1)S(1)}, bf16[768,128]{1,0:T(8,128)(2,1)S(1)}, u32[]{:S(2)}, u32[]{:S(2)}) collective-permute-start(bf16[768,128]{1,0:T(8,128)(2,1)S(1)} %constant_dynamic-update-slice_fusion.refs_11_), channel_id=1, source_target_pairs={{0,384},{128,0},{256,128},{384,256},{1,385},{129,1},{257,129},{385... | collective-permute-start | bytes 589832 | tf_op jit(solution)/shard_map/ppermute | solution.py:275
  111.0 2.3 %collective-permute-start.14 = (bf16[768,128]{1,0:T(8,128)(2,1)S(1)}, bf16[768,128]{1,0:T(8,128)(2,1)S(1)}, u32[]{:S(2)}, u32[]{:S(2)}) collective-permute-start(bf16[768,128]{1,0:T(8,128)(2,1)S(1)} %constant_dynamic-update-slice_fusion.refs_11_), channel_id=1, source_target_pairs={{0,256},{128,384},{256,0},{384,128},{1,257},{129,385},{257,1},{385... | collective-permute-start | bytes 589832 | tf_op jit(solution)/shard_map/ppermute | solution.py:275
  113.3 2.5 %collective-permute-start.16 = (bf16[768,128]{1,0:T(8,128)(2,1)S(1)}, bf16[768,128]{1,0:T(8,128)(2,1)S(1)}, u32[]{:S(2)}, u32[]{:S(2)}) collective-permute-start(bf16[768,128]{1,0:T(8,128)(2,1)S(1)} %constant_dynamic-update-slice_fusion.refs_11_), channel_id=1, source_target_pairs={{0,4},{4,0},{1,5},{5,1},{2,6},{6,2},{3,7},{7,3},{8,12},{12,8},{9,1... | collective-permute-start | bytes 589832 | tf_op jit(solution)/shard_map/ppermute | solution.py:275
  115.8 2.6 %collective-permute-start.13 = (bf16[768,128]{1,0:T(8,128)(2,1)S(1)}, bf16[768,128]{1,0:T(8,128)(2,1)S(1)}, u32[]{:S(2)}, u32[]{:S(2)}) collective-permute-start(bf16[768,128]{1,0:T(8,128)(2,1)S(1)} %constant_dynamic-update-slice_fusion.refs_11_), channel_id=1, source_target_pairs={{0,128},{128,256},{256,384},{384,0},{1,129},{129,257},{257,385},{3... | collective-permute-start | bytes 589832 | tf_op jit(solution)/shard_map/ppermute | solution.py:275
  118.4 0.9 collective-permute-done.15.refs_14_
  119.3 2.9 %collective-permute-start.19 = (bf16[768,128]{1,0:T(8,128)(2,1)S(1)}, bf16[768,128]{1,0:T(8,128)(2,1)S(1)}, u32[]{:S(2)}, u32[]{:S(2)}) collective-permute-start(bf16[768,128]{1,0:T(8,128)(2,1)S(1)} %collective-permute-done.15.refs_14_), channel_id=1, source_target_pairs={{0,4},{4,0},{1,5},{5,1},{2,6},{6,2},{3,7},{7,3},{8,12},{12,8},{9,1... | collective-permute-start | bytes 589832 | tf_op jit(solution)/shard_map/ppermute | solution.py:275
  122.2 0.0 collective-permute-done.14.refs_13_
  122.2 1.9 %collective-permute-start.18 = (bf16[768,128]{1,0:T(8,128)(2,1)S(1)}, bf16[768,128]{1,0:T(8,128)(2,1)S(1)}, u32[]{:S(2)}, u32[]{:S(2)}) collective-permute-start(bf16[768,128]{1,0:T(8,128)(2,1)S(1)} %collective-permute-done.14.refs_13_), channel_id=1, source_target_pairs={{0,4},{4,0},{1,5},{5,1},{2,6},{6,2},{3,7},{7,3},{8,12},{12,8},{9,1... | collective-permute-start | bytes 589832 | tf_op jit(solution)/shard_map/ppermute | solution.py:275
  124.2 0.0 collective-permute-done.3.other_ref
  124.2 1.3 slot_sums.1
  125.4 2.8 %collective-permute-start.4 = (bf16[224,256]{1,0:T(8,128)(2,1)S(1)}, bf16[224,256]{1,0:T(8,128)(2,1)S(1)}, u32[]{:S(2)}, u32[]{:S(2)}) collective-permute-start(bf16[224,256]{1,0:T(8,128)(2,1)S(1)} %get-tuple-element.23.refs_0_), channel_id=1, source_target_pairs={{0,1},{1,2},{2,3},{3,0},{4,5},{5,6},{6,7},{7,4},{8,9},{9,10},{10,1... | collective-permute-start | bytes 344072 | tf_op jit(solution)/shard_map/ppermute | solution.py:275
  128.2 0.0 collective-permute-done.16.refs_15_
  128.2 4.6 %collective-permute-start.7 = (bf16[192,256]{1,0:T(8,128)(2,1)S(1)}, bf16[192,256]{1,0:T(8,128)(2,1)S(1)}, u32[]{:S(2)}, u32[]{:S(2)}) collective-permute-start(bf16[192,256]{1,0:T(8,128)(2,1)S(1)} %get-tuple-element.24.refs_1_), channel_id=1, source_target_pairs={{0,3},{1,0},{2,1},{3,2},{4,7},{5,4},{6,5},{7,6},{8,11},{9,8},{10,9... | collective-permute-start | bytes 294920 | tf_op jit(solution)/shard_map/ppermute | solution.py:275
  132.8 0.0 collective-permute-done.13.refs_12_
  132.9 3.0 %collective-permute-start.17 = (bf16[768,128]{1,0:T(8,128)(2,1)S(1)}, bf16[768,128]{1,0:T(8,128)(2,1)S(1)}, u32[]{:S(2)}, u32[]{:S(2)}) collective-permute-start(bf16[768,128]{1,0:T(8,128)(2,1)S(1)} %collective-permute-done.13.refs_12_), channel_id=1, source_target_pairs={{0,4},{4,0},{1,5},{5,1},{2,6},{6,2},{3,7},{7,3},{8,12},{12,8},{9,1... | collective-permute-start | bytes 589832 | tf_op jit(solution)/shard_map/ppermute | solution.py:275
  135.8 0.0 collective-permute-done.19.refs_18_
  135.8 1.9 %collective-permute-start.5 = (bf16[224,256]{1,0:T(8,128)(2,1)S(1)}, bf16[224,256]{1,0:T(8,128)(2,1)S(1)}, u32[]{:S(2)}, u32[]{:S(2)}) collective-permute-start(bf16[224,256]{1,0:T(8,128)(2,1)S(1)} %get-tuple-element.26), channel_id=1, source_target_pairs={{0,1},{1,2},{2,3},{3,0},{4,5},{5,6},{6,7},{7,4},{8,9},{9,10},{10,1... | collective-permute-start | bytes 344072 | tf_op jit(solution)/shard_map/ppermute | solution.py:275
  137.8 0.0 collective-permute-done.18.refs_17_
  137.8 5.5 %collective-permute-start.9 = (bf16[224,256]{1,0:T(8,128)(2,1)S(1)}, bf16[224,256]{1,0:T(8,128)(2,1)S(1)}, u32[]{:S(2)}, u32[]{:S(2)}) collective-permute-start(bf16[224,256]{1,0:T(8,128)(2,1)S(1)} %get-tuple-element.27), channel_id=1, source_target_pairs={{0,3},{1,0},{2,1},{3,2},{4,7},{5,4},{6,5},{7,6},{8,11},{9,8},{10,9... | collective-permute-start | bytes 344072 | tf_op jit(solution)/shard_map/ppermute | solution.py:275
  143.3 0.0 collective-permute-done.7.refs_8_
  143.3 2.2 %collective-permute-start.8 = (bf16[192,256]{1,0:T(8,128)(2,1)S(1)}, bf16[192,256]{1,0:T(8,128)(2,1)S(1)}, u32[]{:S(2)}, u32[]{:S(2)}) collective-permute-start(bf16[192,256]{1,0:T(8,128)(2,1)S(1)} %collective-permute-done.7.refs_8_), channel_id=1, source_target_pairs={{0,3},{1,0},{2,1},{3,2},{4,7},{5,4},{6,5},{7,6},{8,11},{9,8},{10,9... | collective-permute-start | bytes 294920 | tf_op jit(solution)/shard_map/ppermute | solution.py:275
  145.5 0.0 collective-permute-done.4.refs_3_
  145.5 4.0 %collective-permute-start.6 = (bf16[224,256]{1,0:T(8,128)(2,1)S(1)}, bf16[224,256]{1,0:T(8,128)(2,1)S(1)}, u32[]{:S(2)}, u32[]{:S(2)}) collective-permute-start(bf16[224,256]{1,0:T(8,128)(2,1)S(1)} %collective-permute-done.4.refs_3_), channel_id=1, source_target_pairs={{0,1},{1,2},{2,3},{3,0},{4,5},{5,6},{6,7},{7,4},{8,9},{9,10},{10,1... | collective-permute-start | bytes 344072 | tf_op jit(solution)/shard_map/ppermute | solution.py:275
  149.5 1.0 constant_dynamic-slice_fusion.3
  150.5 0.0 collective-permute-done.17.refs_16_
  150.5 0.0 collective-permute-done.5.refs_4_
  150.5 0.0 collective-permute-done.9.refs_7_
  150.5 2.4 %collective-permute-done.8.refs_6_ = bf16[192,256]{1,0:T(8,128)(2,1)S(1)} collective-permute-done((bf16[192,256]{1,0:T(8,128)(2,1)S(1)}, bf16[192,256]{1,0:T(8,128)(2,1)S(1)}, u32[]{:S(2)}, u32[]{:S(2)}) %collective-permute-start.8) | collective-permute-done | bytes 98336 | tf_op jit(solution)/shard_map/ppermute | solution.py:275
  152.9 2.8 %collective-permute-done.6.refs_5_ = bf16[224,256]{1,0:T(8,128)(2,1)S(1)} collective-permute-done((bf16[224,256]{1,0:T(8,128)(2,1)S(1)}, bf16[224,256]{1,0:T(8,128)(2,1)S(1)}, u32[]{:S(2)}, u32[]{:S(2)}) %collective-permute-start.6) | collective-permute-done | bytes 114720 | tf_op jit(solution)/shard_map/ppermute | solution.py:275
  155.7 2.4 %input_gradient.1 = (bf16[384,1024]{1,0:T(8,128)(2,1)}, bf16[32,32]{1,0:T(8,128)(2,1)}) custom-call(s32[8]{0:T(128)S(1)} %compare_select_fusion.4.where_ref, bf16[224,256]{1,0:T(8,128)(2,1)S(1)} %get-tuple-element.23.refs_0_, bf16[192,256]{1,0:T(8,128)(2,1)S(1)} %get-tuple-element.24.refs_1_, f32[32,128]{1,0:T(8,128)S(1)} %get-tuple-element.25.refs_2_, ...), custom_call_target="tpu_custom_call" | custom-call | tf_op jit(solution)/shard_map/input_gradient/pallas_call | solution.py:396
  (8 shorter events, 0.1 us)
Async XLA Ops:
  0.6 9.7 %collective-permute-start = (s32[1]{0:T(128)}, s32[1]{0:T(128)}, u32[]{:S(2)}, u32[]{:S(2)}) collective-permute-start(s32[1]{0:T(128)} %param.13), channel_id=1, source_target_pairs={{0,4},{4,0},{1,5},{5,1},{2,6},{6,2},{3,7},{7,3},{8,12},{12,8},{9,1... | collective-permute-start | bytes 20 | tf_op jit(solution)/shard_map/ppermute | solution.py:275
  12.6 6.9 %copy-start.1 = (bf16[384,128]{1,0:T(8,128)(2,1)S(1)}, bf16[384,128]{1,0:T(8,128)(2,1)}, u32[]{:S(2)}) copy-start(bf16[384,128]{1,0:T(8,128)(2,1)} %param.12) | copy-start | bytes 294916
  12.6 6.9 %copy-start.2 = (bf16[384,128]{1,0:T(8,128)(2,1)S(1)}, bf16[384,128]{1,0:T(8,128)(2,1)}, u32[]{:S(2)}) copy-start(bf16[384,128]{1,0:T(8,128)(2,1)} %param.11) | copy-start | bytes 294916
  12.6 25.5 %all-to-all-start = ((bf16[64,40,128]{2,1,0:T(8,128)(2,1)}), bf16[64,40,128]{2,1,0:T(8,128)(2,1)S(1)}, u32[]{:S(2)}, u32[]{:S(2)}) async-start(bf16[64,40,128]{2,1,0:T(8,128)(2,1)} %row_pack.1), calls=%async_computation | async-start | bytes 1310720 | tf_op jit(solution)/shard_map/all_to_all | solution.py:270
  19.5 3.6 %collective-permute-start.1 = (bf16[384,256]{1,0:T(8,128)(2,1)S(1)}, bf16[384,256]{1,0:T(8,128)(2,1)S(1)}, u32[]{:S(2)}, u32[]{:S(2)}) collective-permute-start(bf16[384,256]{1,0:T(8,128)(2,1)S(1)} %pad_maximum_fusion.1), channel_id=1, source_target_pairs={{0,4},{4,0},{1,5},{5,1},{2,6},{6,2},{3,7},{7,3},{8,12},{12,8},{9,1... | collective-permute-start | bytes 589832 | tf_op jit(solution)/shard_map/ppermute | solution.py:275
  42.6 25.8 %all-to-all-start.1 = ((bf16[64,40,128]{2,1,0:T(8,128)(2,1)}), bf16[64,40,128]{2,1,0:T(8,128)(2,1)S(1)}, u32[]{:S(2)}, u32[]{:S(2)}) async-start(bf16[64,40,128]{2,1,0:T(8,128)(2,1)} %get-tuple-element.18), calls=%async_computation.1 | async-start | bytes 1310720 | tf_op jit(solution)/shard_map/all_to_all | solution.py:270
  50.2 27.4 %copy-start = (bf16[4096,128]{1,0:T(8,128)(2,1)S(1)}, bf16[4096,128]{1,0:T(8,128)(2,1)}, u32[]{:S(2)}) copy-start(bf16[4096,128]{1,0:T(8,128)(2,1)} %param.17) | copy-start | bytes 3145732
  69.9 30.8 %all-to-all-start.2 = ((bf16[64,24,128]{2,1,0:T(8,128)(2,1)}), bf16[64,24,128]{2,1,0:T(8,128)(2,1)S(1)}, u32[]{:S(2)}, u32[]{:S(2)}) async-start(bf16[64,24,128]{2,1,0:T(8,128)(2,1)} %row_merge.1), calls=%async_computation.2 | async-start | bytes 786432 | tf_op jit(solution)/shard_map/all_to_all | solution.py:270
  77.8 6.5 %copy-start.3 = (bf16[32,2048]{1,0:T(8,128)(2,1)S(1)}, bf16[32,2048]{1,0:T(8,128)(2,1)}, u32[]{:S(2)}) copy-start(bf16[32,2048]{1,0:T(8,128)(2,1)} %param.15) | copy-start | bytes 393220
  78.5 22.1 %collective-permute-start.10 = (bf16[256,128]{1,0:T(8,128)(2,1)S(1)}, bf16[256,128]{1,0:T(8,128)(2,1)S(1)}, u32[]{:S(2)}, u32[]{:S(2)}) collective-permute-start(bf16[256,128]{1,0:T(8,128)(2,1)S(1)} %get-tuple-element.32), channel_id=1, source_target_pairs={{0,1},{1,2},{2,3},{3,0},{4,5},{5,6},{6,7},{7,4},{8,9},{9,10},{10,1... | collective-permute-start | bytes 196616 | tf_op jit(solution)/shard_map/ppermute | solution.py:275
  84.3 16.3 %collective-permute-start.2 = (bf16[32,2048]{1,0:T(8,128)(2,1)S(1)}, bf16[32,2048]{1,0:T(8,128)(2,1)S(1)}, u32[]{:S(2)}, u32[]{:S(2)}) collective-permute-start(bf16[32,2048]{1,0:T(8,128)(2,1)S(1)} %copy-done.3), channel_id=1, source_target_pairs={{0,4},{4,0},{1,5},{5,1},{2,6},{6,2},{3,7},{7,3},{8,12},{12,8},{9,1... | collective-permute-start | bytes 393224 | tf_op jit(solution)/shard_map/ppermute | solution.py:275
  89.3 17.1 %collective-permute-start.12 = (bf16[256,128]{1,0:T(8,128)(2,1)}, bf16[256,128]{1,0:T(8,128)(2,1)S(1)}, u32[]{:S(2)}, u32[]{:S(2)}) collective-permute-start(bf16[256,128]{1,0:T(8,128)(2,1)} %get-tuple-element.30), channel_id=1, source_target_pairs={{0,3},{1,0},{2,1},{3,2},{4,7},{5,4},{6,5},{7,6},{8,11},{9,8},{10,9... | collective-permute-start | bytes 196616 | tf_op jit(solution)/shard_map/ppermute | solution.py:275
  94.9 11.4 %collective-permute-start.11 = (bf16[256,128]{1,0:T(8,128)(2,1)}, bf16[256,128]{1,0:T(8,128)(2,1)S(1)}, u32[]{:S(2)}, u32[]{:S(2)}) collective-permute-start(bf16[256,128]{1,0:T(8,128)(2,1)} %get-tuple-element.31), channel_id=1, source_target_pairs={{0,2},{1,3},{2,0},{3,1},{4,6},{5,7},{6,4},{7,5},{8,10},{9,11},{10,... | collective-permute-start | bytes 196616 | tf_op jit(solution)/shard_map/ppermute | solution.py:275
  103.8 20.3 %collective-permute-start.3 = (f32[448,256]{1,0:T(8,128)S(1)}, f32[448,256]{1,0:T(8,128)S(1)}, u32[]{:S(2)}, u32[]{:S(2)}) collective-permute-start(f32[448,256]{1,0:T(8,128)S(1)} %get-tuple-element.20), channel_id=1, source_target_pairs={{0,4},{4,0},{1,5},{5,1},{2,6},{6,2},{3,7},{7,3},{8,12},{12,8},{9,1... | collective-permute-start | bytes 1376264 | tf_op jit(solution)/shard_map/ppermute | solution.py:275
  106.4 12.9 %collective-permute-start.15 = (bf16[768,128]{1,0:T(8,128)(2,1)S(1)}, bf16[768,128]{1,0:T(8,128)(2,1)S(1)}, u32[]{:S(2)}, u32[]{:S(2)}) collective-permute-start(bf16[768,128]{1,0:T(8,128)(2,1)S(1)} %constant_dynamic-update-slice_fusion.refs_11_), channel_id=1, source_target_pairs={{0,384},{128,0},{256,128},{384,256},{1,385},{129,1},{257,129},{385... | collective-permute-start | bytes 589832 | tf_op jit(solution)/shard_map/ppermute | solution.py:275
  111.0 11.2 %collective-permute-start.14 = (bf16[768,128]{1,0:T(8,128)(2,1)S(1)}, bf16[768,128]{1,0:T(8,128)(2,1)S(1)}, u32[]{:S(2)}, u32[]{:S(2)}) collective-permute-start(bf16[768,128]{1,0:T(8,128)(2,1)S(1)} %constant_dynamic-update-slice_fusion.refs_11_), channel_id=1, source_target_pairs={{0,256},{128,384},{256,0},{384,128},{1,257},{129,385},{257,1},{385... | collective-permute-start | bytes 589832 | tf_op jit(solution)/shard_map/ppermute | solution.py:275
  113.3 14.9 %collective-permute-start.16 = (bf16[768,128]{1,0:T(8,128)(2,1)S(1)}, bf16[768,128]{1,0:T(8,128)(2,1)S(1)}, u32[]{:S(2)}, u32[]{:S(2)}) collective-permute-start(bf16[768,128]{1,0:T(8,128)(2,1)S(1)} %constant_dynamic-update-slice_fusion.refs_11_), channel_id=1, source_target_pairs={{0,4},{4,0},{1,5},{5,1},{2,6},{6,2},{3,7},{7,3},{8,12},{12,8},{9,1... | collective-permute-start | bytes 589832 | tf_op jit(solution)/shard_map/ppermute | solution.py:275
  115.8 17.1 %collective-permute-start.13 = (bf16[768,128]{1,0:T(8,128)(2,1)S(1)}, bf16[768,128]{1,0:T(8,128)(2,1)S(1)}, u32[]{:S(2)}, u32[]{:S(2)}) collective-permute-start(bf16[768,128]{1,0:T(8,128)(2,1)S(1)} %constant_dynamic-update-slice_fusion.refs_11_), channel_id=1, source_target_pairs={{0,128},{128,256},{256,384},{384,0},{1,129},{129,257},{257,385},{3... | collective-permute-start | bytes 589832 | tf_op jit(solution)/shard_map/ppermute | solution.py:275
  119.3 16.5 %collective-permute-start.19 = (bf16[768,128]{1,0:T(8,128)(2,1)S(1)}, bf16[768,128]{1,0:T(8,128)(2,1)S(1)}, u32[]{:S(2)}, u32[]{:S(2)}) collective-permute-start(bf16[768,128]{1,0:T(8,128)(2,1)S(1)} %collective-permute-done.15.refs_14_), channel_id=1, source_target_pairs={{0,4},{4,0},{1,5},{5,1},{2,6},{6,2},{3,7},{7,3},{8,12},{12,8},{9,1... | collective-permute-start | bytes 589832 | tf_op jit(solution)/shard_map/ppermute | solution.py:275
  122.2 15.5 %collective-permute-start.18 = (bf16[768,128]{1,0:T(8,128)(2,1)S(1)}, bf16[768,128]{1,0:T(8,128)(2,1)S(1)}, u32[]{:S(2)}, u32[]{:S(2)}) collective-permute-start(bf16[768,128]{1,0:T(8,128)(2,1)S(1)} %collective-permute-done.14.refs_13_), channel_id=1, source_target_pairs={{0,4},{4,0},{1,5},{5,1},{2,6},{6,2},{3,7},{7,3},{8,12},{12,8},{9,1... | collective-permute-start | bytes 589832 | tf_op jit(solution)/shard_map/ppermute | solution.py:275
  125.4 20.0 %collective-permute-start.4 = (bf16[224,256]{1,0:T(8,128)(2,1)S(1)}, bf16[224,256]{1,0:T(8,128)(2,1)S(1)}, u32[]{:S(2)}, u32[]{:S(2)}) collective-permute-start(bf16[224,256]{1,0:T(8,128)(2,1)S(1)} %get-tuple-element.23.refs_0_), channel_id=1, source_target_pairs={{0,1},{1,2},{2,3},{3,0},{4,5},{5,6},{6,7},{7,4},{8,9},{9,10},{10,1... | collective-permute-start | bytes 344072 | tf_op jit(solution)/shard_map/ppermute | solution.py:275
  128.2 15.0 %collective-permute-start.7 = (bf16[192,256]{1,0:T(8,128)(2,1)S(1)}, bf16[192,256]{1,0:T(8,128)(2,1)S(1)}, u32[]{:S(2)}, u32[]{:S(2)}) collective-permute-start(bf16[192,256]{1,0:T(8,128)(2,1)S(1)} %get-tuple-element.24.refs_1_), channel_id=1, source_target_pairs={{0,3},{1,0},{2,1},{3,2},{4,7},{5,4},{6,5},{7,6},{8,11},{9,8},{10,9... | collective-permute-start | bytes 294920 | tf_op jit(solution)/shard_map/ppermute | solution.py:275
  132.9 17.6 %collective-permute-start.17 = (bf16[768,128]{1,0:T(8,128)(2,1)S(1)}, bf16[768,128]{1,0:T(8,128)(2,1)S(1)}, u32[]{:S(2)}, u32[]{:S(2)}) collective-permute-start(bf16[768,128]{1,0:T(8,128)(2,1)S(1)} %collective-permute-done.13.refs_12_), channel_id=1, source_target_pairs={{0,4},{4,0},{1,5},{5,1},{2,6},{6,2},{3,7},{7,3},{8,12},{12,8},{9,1... | collective-permute-start | bytes 589832 | tf_op jit(solution)/shard_map/ppermute | solution.py:275
  135.8 14.6 %collective-permute-start.5 = (bf16[224,256]{1,0:T(8,128)(2,1)S(1)}, bf16[224,256]{1,0:T(8,128)(2,1)S(1)}, u32[]{:S(2)}, u32[]{:S(2)}) collective-permute-start(bf16[224,256]{1,0:T(8,128)(2,1)S(1)} %get-tuple-element.26), channel_id=1, source_target_pairs={{0,1},{1,2},{2,3},{3,0},{4,5},{5,6},{6,7},{7,4},{8,9},{9,10},{10,1... | collective-permute-start | bytes 344072 | tf_op jit(solution)/shard_map/ppermute | solution.py:275
  137.8 12.7 %collective-permute-start.9 = (bf16[224,256]{1,0:T(8,128)(2,1)S(1)}, bf16[224,256]{1,0:T(8,128)(2,1)S(1)}, u32[]{:S(2)}, u32[]{:S(2)}) collective-permute-start(bf16[224,256]{1,0:T(8,128)(2,1)S(1)} %get-tuple-element.27), channel_id=1, source_target_pairs={{0,3},{1,0},{2,1},{3,2},{4,7},{5,4},{6,5},{7,6},{8,11},{9,8},{10,9... | collective-permute-start | bytes 344072 | tf_op jit(solution)/shard_map/ppermute | solution.py:275
  143.3 9.6 %collective-permute-start.8 = (bf16[192,256]{1,0:T(8,128)(2,1)S(1)}, bf16[192,256]{1,0:T(8,128)(2,1)S(1)}, u32[]{:S(2)}, u32[]{:S(2)}) collective-permute-start(bf16[192,256]{1,0:T(8,128)(2,1)S(1)} %collective-permute-done.7.refs_8_), channel_id=1, source_target_pairs={{0,3},{1,0},{2,1},{3,2},{4,7},{5,4},{6,5},{7,6},{8,11},{9,8},{10,9... | collective-permute-start | bytes 294920 | tf_op jit(solution)/shard_map/ppermute | solution.py:275
  145.5 10.2 %collective-permute-start.6 = (bf16[224,256]{1,0:T(8,128)(2,1)S(1)}, bf16[224,256]{1,0:T(8,128)(2,1)S(1)}, u32[]{:S(2)}, u32[]{:S(2)}) collective-permute-start(bf16[224,256]{1,0:T(8,128)(2,1)S(1)} %collective-permute-done.4.refs_3_), channel_id=1, source_target_pairs={{0,1},{1,2},{2,3},{3,0},{4,5},{5,6},{6,7},{7,4},{8,9},{9,10},{10,1... | collective-permute-start | bytes 344072 | tf_op jit(solution)/shard_map/ppermute | solution.py:275

commit v5 on v3

--- a/solution.py
+++ b/solution.py
@@ -223,29 +223,40 @@
         ref[half:, :] = jnp.concatenate([wide, jnp.zeros_like(wide)], axis=1).astype(BF16)
 
 
-def input_kernel(groups, where_ref, own_ref, span_ref, *refs):
-    arrived, refs = refs[: groups - 1], refs[groups - 1 :]
-    own_k_ref, own_v_ref = refs[:2]
-    here, there = refs[2 : 1 + groups], refs[1 + groups : 2 * groups]
-    out_ref, block_ref, turn_ref = refs[2 * groups :]
+def input_kernel(others, sharers, first, more, where_ref, *refs):
+    is_first = where_ref[1] == 0
+    if first:
+        own_ref, own_k_ref, own_v_ref = refs[:3]
+    else:
+        total_ref, span_ref, *spans = refs[: 2 + more]
+    refs = refs[3:] if first else refs[2 + more :]
+    arrived, refs = refs[: len(others)], refs[len(others) :]
+    here, there, refs = refs[:sharers], refs[sharers : 2 * sharers], refs[2 * sharers :]
+    out_ref = refs[0]
     half = out_ref.shape[0]
-    rows, features = block_ref.shape
-    is_first = where_ref[1] == 0
-    left = [own_ref[:half, :]]
-    span = span_ref[...]
+    left = [own_ref[:half, :]] if first else []
     for ref in arrived:
         keys, values = ref[:half, :HEAD_WIDTH], ref[:half, HEAD_WIDTH:]
         left += [jnp.where(is_first, keys, values), jnp.where(is_first, values, keys)]
+    left = jnp.concatenate(left, axis=1)
+    share = out_ref.shape[1] // sharers
+    for k, (near_ref, far_ref) in enumerate(zip(here, there)):
+        start = lax.rem(where_ref[5] - k + sharers, sharers) * share
+        part = pl.ds(pl.multiple_of(start, share), share)
+        right = [own_k_ref[part, :], own_v_ref[part, :]] if first else []
+        for other in others:
+            lines = slice((other - 1) * share, other * share)
+            right += [near_ref[lines, :], far_ref[lines, :]]
+        term = rows_dot(left, jnp.concatenate(right, axis=1))
+        out_ref[:, part] = term if first else (total_ref[:, part] + term).astype(BF16)
+    if first:
+        return
+    block_ref, turn_ref = refs[1:3]
+    rows, features = block_ref.shape
+    span = span_ref[...]
+    for ref in (*spans, *arrived):
         wide = ref[half:, :128].astype(F32)
         span += wide + pltpu.roll(wide, 128 - features, 1) + pltpu.roll(wide, 128 - 2 * features, 1)
-    left = jnp.concatenate(left, axis=1)
-    step = min(256, out_ref.shape[1])
-    for first in range(0, out_ref.shape[1], step):
-        part = pl.ds(first, step)
-        right = [own_k_ref[part, :], own_v_ref[part, :]]
-        for near_ref, far_ref in zip(here, there):
-            right += [near_ref[part, :], far_ref[part, :]]
-        out_ref[:, part] = rows_dot(left, jnp.concatenate(right, axis=1)).astype(BF16)
     turn_ref[pl.ds(0, rows // 2, stride=2), :] = span[: rows // 2]
     turn_ref[pl.ds(1, rows // 2, stride=2), :] = span[rows // 2 :]
     block_ref[...] = turn_ref[:, :features].astype(BF16)
@@ -297,17 +308,21 @@
     values = jnp.concatenate([saved_value_rows, other_cache[:, HEAD_WIDTH:]], axis=0)
 
     features = key_projection_weight.shape[0] // groups
+    sharers = lax.axis_size("seq_0")
+    share = features // sharers
     first_is_key = core == 0
     half_weights = jnp.where(first_is_key, key_projection_weight, value_projection_weight)
-    half_weights = half_weights.reshape(groups, features, HEAD_WIDTH)
     arriving = []
     for k in range(1, groups):
-        target = lax.rem(mine + k, groups)
-        piece = lax.dynamic_index_in_dim(half_weights, target, 0, keepdims=False)
+        start = lax.rem(mine + k, groups) * features + lax.axis_index("seq_0") * share
+        piece = lax.dynamic_slice_in_dim(half_weights, start, share, 0)
         arriving.append(shifted(piece, "head", k))
-    other_half = []
-    for k, piece in enumerate(arriving, 1):
-        other_half.append(shifted(piece, CORE, 1))
+    near = [jnp.concatenate(arriving, axis=0)]
+    for k in range(1, sharers):
+        near.append(shifted(near[0], "seq_0", k))
+    there = []
+    for piece in near:
+        there.append(shifted(piece, CORE, 1))
     own_weights = [
         lax.dynamic_slice_in_dim(w, mine * features, features, 0)
         for w in (key_projection_weight, value_projection_weight)
@@ -316,7 +331,7 @@
     both_query = jnp.concatenate([w_query, other_query], axis=0)
 
     where = jnp.full((8,), 2 * rows, jnp.int32)
-    for k, number in ((0, far), (1, core), (2, span_index[0]), (4, mine)):
+    for k, number in ((0, far), (1, core), (2, span_index[0]), (4, mine), (5, lax.axis_index("seq_0"))):
         where = jnp.where(jnp.arange(8) == k, number, where)
     y, place = pl.pallas_call(
         functools.partial(first_kernel, heads, group),
@@ -364,29 +379,30 @@
         compiler_params=PARAMS,
     )(where, own_part, other_sums)
 
-    pieces = []
+    pieces = {}
     for k, piece in enumerate(leaving, 1):
-        pieces.append(shifted(piece, "head", k))
+        pieces[k] = shifted(piece, "head", k)
+    early = [k for k in pieces if k != 2]
+    total = pl.pallas_call(
+        functools.partial(input_kernel, early, sharers, True, 0),
+        out_shape=jax.ShapeDtypeStruct((block, features), F32),
+        in_specs=[SMEM] + [VMEM] * (3 + len(early) + 2 * sharers),
+        out_specs=VMEM,
+        name="input_first",
+        compiler_params=PARAMS,
+    )(where, leaving[0], *own_weights, *[pieces[k] for k in early], *near, *there)
     cached_input_gradient, grad_span_input = pl.pallas_call(
-        functools.partial(input_kernel, groups),
+        functools.partial(input_kernel, [2], sharers, False, len(early)),
         out_shape=(
             jax.ShapeDtypeStruct((block, features), BF16),
             jax.ShapeDtypeStruct((2 * per, width), BF16),
         ),
-        in_specs=[SMEM] + [VMEM] * (1 + 3 * groups),
+        in_specs=[SMEM] + [VMEM] * (3 + len(early) + 2 * sharers),
         out_specs=(VMEM, VMEM),
         scratch_shapes=[pltpu.VMEM((2 * per, 128), F32)],
         name="input_gradient",
         compiler_params=PARAMS,
-    )(
-        where,
-        leaving[0],
-        own_span,
-        *pieces,
-        *own_weights,
-        *arriving,
-        *other_half,
-    )
+    )(where, total, own_span, *[pieces[k] for k in early], pieces[2], *near, *there)
     return (saved_key_gradient, saved_value_gradient, cached_input_gradient, grad_span_input)
 
 

time: 164 us -> 156 us (0.951)
  the two profiles are of different devices: /device:TPU:8 before, /device:TPU:1 now
where the time goes in v5:
time: 156 us; the launch traced here: 154 us
  starting transfers between devices  91 us (58%)
  waiting for transfers between devices  42 us (27%)
  Pallas kernels  15.9 us (10%)
  between operations  2.34 us (2%)
    ppermute x17, starting transfers between devices, shifted(): lax.ppermute(value, axis, [(k, (k + by) % count) for k in range(count)])  68.8 us
    all_to_all x3, waiting for transfers between devices, exchanged(): return lax.all_to_all(value, axes, split_axis=0, concat_axis=0, tiled=True)  33.1 us
    all_to_all x3, starting transfers between devices, exchanged(): return lax.all_to_all(value, axes, split_axis=0, concat_axis=0, tiled=True)  22.2 us
    ppermute x17, waiting for transfers between devices, shifted(): lax.ppermute(value, axis, [(k, (k + by) % count) for k in range(count)])  8.85 us
    pallas_call x1, Pallas kernels, local(): pl.pallas_call(functools.partial(first_kernel, heads, group), out_shape=(...  4.51 us
    pallas_call x1, Pallas kernels, local(): pl.pallas_call(functools.partial(second_kernel, heads, group), out_shape=...  3.14 us
  transfers between devices with their start and end apart: 20, of which 7 were waited for; matrix products, arithmetic and copies ran while one was open for 2% of the time, Pallas kernels for 4%

profile of v5, /device:TPU:1, one launch (start us, length us, event | category | flops | bytes accessed | tf_op | source)
XLA Modules:
  0.0 153.5 jit_solution(5153281804298951082)
XLA Ops:
  0.6 0.0 copy-start.1
  0.6 0.0 copy-start.2
  0.7 8.9 %collective-permute-start = (s32[1]{0:T(128)}, s32[1]{0:T(128)}, u32[]{:S(2)}, u32[]{:S(2)}) collective-permute-start(s32[1]{0:T(128)} %param.13), channel_id=1, source_target_pairs={{0,4},{4,0},{1,5},{5,1},{2,6},{6,2},{3,7},{7,3},{8,12},{12,8},{9,1... | collective-permute-start | bytes 20 | tf_op jit(solution)/shard_map/ppermute | solution.py:271
  10.2 0.3 collective-permute-done.other_ref
  10.5 2.2 %row_pack.1 = bf16[64,40,128]{2,1,0:T(8,128)(2,1)} custom-call(s32[1]{0:T(128)S(6)} %copy.15.own_ref, s32[1]{0:T(128)} %collective-permute-done.other_ref, bf16[1,2048]{1,0:T(2,128)(2,1)} %q_ref.1, bf16[1,2048]{1,0:T(2,128)(2,1)} %g_ref.1), custom_call_target="tpu_custom_call" | custom-call | tf_op jit(solution)/shard_map/row_pack/pallas_call | solution.py:296
  12.7 6.8 %all-to-all-start = ((bf16[64,40,128]{2,1,0:T(8,128)(2,1)}), bf16[64,40,128]{2,1,0:T(8,128)(2,1)S(1)}, u32[]{:S(2)}, u32[]{:S(2)}) async-start(bf16[64,40,128]{2,1,0:T(8,128)(2,1)} %row_pack.1), calls=%async_computation | async-start | bytes 1310720 | tf_op jit(solution)/shard_map/all_to_all | solution.py:266
  19.5 0.0 copy-done.1
  19.5 0.0 copy-done.2
  19.5 2.5 %collective-permute-start.1 = (bf16[384,256]{1,0:T(8,128)(2,1)S(1)}, bf16[384,256]{1,0:T(8,128)(2,1)S(1)}, u32[]{:S(2)}, u32[]{:S(2)}) collective-permute-start(bf16[384,256]{1,0:T(8,128)(2,1)S(1)} %pad_maximum_fusion.1), channel_id=1, source_target_pairs={{0,4},{4,0},{1,5},{5,1},{2,6},{6,2},{3,7},{7,3},{8,12},{12,8},{9,1... | collective-permute-start | bytes 589832 | tf_op jit(solution)/shard_map/ppermute | solution.py:271
  22.7 0.4 collective-permute-done.1
  23.1 14.9 %all-to-all-done.x_ref = bf16[64,40,128]{2,1,0:T(8,128)(2,1)S(1)} async-done(((bf16[64,40,128]{2,1,0:T(8,128)(2,1)}), bf16[64,40,128]{2,1,0:T(8,128)(2,1)S(1)}, u32[]{:S(2)}, u32[]{:S(2)}) %all-to-all-start) | async-done | bytes 655392 | tf_op jit(solution)/shard_map/all_to_all | solution.py:266
  38.1 4.5 %row_partials.1 = (bf16[64,40,128]{2,1,0:T(8,128)(2,1)}, f32[4]{0:T(128)S(1)}) custom-call(s32[8]{0:T(128)S(1)} %compare_select_fusion.4.where_ref, bf16[64,40,128]{2,1,0:T(8,128)(2,1)S(1)} %all-to-all-done.x_ref, bf16[768,128]{1,0:T(8,128)(2,1)S(1)} %get-tuple-element.33.k_ref, bf16[768,128]{1,0:T(8,128)(2,1)S(1)} %get-tuple-element.34.v_ref), custom_call_target="tpu_custom_call" | custom-call | tf_op jit(solution)/shard_map/row_partials/pallas_call | solution.py:336
  42.6 0.0 copy-start
  42.6 7.7 %all-to-all-start.1 = ((bf16[64,40,128]{2,1,0:T(8,128)(2,1)}), bf16[64,40,128]{2,1,0:T(8,128)(2,1)S(1)}, u32[]{:S(2)}, u32[]{:S(2)}) async-start(bf16[64,40,128]{2,1,0:T(8,128)(2,1)} %get-tuple-element.17), calls=%async_computation.1 | async-start | bytes 1310720 | tf_op jit(solution)/shard_map/all_to_all | solution.py:266
  50.3 18.2 %all-to-all-done.1.z_ref = bf16[64,40,128]{2,1,0:T(8,128)(2,1)S(1)} async-done(((bf16[64,40,128]{2,1,0:T(8,128)(2,1)}), bf16[64,40,128]{2,1,0:T(8,128)(2,1)S(1)}, u32[]{:S(2)}, u32[]{:S(2)}) %all-to-all-start.1) | async-done | bytes 655392 | tf_op jit(solution)/shard_map/all_to_all | solution.py:266
  68.5 1.5 %row_merge.1 = bf16[64,24,128]{2,1,0:T(8,128)(2,1)} custom-call(bf16[64,40,128]{2,1,0:T(8,128)(2,1)S(1)} %all-to-all-done.1.z_ref), custom_call_target="tpu_custom_call" | custom-call | tf_op jit(solution)/shard_map/row_merge/pallas_call | solution.py:348
  70.0 7.7 %all-to-all-start.2 = ((bf16[64,24,128]{2,1,0:T(8,128)(2,1)}), bf16[64,24,128]{2,1,0:T(8,128)(2,1)S(1)}, u32[]{:S(2)}, u32[]{:S(2)}) async-start(bf16[64,24,128]{2,1,0:T(8,128)(2,1)} %row_merge.1), calls=%async_computation.2 | async-start | bytes 786432 | tf_op jit(solution)/shard_map/all_to_all | solution.py:266
  77.7 0.0 copy-done
  77.7 0.2 broadcast_select_fusion
  78.0 5.8 %collective-permute-start.6 = (bf16[256,128]{1,0:T(8,128)(2,1)S(1)}, bf16[256,128]{1,0:T(8,128)(2,1)S(1)}, u32[]{:S(2)}, u32[]{:S(2)}) collective-permute-start(bf16[256,128]{1,0:T(8,128)(2,1)S(1)} %get-tuple-element.30), channel_id=1, source_target_pairs={{0,1},{1,2},{2,3},{3,0},{4,5},{5,6},{6,7},{7,4},{8,9},{9,10},{10,1... | collective-permute-start | bytes 196616 | tf_op jit(solution)/shard_map/ppermute | solution.py:271
  83.8 4.9 %collective-permute-start.2 = (bf16[32,2048]{1,0:T(8,128)(2,1)}, bf16[32,2048]{1,0:T(8,128)(2,1)S(1)}, u32[]{:S(2)}, u32[]{:S(2)}) collective-permute-start(bf16[32,2048]{1,0:T(8,128)(2,1)} %param.15), channel_id=1, source_target_pairs={{0,4},{4,0},{1,5},{5,1},{2,6},{6,2},{3,7},{7,3},{8,12},{12,8},{9,1... | collective-permute-start | bytes 393224 | tf_op jit(solution)/shard_map/ppermute | solution.py:271
  88.8 5.6 %collective-permute-start.8 = (bf16[256,128]{1,0:T(8,128)(2,1)S(1)}, bf16[256,128]{1,0:T(8,128)(2,1)S(1)}, u32[]{:S(2)}, u32[]{:S(2)}) collective-permute-start(bf16[256,128]{1,0:T(8,128)(2,1)S(1)} %get-tuple-element.28), channel_id=1, source_target_pairs={{0,3},{1,0},{2,1},{3,2},{4,7},{5,4},{6,5},{7,6},{8,11},{9,8},{10,9... | collective-permute-start | bytes 196616 | tf_op jit(solution)/shard_map/ppermute | solution.py:271
  94.4 5.7 %collective-permute-start.7 = (bf16[256,128]{1,0:T(8,128)(2,1)S(1)}, bf16[256,128]{1,0:T(8,128)(2,1)S(1)}, u32[]{:S(2)}, u32[]{:S(2)}) collective-permute-start(bf16[256,128]{1,0:T(8,128)(2,1)S(1)} %get-tuple-element.29), channel_id=1, source_target_pairs={{0,2},{1,3},{2,0},{3,1},{4,6},{5,7},{6,4},{7,5},{8,10},{9,11},{10,... | collective-permute-start | bytes 196616 | tf_op jit(solution)/shard_map/ppermute | solution.py:271
  100.1 0.0 collective-permute-done.6
  100.1 3.2 %collective-permute-done.7 = bf16[256,128]{1,0:T(8,128)(2,1)S(1)} collective-permute-done((bf16[256,128]{1,0:T(8,128)(2,1)S(1)}, bf16[256,128]{1,0:T(8,128)(2,1)S(1)}, u32[]{:S(2)}, u32[]{:S(2)}) %collective-permute-start.7) | collective-permute-done | bytes 65568 | tf_op jit(solution)/shard_map/ppermute | solution.py:271
  103.3 0.0 collective-permute-done.2
  103.3 0.9 pad_maximum_fusion.w_ref
  104.2 0.0 all-to-all-done.2.u_ref
  104.3 3.1 %slot_gradients.1 = (f32[448,256]{1,0:T(8,128)S(1)}, f32[448,256]{1,0:T(8,128)S(1)}) custom-call(s32[8]{0:T(128)S(1)} %compare_select_fusion.4.where_ref, f32[4]{0:T(128)S(1)} %get-tuple-element.16.place_ref, bf16[64,40,128]{2,1,0:T(8,128)(2,1)S(1)} %all-to-all-done.x_ref, bf16[64,24,128]{2,1,0:T(8,128)(2,1)S(1)} %all-to-all-done.2.u_ref, ...), custom_call_target="tpu_custom_call" | custom-call | tf_op jit(solution)/shard_map/slot_gradients/pallas_call | solution.py:358
  107.4 3.3 %collective-permute-start.3 = (f32[448,256]{1,0:T(8,128)S(1)}, f32[448,256]{1,0:T(8,128)S(1)}, u32[]{:S(2)}, u32[]{:S(2)}) collective-permute-start(f32[448,256]{1,0:T(8,128)S(1)} %get-tuple-element.19), channel_id=1, source_target_pairs={{0,4},{4,0},{1,5},{5,1},{2,6},{6,2},{3,7},{7,3},{8,12},{12,8},{9,1... | collective-permute-start | bytes 1376264 | tf_op jit(solution)/shard_map/ppermute | solution.py:271
  110.8 0.0 collective-permute-done.8
  110.8 4.6 %collective-permute-start.11 = (bf16[768,128]{1,0:T(8,128)(2,1)S(1)}, bf16[768,128]{1,0:T(8,128)(2,1)S(1)}, u32[]{:S(2)}, u32[]{:S(2)}) collective-permute-start(bf16[768,128]{1,0:T(8,128)(2,1)S(1)} %constant_dynamic-update-slice_fusion.refs_5_), channel_id=1, source_target_pairs={{0,384},{128,0},{256,128},{384,256},{1,385},{129,1},{257,129},{385... | collective-permute-start | bytes 589832 | tf_op jit(solution)/shard_map/ppermute | solution.py:271
  115.4 2.2 %collective-permute-start.12 = (bf16[768,128]{1,0:T(8,128)(2,1)S(1)}, bf16[768,128]{1,0:T(8,128)(2,1)S(1)}, u32[]{:S(2)}, u32[]{:S(2)}) collective-permute-start(bf16[768,128]{1,0:T(8,128)(2,1)S(1)} %constant_dynamic-update-slice_fusion.refs_5_), channel_id=1, source_target_pairs={{0,4},{4,0},{1,5},{5,1},{2,6},{6,2},{3,7},{7,3},{8,12},{12,8},{9,1... | collective-permute-start | bytes 589832 | tf_op jit(solution)/shard_map/ppermute | solution.py:271
  117.6 2.3 %collective-permute-start.10 = (bf16[768,128]{1,0:T(8,128)(2,1)S(1)}, bf16[768,128]{1,0:T(8,128)(2,1)S(1)}, u32[]{:S(2)}, u32[]{:S(2)}) collective-permute-start(bf16[768,128]{1,0:T(8,128)(2,1)S(1)} %constant_dynamic-update-slice_fusion.refs_5_), channel_id=1, source_target_pairs={{0,256},{128,384},{256,0},{384,128},{1,257},{129,385},{257,1},{385... | collective-permute-start | bytes 589832 | tf_op jit(solution)/shard_map/ppermute | solution.py:271
  119.9 2.6 %collective-permute-start.9 = (bf16[768,128]{1,0:T(8,128)(2,1)S(1)}, bf16[768,128]{1,0:T(8,128)(2,1)S(1)}, u32[]{:S(2)}, u32[]{:S(2)}) collective-permute-start(bf16[768,128]{1,0:T(8,128)(2,1)S(1)} %constant_dynamic-update-slice_fusion.refs_5_), channel_id=1, source_target_pairs={{0,128},{128,256},{256,384},{384,0},{1,129},{129,257},{257,385},{3... | collective-permute-start | bytes 589832 | tf_op jit(solution)/shard_map/ppermute | solution.py:271
  122.5 0.0 collective-permute-done.11.refs_8_
  122.5 2.7 %collective-permute-start.15 = (bf16[768,128]{1,0:T(8,128)(2,1)S(1)}, bf16[768,128]{1,0:T(8,128)(2,1)S(1)}, u32[]{:S(2)}, u32[]{:S(2)}) collective-permute-start(bf16[768,128]{1,0:T(8,128)(2,1)S(1)} %collective-permute-done.11.refs_8_), channel_id=1, source_target_pairs={{0,4},{4,0},{1,5},{5,1},{2,6},{6,2},{3,7},{7,3},{8,12},{12,8},{9,1... | collective-permute-start | bytes 589832 | tf_op jit(solution)/shard_map/ppermute | solution.py:271
  125.2 0.0 collective-permute-done.3.other_ref
  125.2 1.3 slot_sums.1
  126.5 4.6 %collective-permute-start.5 = (bf16[416,256]{1,0:T(8,128)(2,1)S(1)}, bf16[416,256]{1,0:T(8,128)(2,1)S(1)}, u32[]{:S(2)}, u32[]{:S(2)}) collective-permute-start(bf16[416,256]{1,0:T(8,128)(2,1)S(1)} %get-tuple-element.23), channel_id=1, source_target_pairs={{0,3},{1,0},{2,1},{3,2},{4,7},{5,4},{6,5},{7,6},{8,11},{9,8},{10,9... | collective-permute-start | bytes 638984 | tf_op jit(solution)/shard_map/ppermute | solution.py:271
  131.0 0.0 collective-permute-done.12.refs_9_
  131.1 1.9 %collective-permute-start.4 = (bf16[416,256]{1,0:T(8,128)(2,1)S(1)}, bf16[416,256]{1,0:T(8,128)(2,1)S(1)}, u32[]{:S(2)}, u32[]{:S(2)}) collective-permute-start(bf16[416,256]{1,0:T(8,128)(2,1)S(1)} %get-tuple-element.22.refs_0_), channel_id=1, source_target_pairs={{0,1},{1,2},{2,3},{3,0},{4,5},{5,6},{6,7},{7,4},{8,9},{9,10},{10,1... | collective-permute-start | bytes 638984 | tf_op jit(solution)/shard_map/ppermute | solution.py:271
  133.0 0.0 collective-permute-done.10.refs_7_
  133.0 6.5 %collective-permute-start.16 = (bf16[416,256]{1,0:T(8,128)(2,1)S(1)}, bf16[416,256]{1,0:T(8,128)(2,1)S(1)}, u32[]{:S(2)}, u32[]{:S(2)}) collective-permute-start(bf16[416,256]{1,0:T(8,128)(2,1)S(1)} %get-tuple-element.25), channel_id=1, source_target_pairs={{0,2},{1,3},{2,0},{3,1},{4,6},{5,7},{6,4},{7,5},{8,10},{9,11},{10,... | collective-permute-start | bytes 638984 | tf_op jit(solution)/shard_map/ppermute | solution.py:271
  139.5 0.0 collective-permute-done.9.refs_6_
  139.5 2.8 %collective-permute-start.14 = (bf16[768,128]{1,0:T(8,128)(2,1)S(1)}, bf16[768,128]{1,0:T(8,128)(2,1)S(1)}, u32[]{:S(2)}, u32[]{:S(2)}) collective-permute-start(bf16[768,128]{1,0:T(8,128)(2,1)S(1)} %collective-permute-done.10.refs_7_), channel_id=1, source_target_pairs={{0,4},{4,0},{1,5},{5,1},{2,6},{6,2},{3,7},{7,3},{8,12},{12,8},{9,1... | collective-permute-start | bytes 589832 | tf_op jit(solution)/shard_map/ppermute | solution.py:271
  142.3 0.0 collective-permute-done.15.refs_12_
  142.3 1.9 %collective-permute-start.13 = (bf16[768,128]{1,0:T(8,128)(2,1)S(1)}, bf16[768,128]{1,0:T(8,128)(2,1)S(1)}, u32[]{:S(2)}, u32[]{:S(2)}) collective-permute-start(bf16[768,128]{1,0:T(8,128)(2,1)S(1)} %collective-permute-done.9.refs_6_), channel_id=1, source_target_pairs={{0,4},{4,0},{1,5},{5,1},{2,6},{6,2},{3,7},{7,3},{8,12},{12,8},{9,1... | collective-permute-start | bytes 589832 | tf_op jit(solution)/shard_map/ppermute | solution.py:271
  144.2 1.1 constant_dynamic-slice_fusion.3
  145.3 0.0 collective-permute-done.14.refs_11_
  145.3 0.3 collective-permute-done.13.refs_10_
  145.6 0.0 collective-permute-done.5.refs_4_.refs_3_
  145.6 0.0 collective-permute-done.4.refs_3_.refs_2_
  145.6 1.4 input_first.1.refs_0_
  147.0 4.7 %collective-permute-done.16.refs_4_ = bf16[416,256]{1,0:T(8,128)(2,1)S(1)} collective-permute-done((bf16[416,256]{1,0:T(8,128)(2,1)S(1)}, bf16[416,256]{1,0:T(8,128)(2,1)S(1)}, u32[]{:S(2)}, u32[]{:S(2)}) %collective-permute-start.16) | collective-permute-done | bytes 213024 | tf_op jit(solution)/shard_map/ppermute | solution.py:271
  151.7 1.8 %input_gradient.1 = (bf16[384,1024]{1,0:T(8,128)(2,1)}, bf16[32,32]{1,0:T(8,128)(2,1)}) custom-call(s32[8]{0:T(128)S(1)} %compare_select_fusion.4.where_ref, f32[384,1024]{1,0:T(8,128)S(1)} %input_first.1.refs_0_, f32[32,128]{1,0:T(8,128)S(1)} %get-tuple-element.24.refs_1_, bf16[416,256]{1,0:T(8,128)(2,1)S(1)} %collective-permute-done.4.refs_3_.refs_2_, ...), custom_call_target="tpu_custom_call" | custom-call | tf_op jit(solution)/shard_map/input_gradient/pallas_call | solution.py:394
  (8 shorter events, 0.1 us)
Async XLA Ops:
  0.6 18.8 %copy-start.1 = (bf16[384,128]{1,0:T(8,128)(2,1)S(1)}, bf16[384,128]{1,0:T(8,128)(2,1)}, u32[]{:S(2)}) copy-start(bf16[384,128]{1,0:T(8,128)(2,1)} %param.12) | copy-start | bytes 294916
  0.6 18.8 %copy-start.2 = (bf16[384,128]{1,0:T(8,128)(2,1)S(1)}, bf16[384,128]{1,0:T(8,128)(2,1)}, u32[]{:S(2)}) copy-start(bf16[384,128]{1,0:T(8,128)(2,1)} %param.11) | copy-start | bytes 294916
  0.7 9.8 %collective-permute-start = (s32[1]{0:T(128)}, s32[1]{0:T(128)}, u32[]{:S(2)}, u32[]{:S(2)}) collective-permute-start(s32[1]{0:T(128)} %param.13), channel_id=1, source_target_pairs={{0,4},{4,0},{1,5},{5,1},{2,6},{6,2},{3,7},{7,3},{8,12},{12,8},{9,1... | collective-permute-start | bytes 20 | tf_op jit(solution)/shard_map/ppermute | solution.py:271
  12.7 25.3 %all-to-all-start = ((bf16[64,40,128]{2,1,0:T(8,128)(2,1)}), bf16[64,40,128]{2,1,0:T(8,128)(2,1)S(1)}, u32[]{:S(2)}, u32[]{:S(2)}) async-start(bf16[64,40,128]{2,1,0:T(8,128)(2,1)} %row_pack.1), calls=%async_computation | async-start | bytes 1310720 | tf_op jit(solution)/shard_map/all_to_all | solution.py:266
  19.5 3.6 %collective-permute-start.1 = (bf16[384,256]{1,0:T(8,128)(2,1)S(1)}, bf16[384,256]{1,0:T(8,128)(2,1)S(1)}, u32[]{:S(2)}, u32[]{:S(2)}) collective-permute-start(bf16[384,256]{1,0:T(8,128)(2,1)S(1)} %pad_maximum_fusion.1), channel_id=1, source_target_pairs={{0,4},{4,0},{1,5},{5,1},{2,6},{6,2},{3,7},{7,3},{8,12},{12,8},{9,1... | collective-permute-start | bytes 589832 | tf_op jit(solution)/shard_map/ppermute | solution.py:271
  42.6 35.2 %copy-start = (bf16[4096,128]{1,0:T(8,128)(2,1)S(1)}, bf16[4096,128]{1,0:T(8,128)(2,1)}, u32[]{:S(2)}) copy-start(bf16[4096,128]{1,0:T(8,128)(2,1)} %param.17) | copy-start | bytes 3145732
  42.6 25.9 %all-to-all-start.1 = ((bf16[64,40,128]{2,1,0:T(8,128)(2,1)}), bf16[64,40,128]{2,1,0:T(8,128)(2,1)S(1)}, u32[]{:S(2)}, u32[]{:S(2)}) async-start(bf16[64,40,128]{2,1,0:T(8,128)(2,1)} %get-tuple-element.17), calls=%async_computation.1 | async-start | bytes 1310720 | tf_op jit(solution)/shard_map/all_to_all | solution.py:266
  70.0 34.2 %all-to-all-start.2 = ((bf16[64,24,128]{2,1,0:T(8,128)(2,1)}), bf16[64,24,128]{2,1,0:T(8,128)(2,1)S(1)}, u32[]{:S(2)}, u32[]{:S(2)}) async-start(bf16[64,24,128]{2,1,0:T(8,128)(2,1)} %row_merge.1), calls=%async_computation.2 | async-start | bytes 786432 | tf_op jit(solution)/shard_map/all_to_all | solution.py:266
  78.0 22.1 %collective-permute-start.6 = (bf16[256,128]{1,0:T(8,128)(2,1)S(1)}, bf16[256,128]{1,0:T(8,128)(2,1)S(1)}, u32[]{:S(2)}, u32[]{:S(2)}) collective-permute-start(bf16[256,128]{1,0:T(8,128)(2,1)S(1)} %get-tuple-element.30), channel_id=1, source_target_pairs={{0,1},{1,2},{2,3},{3,0},{4,5},{5,6},{6,7},{7,4},{8,9},{9,10},{10,1... | collective-permute-start | bytes 196616 | tf_op jit(solution)/shard_map/ppermute | solution.py:271
  83.8 19.5 %collective-permute-start.2 = (bf16[32,2048]{1,0:T(8,128)(2,1)}, bf16[32,2048]{1,0:T(8,128)(2,1)S(1)}, u32[]{:S(2)}, u32[]{:S(2)}) collective-permute-start(bf16[32,2048]{1,0:T(8,128)(2,1)} %param.15), channel_id=1, source_target_pairs={{0,4},{4,0},{1,5},{5,1},{2,6},{6,2},{3,7},{7,3},{8,12},{12,8},{9,1... | collective-permute-start | bytes 393224 | tf_op jit(solution)/shard_map/ppermute | solution.py:271
  88.8 22.0 %collective-permute-start.8 = (bf16[256,128]{1,0:T(8,128)(2,1)S(1)}, bf16[256,128]{1,0:T(8,128)(2,1)S(1)}, u32[]{:S(2)}, u32[]{:S(2)}) collective-permute-start(bf16[256,128]{1,0:T(8,128)(2,1)S(1)} %get-tuple-element.28), channel_id=1, source_target_pairs={{0,3},{1,0},{2,1},{3,2},{4,7},{5,4},{6,5},{7,6},{8,11},{9,8},{10,9... | collective-permute-start | bytes 196616 | tf_op jit(solution)/shard_map/ppermute | solution.py:271
  94.4 8.9 %collective-permute-start.7 = (bf16[256,128]{1,0:T(8,128)(2,1)S(1)}, bf16[256,128]{1,0:T(8,128)(2,1)S(1)}, u32[]{:S(2)}, u32[]{:S(2)}) collective-permute-start(bf16[256,128]{1,0:T(8,128)(2,1)S(1)} %get-tuple-element.29), channel_id=1, source_target_pairs={{0,2},{1,3},{2,0},{3,1},{4,6},{5,7},{6,4},{7,5},{8,10},{9,11},{10,... | collective-permute-start | bytes 196616 | tf_op jit(solution)/shard_map/ppermute | solution.py:271
  107.4 17.8 %collective-permute-start.3 = (f32[448,256]{1,0:T(8,128)S(1)}, f32[448,256]{1,0:T(8,128)S(1)}, u32[]{:S(2)}, u32[]{:S(2)}) collective-permute-start(f32[448,256]{1,0:T(8,128)S(1)} %get-tuple-element.19), channel_id=1, source_target_pairs={{0,4},{4,0},{1,5},{5,1},{2,6},{6,2},{3,7},{7,3},{8,12},{12,8},{9,1... | collective-permute-start | bytes 1376264 | tf_op jit(solution)/shard_map/ppermute | solution.py:271
  110.8 11.7 %collective-permute-start.11 = (bf16[768,128]{1,0:T(8,128)(2,1)S(1)}, bf16[768,128]{1,0:T(8,128)(2,1)S(1)}, u32[]{:S(2)}, u32[]{:S(2)}) collective-permute-start(bf16[768,128]{1,0:T(8,128)(2,1)S(1)} %constant_dynamic-update-slice_fusion.refs_5_), channel_id=1, source_target_pairs={{0,384},{128,0},{256,128},{384,256},{1,385},{129,1},{257,129},{385... | collective-permute-start | bytes 589832 | tf_op jit(solution)/shard_map/ppermute | solution.py:271
  115.4 15.6 %collective-permute-start.12 = (bf16[768,128]{1,0:T(8,128)(2,1)S(1)}, bf16[768,128]{1,0:T(8,128)(2,1)S(1)}, u32[]{:S(2)}, u32[]{:S(2)}) collective-permute-start(bf16[768,128]{1,0:T(8,128)(2,1)S(1)} %constant_dynamic-update-slice_fusion.refs_5_), channel_id=1, source_target_pairs={{0,4},{4,0},{1,5},{5,1},{2,6},{6,2},{3,7},{7,3},{8,12},{12,8},{9,1... | collective-permute-start | bytes 589832 | tf_op jit(solution)/shard_map/ppermute | solution.py:271
  117.6 15.4 %collective-permute-start.10 = (bf16[768,128]{1,0:T(8,128)(2,1)S(1)}, bf16[768,128]{1,0:T(8,128)(2,1)S(1)}, u32[]{:S(2)}, u32[]{:S(2)}) collective-permute-start(bf16[768,128]{1,0:T(8,128)(2,1)S(1)} %constant_dynamic-update-slice_fusion.refs_5_), channel_id=1, source_target_pairs={{0,256},{128,384},{256,0},{384,128},{1,257},{129,385},{257,1},{385... | collective-permute-start | bytes 589832 | tf_op jit(solution)/shard_map/ppermute | solution.py:271
  119.9 19.6 %collective-permute-start.9 = (bf16[768,128]{1,0:T(8,128)(2,1)S(1)}, bf16[768,128]{1,0:T(8,128)(2,1)S(1)}, u32[]{:S(2)}, u32[]{:S(2)}) collective-permute-start(bf16[768,128]{1,0:T(8,128)(2,1)S(1)} %constant_dynamic-update-slice_fusion.refs_5_), channel_id=1, source_target_pairs={{0,128},{128,256},{256,384},{384,0},{1,129},{129,257},{257,385},{3... | collective-permute-start | bytes 589832 | tf_op jit(solution)/shard_map/ppermute | solution.py:271
  122.5 19.8 %collective-permute-start.15 = (bf16[768,128]{1,0:T(8,128)(2,1)S(1)}, bf16[768,128]{1,0:T(8,128)(2,1)S(1)}, u32[]{:S(2)}, u32[]{:S(2)}) collective-permute-start(bf16[768,128]{1,0:T(8,128)(2,1)S(1)} %collective-permute-done.11.refs_8_), channel_id=1, source_target_pairs={{0,4},{4,0},{1,5},{5,1},{2,6},{6,2},{3,7},{7,3},{8,12},{12,8},{9,1... | collective-permute-start | bytes 589832 | tf_op jit(solution)/shard_map/ppermute | solution.py:271
  126.5 19.2 %collective-permute-start.5 = (bf16[416,256]{1,0:T(8,128)(2,1)S(1)}, bf16[416,256]{1,0:T(8,128)(2,1)S(1)}, u32[]{:S(2)}, u32[]{:S(2)}) collective-permute-start(bf16[416,256]{1,0:T(8,128)(2,1)S(1)} %get-tuple-element.23), channel_id=1, source_target_pairs={{0,3},{1,0},{2,1},{3,2},{4,7},{5,4},{6,5},{7,6},{8,11},{9,8},{10,9... | collective-permute-start | bytes 638984 | tf_op jit(solution)/shard_map/ppermute | solution.py:271
  131.1 14.6 %collective-permute-start.4 = (bf16[416,256]{1,0:T(8,128)(2,1)S(1)}, bf16[416,256]{1,0:T(8,128)(2,1)S(1)}, u32[]{:S(2)}, u32[]{:S(2)}) collective-permute-start(bf16[416,256]{1,0:T(8,128)(2,1)S(1)} %get-tuple-element.22.refs_0_), channel_id=1, source_target_pairs={{0,1},{1,2},{2,3},{3,0},{4,5},{5,6},{6,7},{7,4},{8,9},{9,10},{10,1... | collective-permute-start | bytes 638984 | tf_op jit(solution)/shard_map/ppermute | solution.py:271
  133.0 18.7 %collective-permute-start.16 = (bf16[416,256]{1,0:T(8,128)(2,1)S(1)}, bf16[416,256]{1,0:T(8,128)(2,1)S(1)}, u32[]{:S(2)}, u32[]{:S(2)}) collective-permute-start(bf16[416,256]{1,0:T(8,128)(2,1)S(1)} %get-tuple-element.25), channel_id=1, source_target_pairs={{0,2},{1,3},{2,0},{3,1},{4,6},{5,7},{6,4},{7,5},{8,10},{9,11},{10,... | collective-permute-start | bytes 638984 | tf_op jit(solution)/shard_map/ppermute | solution.py:271
  139.5 5.8 %collective-permute-start.14 = (bf16[768,128]{1,0:T(8,128)(2,1)S(1)}, bf16[768,128]{1,0:T(8,128)(2,1)S(1)}, u32[]{:S(2)}, u32[]{:S(2)}) collective-permute-start(bf16[768,128]{1,0:T(8,128)(2,1)S(1)} %collective-permute-done.10.refs_7_), channel_id=1, source_target_pairs={{0,4},{4,0},{1,5},{5,1},{2,6},{6,2},{3,7},{7,3},{8,12},{12,8},{9,1... | collective-permute-start | bytes 589832 | tf_op jit(solution)/shard_map/ppermute | solution.py:271
  142.3 3.3 %collective-permute-start.13 = (bf16[768,128]{1,0:T(8,128)(2,1)S(1)}, bf16[768,128]{1,0:T(8,128)(2,1)S(1)}, u32[]{:S(2)}, u32[]{:S(2)}) collective-permute-start(bf16[768,128]{1,0:T(8,128)(2,1)S(1)} %collective-permute-done.9.refs_6_), channel_id=1, source_target_pairs={{0,4},{4,0},{1,5},{5,1},{2,6},{6,2},{3,7},{7,3},{8,12},{12,8},{9,1... | collective-permute-start | bytes 589832 | tf_op jit(solution)/shard_map/ppermute | solution.py:271

commit v6 on v5

v6 whole, which is shorter than its diff:
```python
import functools

import jax
import jax.numpy as jnp
from jax import lax
from jax.experimental import pallas as pl
from jax.experimental.pallas import tpu as pltpu
from jax.sharding import Mesh
from jax.sharding import PartitionSpec as P

HEAD_WIDTH = 128
SEQ = ("seq_0", "seq_1", "seq_2", "seq_3")
FAR = ("seq_0", "seq_1")
TEAM = ("seq_2", "seq_3")
MEMBERS = 4
LOWEST_SCORE = -1e30
LOWEST_PEAK = -1e29
DEAD = 1e9
SCALE = HEAD_WIDTH ** (-0.5)
F32 = jnp.float32
BF16 = jnp.bfloat16
VMEM = pl.BlockSpec(memory_space=pltpu.VMEM)
PARAMS = pltpu.CompilerParams(vmem_limit_bytes=32 * 1024 * 1024)
SMEM = pl.BlockSpec(memory_space=pltpu.SMEM)


def rows_dot(a, b):
    return lax.dot_general(a, b, (((1,), (1,)), ((), ())), preferred_element_type=F32)


def plain_dot(a, b):
    return lax.dot_general(a, b, (((1,), (0,)), ((), ())), preferred_element_type=F32)


def three_parts(value):
    high = value.astype(BF16).astype(F32)
    rest = value - high
    middle = rest.astype(BF16).astype(F32)
    low = (rest - middle).astype(BF16).astype(F32)
    return high, middle, low


def spread(held):
    axis = held.ndim - 1
    high, middle, low = three_parts(held)
    return high + pltpu.roll(middle, 16, axis) + pltpu.roll(low, 32, axis)


def gathered_parts(block):
    wide = block.astype(F32)
    axis = wide.ndim - 1
    return wide + pltpu.roll(wide, 112, axis) + pltpu.roll(wide, 96, axis)


def pack_kernel(heads, *refs):
    length_refs, (q_ref, g_ref, row_ref) = refs[:MEMBERS], refs[MEMBERS:]
    lane = lax.broadcasted_iota(jnp.int32, (8, 128), 1)
    numbers = jnp.zeros((8, 128), jnp.int32)
    for e, ref in enumerate(length_refs):
        numbers += jnp.where(lane == 2 * e, ref[0] // 16, 0)
        numbers += jnp.where(lane == 2 * e + 1, ref[0] % 16, 0)
    lines = []
    for ref in (q_ref, g_ref):
        wide = ref[...].astype(F32)
        lines += [wide[:, h * HEAD_WIDTH : (h + 1) * HEAD_WIDTH] for h in range(heads)]
    row = jnp.concatenate([*lines, numbers.astype(F32)], axis=0).astype(BF16)
    for k in range(row_ref.shape[0]):
        row_ref[k] = row


def first_kernel(heads, group, where_ref, x_ref, *refs):
    cache_refs, (y_ref, place_ref) = refs[:MEMBERS], refs[MEMBERS:]
    rows = x_ref.shape[0]
    block = cache_refs[0].shape[0]
    far, team, span, row_total = (where_ref[0], where_ref[1], where_ref[2], where_ref[3])
    lens = x_ref[:, 2 * heads :, :].astype(F32)
    lane = lax.broadcasted_iota(jnp.int32, lens.shape, 2)
    row = lax.broadcasted_iota(jnp.int32, lens.shape, 0)
    first_line = lax.broadcasted_iota(jnp.int32, lens.shape, 1) == 0
    used = first_line & (lane < 2 * MEMBERS)
    lens = lens * jnp.where(used, jnp.where(lane % 2 == 0, 16.0, 1.0), 0.0)
    base = jnp.sum(jnp.where(row < far, lens, 0.0))
    here = jnp.where(row == far, lens, 0.0)
    held = [jnp.sum(jnp.where(lane // 2 == e, here, 0.0)) for e in range(MEMBERS)]
    within = lax.broadcasted_iota(jnp.int32, (1, block), 1).astype(F32)
    position = []
    for e in range(MEMBERS):
        offset = base
        for other in range(MEMBERS):
            offset += jnp.where((team ^ other) < (team ^ e), held[other], 0.0)
        place_ref[e] = offset
        place_ref[MEMBERS + e] = held[e]
        position.append(jnp.where(within < held[e], offset + within, DEAD))
    position = jnp.concatenate(position, axis=1)
    tall = group * heads
    index = lax.broadcasted_iota(jnp.int32, (tall, 1), 0) // heads
    lane = lax.broadcasted_iota(jnp.int32, (tall, 128), 1)
    keys = jnp.concatenate([ref[:, :HEAD_WIDTH] for ref in cache_refs], axis=0)
    values = jnp.concatenate([ref[:, HEAD_WIDTH:] for ref in cache_refs], axis=0)
    for first in range(0, rows, group):
        part = pl.ds(first, group)
        q = x_ref[part, :heads, :].reshape(tall, HEAD_WIDTH)
        g = x_ref[part, heads : 2 * heads, :].reshape(tall, HEAD_WIDTH)
        asked = (span * row_total + MEMBERS * (first + index) + team).astype(F32)
        scores = jnp.where(position <= asked, rows_dot(q, keys) * SCALE, LOWEST_SCORE)
        peak = jnp.maximum(jnp.max(scores, axis=1, keepdims=True), LOWEST_PEAK)
        raised = jnp.exp(scores - peak)
        grads = rows_dot(g, values)
        total = jnp.sum(raised, axis=1, keepdims=True)
        mean = jnp.sum(raised * grads, axis=1, keepdims=True) / jnp.maximum(total, 0.5)
        moved = (raised * (grads - mean)).astype(BF16)
        both = plain_dot(jnp.concatenate([moved, raised.astype(BF16)], axis=0), keys)
        y_ref[part, :heads, :] = both[:tall].astype(BF16).reshape(group, heads, HEAD_WIDTH)
        y_ref[part, heads : 2 * heads, :] = both[tall:].astype(BF16).reshape(group, heads, HEAD_WIDTH)
        held = jnp.where(lane == 0, peak, jnp.where(lane == 1, total, jnp.where(lane == 2, mean, 0.0)))
        held = spread(held).reshape(group, 2, heads // 2, 128)
        held = held[:, 0] + pltpu.roll(held[:, 1], 64, 2)
        y_ref[part, 2 * heads :, :] = held.astype(BF16)


def merge_kernel(heads, z_ref, u_ref):
    stats = gathered_parts(z_ref[:, 2 * heads :, :])
    total = pltpu.roll(stats, 127, 2)
    mean = pltpu.roll(stats, 126, 2)
    row_peak = jnp.max(stats, axis=0, keepdims=True)
    share = jnp.exp(stats - row_peak)
    part = share * total
    row_total = jnp.sum(part, axis=0, keepdims=True)
    row_mean = jnp.sum(part * mean, axis=0, keepdims=True) / row_total
    moved_factor = share * (SCALE / row_total)
    plain_factor = moved_factor * (mean - row_mean)

    def of_heads(factor):
        return jnp.concatenate([factor[:, :, 0:1], factor[:, :, 64:65]], axis=1)

    term = z_ref[:, :heads, :].astype(F32) * of_heads(moved_factor)
    term += z_ref[:, heads : 2 * heads, :].astype(F32) * of_heads(plain_factor)
    query_grads = jnp.sum(term, axis=0).astype(BF16)
    lane = lax.broadcasted_iota(jnp.int32, (heads // 2, 128), 1) % 64
    found = jnp.where(lane == 0, row_peak[0], 0.0)
    found = jnp.where(lane == 1, pltpu.roll(row_total[0], 1, 1), found)
    found = jnp.where(lane == 2, pltpu.roll(row_mean[0], 2, 1), found)
    found = spread(found).astype(BF16)
    for k in range(u_ref.shape[0]):
        u_ref[k, :heads, :] = query_grads
        u_ref[k, heads:, :] = found


def second_kernel(heads, group, where_ref, place_ref, x_ref, u_ref, *refs):
    cache_refs, w_refs = refs[:MEMBERS], refs[MEMBERS : 2 * MEMBERS]
    keep_ref, send_ref = refs[2 * MEMBERS :]
    rows = x_ref.shape[0]
    block = cache_refs[0].shape[0]
    slots = MEMBERS * block
    team, span, row_total = (where_ref[1], where_ref[2], where_ref[3])
    within = lax.broadcasted_iota(jnp.int32, (block, 1), 0).astype(F32)
    position = jnp.concatenate(
        [
            jnp.where(within < place_ref[MEMBERS + e], place_ref[e] + within, DEAD)
            for e in range(MEMBERS)
        ],
        axis=0,
    )
    wide = group * heads
    index = lax.broadcasted_iota(jnp.int32, (1, wide), 1) // heads
    stats = gathered_parts(u_ref[:, heads:, :])
    keys = jnp.concatenate([ref[:, :HEAD_WIDTH] for ref in cache_refs], axis=0)
    values = jnp.concatenate([ref[:, HEAD_WIDTH:] for ref in cache_refs], axis=0)
    value_grads = jnp.zeros((slots, HEAD_WIDTH), F32)
    key_grads = jnp.zeros((slots, HEAD_WIDTH), F32)
    for first in range(0, rows, group):
        part = pl.ds(first, group)
        q = x_ref[part, :heads, :].reshape(wide, HEAD_WIDTH)
        g = x_ref[part, heads : 2 * heads, :].reshape(wide, HEAD_WIDTH)
        held = stats[first : first + group]
        held = jnp.concatenate([held, pltpu.roll(held, 64, 2)], axis=1).reshape(wide, 128)
        turned = jnp.transpose(held)
        asked = (span * row_total + MEMBERS * (first + index) + team).astype(F32)
        scores = rows_dot(keys, q) * SCALE
        raised = jnp.exp(jnp.where(position <= asked, scores - turned[0:1], LOWEST_SCORE))
        weights = raised * (1.0 / turned[1:2])
        score_grads = weights * (rows_dot(values, g) - turned[2:3])
        value_grads += plain_dot(weights.astype(BF16), g)
        key_grads += plain_dot(score_grads.astype(BF16), q)
    key_grads *= SCALE
    low = jnp.concatenate([u_ref[:, h, :] for h in range(heads)], axis=1)
    features = w_refs[0].shape[0]
    both = rows_dot(low, jnp.concatenate([ref[...] for ref in w_refs], axis=0))
    for e in range(MEMBERS):
        ref, at = (keep_ref, send_ref)[e % 2], e // 2
        part = slice(e * block, (e + 1) * block)
        ref[at, :block, :HEAD_WIDTH] = key_grads[part]
        ref[at, :block, HEAD_WIDTH:] = value_grads[part]
        ref[at, block:, :] = jnp.zeros((rows, 2 * HEAD_WIDTH), F32)
        ref[at, block:, :features] = both[:, e * features : (e + 1) * features]


def joined_parts(value, features):
    lane = lax.broadcasted_iota(jnp.int32, value.shape, 1)
    high, middle, low = three_parts(jnp.where(lane < features, value, 0.0))
    wide = high + pltpu.roll(middle, features, 1) + pltpu.roll(low, 2 * features, 1)
    return jnp.concatenate([wide, jnp.zeros_like(wide)], axis=1).astype(BF16)


def split_parts(block, features):
    wide = block[:, :128].astype(F32)
    return wide + pltpu.roll(wide, 128 - features, 1) + pltpu.roll(wide, 128 - 2 * features, 1)


def core_kernel(block, features, keep_ref, other_ref, stay_ref, leave_ref):
    rows = keep_ref.shape[1] - block
    stay_ref[:block, :] = keep_ref[0, :block, :] + other_ref[0, :block, :]
    stay_ref[block : block + rows, :] = keep_ref[0, block:, :]
    stay_ref[block + rows :, :] = other_ref[0, block:, :]
    leave_ref[:block, :] = (keep_ref[1, :block, :] + other_ref[1, :block, :]).astype(BF16)
    leave_ref[block : block + rows, :] = joined_parts(keep_ref[1, block:, :128], features)
    leave_ref[block + rows :, :] = joined_parts(other_ref[1, block:, :128], features)


def finish_kernel(
    groups, features, where_ref, stay_ref, other_ref, k_ref, v_ref, span_ref, *out_refs
):
    out_refs, lines_ref = out_refs[:-1], out_refs[-1]
    block = k_ref.shape[0]
    rows = (stay_ref.shape[0] - block) // 2
    per = rows // groups
    sums = (stay_ref[:block, :] + other_ref[:block, :].astype(F32)).astype(BF16)
    k_ref[...] = sums[:, :HEAD_WIDTH]
    v_ref[...] = sums[:, HEAD_WIDTH:]
    team, mine = where_ref[1], where_ref[4]
    lane = lax.broadcasted_iota(jnp.int32, (rows, 128), 1)
    apart = [stay_ref[block : block + rows, :128], stay_ref[block + rows :, :128]]
    apart += [
        split_parts(other_ref[block : block + rows, :], features),
        split_parts(other_ref[block + rows :, :], features),
    ]
    for member in range(MEMBERS):
        value = apart[0]
        for e in range(1, MEMBERS):
            value = jnp.where((team ^ e) == member, apart[e], value)
        lines_ref[member, :, :] = jnp.where(lane < features, value, 0.0)

    def block_rows(target):
        start = per * target
        if per % 8 == 0:
            start = pl.multiple_of(start, 8)
        part = pl.ds(start, per)
        return jnp.concatenate([lines_ref[m, part, :] for m in range(MEMBERS)], axis=0)

    span_ref[...] = block_rows(mine)
    for k, ref in enumerate(out_refs, 1):
        ref[:block, :] = sums
        ref[block:, :] = joined_parts(block_rows(lax.rem(mine + k, groups)), features)


def input_kernel(others, groups, first, where_ref, *refs):
    is_first = where_ref[5] == 0
    count = len(others)
    if first:
        (own_ref, own_k_ref, own_v_ref), refs = refs[:3], refs[3:]
    else:
        total_ref, span_ref, *spans = refs[: groups]
        refs = refs[groups:]
    arrived, here, there = (refs[:count], refs[count : 2 * count], refs[2 * count : 3 * count])
    refs = refs[3 * count :]
    out_ref = refs[0]
    half = out_ref.shape[0]
    left = [own_ref[:half, :]] if first else []
    for ref in arrived:
        keys, values = ref[:half, :HEAD_WIDTH], ref[:half, HEAD_WIDTH:]
        left += [jnp.where(is_first, keys, values), jnp.where(is_first, values, keys)]
    left = jnp.concatenate(left, axis=1)
    step = min(256, out_ref.shape[1])
    for start in range(0, out_ref.shape[1], step):
        part = pl.ds(start, step)
        right = [own_k_ref[part, :], own_v_ref[part, :]] if first else []
        for near_ref, far_ref in zip(here, there):
            right += [near_ref[part, :], far_ref[part, :]]
        term = rows_dot(left, jnp.concatenate(right, axis=1))
        out_ref[:, part] = term if first else (total_ref[:, part] + term).astype(BF16)
    if first:
        return
    block_ref, turn_ref = refs[1:3]
    rows, features = block_ref.shape
    span = span_ref[...]
    for ref in (*spans, *arrived):
        span += split_parts(ref[half:, :], features)
    per = rows // MEMBERS
    for member in range(MEMBERS):
        turn_ref[pl.ds(member, per, stride=MEMBERS), :] = span[member * per : (member + 1) * per]
    block_ref[...] = turn_ref[:, :features].astype(BF16)


def exchanged(value, axes):
    return lax.all_to_all(value, axes, split_axis=0, concat_axis=0, tiled=True)


def shifted(value, axis, by):
    count = lax.axis_size(axis)
    return lax.ppermute(value, axis, [(k, (k + by) % count) for k in range(count)])


def partner(value, distance):
    return lax.ppermute(value, TEAM, [(k, k ^ distance) for k in range(MEMBERS)])


def local(
    queries,
    grad_output,
    key_cache,
    saved_value_rows,
    lengths,
    span_index,
    w_query,
    key_projection_weight,
    value_projection_weight,
):
    heads = queries.shape[1] // HEAD_WIDTH
    rows = lax.axis_size(FAR)
    block = key_cache.shape[0]
    groups = lax.axis_size("head")
    team = lax.axis_index(TEAM)
    core = lax.axis_index("seq_3")
    far = lax.axis_index(FAR)
    mine = lax.axis_index("head")
    lines = 2 * heads + 8
    group = min(8, rows)

    lens = [lengths]
    for e in range(1, MEMBERS):
        lens.append(partner(lengths, e))
    row = pl.pallas_call(
        functools.partial(pack_kernel, heads),
        out_shape=jax.ShapeDtypeStruct((rows, lines, HEAD_WIDTH), BF16),
        in_specs=[SMEM] * MEMBERS + [VMEM, VMEM],
        out_specs=VMEM,
        name="row_pack",
    )(*lens, queries, grad_output)
    x = exchanged(row, FAR)

    cache = jnp.concatenate([key_cache, saved_value_rows], axis=1)
    cache_2 = partner(cache, 2)
    cache_1 = partner(cache, 1)
    cache_3 = partner(cache_2, 1)
    caches = (cache, cache_1, cache_2, cache_3)

    features = key_projection_weight.shape[0] // groups
    half_weights = jnp.where(core == 0, key_projection_weight, value_projection_weight)
    near, there = {}, {}
    for k in range(1, groups):
        start = lax.rem(mine + k, groups) * features
        piece = lax.dynamic_slice_in_dim(half_weights, start, features, 0)
        near[k] = shifted(piece, "head", k)
        there[k] = partner(near[k], 1)
    own_weights = [
        lax.dynamic_slice_in_dim(w, mine * features, features, 0)
        for w in (key_projection_weight, value_projection_weight)
    ]
    query_2 = partner(w_query, 2)
    query_1 = partner(w_query, 1)
    query_3 = partner(query_2, 1)
    query_weights = (w_query, query_1, query_2, query_3)

    where = jnp.full((8,), MEMBERS * rows, jnp.int32)
    for k, number in ((0, far), (1, team), (2, span_index[0]), (4, mine), (5, core)):
        where = jnp.where(jnp.arange(8) == k, number, where)
    y, place = pl.pallas_call(
        functools.partial(first_kernel, heads, group),
        out_shape=(
            jax.ShapeDtypeStruct((rows, lines, HEAD_WIDTH), BF16),
            jax.ShapeDtypeStruct((2 * MEMBERS,), F32),
        ),
        in_specs=[SMEM] + [VMEM] * (1 + MEMBERS),
        out_specs=(VMEM, SMEM),
        name="row_partials",
        compiler_params=PARAMS,
    )(where, x, *caches)
    arrived = exchanged(y, FAR)
    merged = pl.pallas_call(
        functools.partial(merge_kernel, heads),
        out_shape=jax.ShapeDtypeStruct((rows, heads + 8, HEAD_WIDTH), BF16),
        in_specs=[VMEM],
        out_specs=VMEM,
        name="row_merge",
        compiler_params=PARAMS,
    )(arrived)
    u = exchanged(merged, FAR)
    width = w_query.shape[0]
    slot_call = pl.pallas_call(
        functools.partial(second_kernel, heads, min(16, rows)),
        out_shape=(jax.ShapeDtypeStruct((2, block + rows, 2 * HEAD_WIDTH), F32),) * 2,
        in_specs=[SMEM, SMEM] + [VMEM] * (2 + 2 * MEMBERS),
        out_specs=(VMEM, VMEM),
        name="slot_gradients",
        compiler_params=PARAMS,
    )
    kept, crossing = slot_call(where, place, x, u, *caches, *query_weights)
    other_core = partner(crossing, 1)
    stay, leave = pl.pallas_call(
        functools.partial(core_kernel, block, width),
        out_shape=(
            jax.ShapeDtypeStruct((block + 2 * rows, 2 * HEAD_WIDTH), F32),
            jax.ShapeDtypeStruct((block + 2 * rows, 2 * HEAD_WIDTH), BF16),
        ),
        in_specs=[VMEM, VMEM],
        out_specs=(VMEM, VMEM),
        name="core_sums",
        compiler_params=PARAMS,
    )(kept, other_core)
    other_chip = partner(leave, 2)
    per = rows // groups
    saved_key_gradient, saved_value_gradient, own_span, *leaving = pl.pallas_call(
        functools.partial(finish_kernel, groups, width),
        out_shape=(
            jax.ShapeDtypeStruct((block, HEAD_WIDTH), BF16),
            jax.ShapeDtypeStruct((block, HEAD_WIDTH), BF16),
            jax.ShapeDtypeStruct((MEMBERS * per, 128), F32),
        )
        + (jax.ShapeDtypeStruct((block + MEMBERS * per, 2 * HEAD_WIDTH), BF16),) * (groups - 1),
        in_specs=[SMEM, VMEM, VMEM],
        out_specs=(VMEM,) * (2 + groups),
        scratch_shapes=[pltpu.VMEM((MEMBERS, rows, 128), F32)],
        name="slot_sums",
        compiler_params=PARAMS,
    )(where, stay, other_chip)

    pieces = {}
    for k, piece in enumerate(leaving, 1):
        pieces[k] = shifted(piece, "head", k)
    early = [k for k in pieces if k != 2]
    of = lambda held, wanted: [held[k] for k in wanted]
    total = pl.pallas_call(
        functools.partial(input_kernel, early, groups, True),
        out_shape=jax.ShapeDtypeStruct((block, features), F32),
        in_specs=[SMEM] + [VMEM] * (3 + 3 * len(early)),
        out_specs=VMEM,
        name="input_first",
        compiler_params=PARAMS,
    )(where, leaving[0], *own_weights, *of(pieces, early), *of(near, early), *of(there, early))
    cached_input_gradient, grad_span_input = pl.pallas_call(
        functools.partial(input_kernel, [2], groups, False),
        out_shape=(
            jax.ShapeDtypeStruct((block, features), BF16),
            jax.ShapeDtypeStruct((MEMBERS * per, width), BF16),
        ),
        in_specs=[SMEM] + [VMEM] * (groups + 3),
        out_specs=(VMEM, VMEM),
        scratch_shapes=[pltpu.VMEM((MEMBERS * per, 128), F32)],
        name="input_gradient",
        compiler_params=PARAMS,
    )(where, total, own_span, *of(pieces, early), pieces[2], near[2], there[2])
    return (saved_key_gradient, saved_value_gradient, cached_input_gradient, grad_span_input)


def solution(mesh):
    split = Mesh(
        mesh.devices.reshape(4, 8, 2, 2, mesh.shape["head"]),
        ("seq_0", "seq_1", "seq_2", "seq_3", "head"),
    )
    in_specs = (
        P(SEQ, "head"),
        P(SEQ, "head"),
        P(SEQ, "head"),
        P(SEQ, "head"),
        P(SEQ),
        P(),
        P(SEQ, "head"),
        P(None, "head"),
        P(None, "head"),
    )
    out_specs = (P(SEQ, "head"), P(SEQ, "head"), P(SEQ, "head"), P("head", SEQ))
    return jax.shard_map(local, mesh=split, in_specs=in_specs, out_specs=out_specs, check_vma=False)
```

time: 156 us -> 169 us (1.083)
  the two profiles are of different devices: /device:TPU:1 before, /device:TPU:64 now
where the time goes in v6:
time: 169 us; the launch traced here: 168 us
  starting transfers between devices  85.8 us (51%)
  waiting for transfers between devices  34.2 us (20%)
  blocking collectives  22.9 us (14%)
  Pallas kernels  17.9 us (11%)
  local copies, waits for them, and re-layouts  3 us (2%)
  between operations  2.32 us (1%)
    ppermute x14, starting transfers between devices, partner(): lax.ppermute(value, TEAM, [(k, k ^ distance) for k in range(MEMBERS)])  39.3 us
    ppermute x6, starting transfers between devices, shifted(): lax.ppermute(value, axis, [(k, (k + by) % count) for k in range(count)])  36.4 us
    ppermute x6, waiting for transfers between devices, shifted(): lax.ppermute(value, axis, [(k, (k + by) % count) for k in range(count)])  24.5 us
    all_to_all x1, blocking collectives, exchanged(): return lax.all_to_all(value, axes, split_axis=0, concat_axis=0, tiled=True)  22.9 us
    all_to_all x2, starting transfers between devices, exchanged(): return lax.all_to_all(value, axes, split_axis=0, concat_axis=0, tiled=True)  10.1 us
    ppermute x14, waiting for transfers between devices, partner(): lax.ppermute(value, TEAM, [(k, k ^ distance) for k in range(MEMBERS)])  8.81 us
    pallas_call x1, Pallas kernels, local(): pl.pallas_call(functools.partial(first_kernel, heads, group), out_shape=(...  4.43 us
    pallas_call x1, Pallas kernels, local(): kept, crossing = slot_call(where, place, x, u, *caches, *query_weights)  4.32 us
  transfers between devices with their start and end apart: 22, of which 10 were waited for; matrix products, arithmetic and copies ran while one was open for 3% of the time, Pallas kernels for 2%

profile of v6, /device:TPU:64, one launch (start us, length us, event | category | flops | bytes accessed | tf_op | source)
XLA Modules:
  0.0 167.6 jit_solution(5197509545915225138)
XLA Ops:
  0.6 1.9 %collective-permute-start = (s32[1]{0:T(128)}, s32[1]{0:T(128)}, u32[]{:S(2)}, u32[]{:S(2)}) collective-permute-start(s32[1]{0:T(128)} %param.13), channel_id=1, source_target_pairs={{0,4},{4,0},{8,12},{12,8},{1,5},{5,1},{9,13},{13,9},{2,6},{6,2},{1... | collective-permute-start | bytes 20 | tf_op jit(solution)/shard_map/ppermute | solution.py:304
  2.6 6.9 %collective-permute-start.1 = (s32[1]{0:T(128)}, s32[1]{0:T(128)}, u32[]{:S(2)}, u32[]{:S(2)}) collective-permute-start(s32[1]{0:T(128)} %param.13), channel_id=1, source_target_pairs={{0,8},{4,12},{8,0},{12,4},{1,9},{5,13},{9,1},{13,5},{2,10},{6,14},... | collective-permute-start | bytes 20 | tf_op jit(solution)/shard_map/ppermute | solution.py:304
  9.5 2.0 %collective-permute-start.2 = (s32[1]{0:T(128)}, s32[1]{0:T(128)}, u32[]{:S(2)}, u32[]{:S(2)}) collective-permute-start(s32[1]{0:T(128)} %param.13), channel_id=1, source_target_pairs={{0,12},{4,8},{8,4},{12,0},{1,13},{5,9},{9,5},{13,1},{2,14},{6,10},... | collective-permute-start | bytes 20 | tf_op jit(solution)/shard_map/ppermute | solution.py:304
  12.2 0.0 collective-permute-done.refs_1_
  12.2 0.0 collective-permute-done.1.refs_2_
  12.2 2.3 %collective-permute-done.2.refs_3_ = s32[1]{0:T(128)} collective-permute-done((s32[1]{0:T(128)}, s32[1]{0:T(128)}, u32[]{:S(2)}, u32[]{:S(2)}) %collective-permute-start.2) | collective-permute-done | bytes 36 | tf_op jit(solution)/shard_map/ppermute | solution.py:304
  14.5 3.4 %row_pack.1 = bf16[32,40,128]{2,1,0:T(8,128)(2,1)} custom-call(s32[1]{0:T(128)S(6)} %copy.14.refs_0_, s32[1]{0:T(128)} %collective-permute-done.refs_1_, s32[1]{0:T(128)} %collective-permute-done.1.refs_2_, s32[1]{0:T(128)} %collective-permute-done.2.refs_3_, bf16[1,2048]{1,0:T(2,128)(2,1)} %refs_4_.2, bf16[1,2048]{1,0:T(2,128)(2,1)} %refs_5_.1), custom_call_target="tpu_custom_call" | custom-call | tf_op jit(solution)/shard_map/row_pack/pallas_call | solution.py:332
  17.8 5.1 %all-to-all-start = ((bf16[32,40,128]{2,1,0:T(8,128)(2,1)}), bf16[32,40,128]{2,1,0:T(8,128)(2,1)S(1)}, u32[]{:S(2)}, u32[]{:S(2)}) async-start(bf16[32,40,128]{2,1,0:T(8,128)(2,1)} %row_pack.1), calls=%async_computation | async-start | bytes 655360 | tf_op jit(solution)/shard_map/all_to_all | solution.py:295
  23.0 0.0 copy-start
  23.0 0.9 constant_dynamic-update-slice_fusion.1
  23.9 0.9 constant_dynamic-update-slice_fusion.refs_0_
  24.9 3.7 %collective-permute-start.4 = (bf16[384,256]{1,0:T(8,128)(2,1)S(1)}, bf16[384,256]{1,0:T(8,128)(2,1)S(1)}, u32[]{:S(2)}, u32[]{:S(2)}) collective-permute-start(bf16[384,256]{1,0:T(8,128)(2,1)S(1)} %constant_dynamic-update-slice_fusion.refs_0_), channel_id=1, source_target_pairs={{0,8},{4,12},{8,0},{12,4},{1,9},{5,13},{9,1},{13,5},{2,10},{6,14},... | collective-permute-start | bytes 589832 | tf_op jit(solution)/shard_map/ppermute | solution.py:304
  28.6 1.9 %collective-permute-start.3 = (bf16[384,256]{1,0:T(8,128)(2,1)S(1)}, bf16[384,256]{1,0:T(8,128)(2,1)S(1)}, u32[]{:S(2)}, u32[]{:S(2)}) collective-permute-start(bf16[384,256]{1,0:T(8,128)(2,1)S(1)} %constant_dynamic-update-slice_fusion.refs_0_), channel_id=1, source_target_pairs={{0,4},{4,0},{8,12},{12,8},{1,5},{5,1},{9,13},{13,9},{2,6},{6,2},{1... | collective-permute-start | bytes 589832 | tf_op jit(solution)/shard_map/ppermute | solution.py:304
  30.5 3.2 %collective-permute-done.4.refs_2_ = bf16[384,256]{1,0:T(8,128)(2,1)S(1)} collective-permute-done((bf16[384,256]{1,0:T(8,128)(2,1)S(1)}, bf16[384,256]{1,0:T(8,128)(2,1)S(1)}, u32[]{:S(2)}, u32[]{:S(2)}) %collective-permute-start.4) | collective-permute-done | bytes 196640 | tf_op jit(solution)/shard_map/ppermute | solution.py:304
  33.7 1.9 %collective-permute-start.5 = (bf16[384,256]{1,0:T(8,128)(2,1)S(1)}, bf16[384,256]{1,0:T(8,128)(2,1)S(1)}, u32[]{:S(2)}, u32[]{:S(2)}) collective-permute-start(bf16[384,256]{1,0:T(8,128)(2,1)S(1)} %collective-permute-done.4.refs_2_), channel_id=1, source_target_pairs={{0,4},{4,0},{8,12},{12,8},{1,5},{5,1},{9,13},{13,9},{2,6},{6,2},{1... | collective-permute-start | bytes 589832 | tf_op jit(solution)/shard_map/ppermute | solution.py:304
  36.3 0.0 collective-permute-done.3.refs_1_
  36.3 0.7 collective-permute-done.5.refs_3_
  37.1 0.0 all-to-all-done.x_ref
  37.1 4.4 %row_partials.1 = (bf16[32,40,128]{2,1,0:T(8,128)(2,1)S(1)}, f32[8]{0:T(128)S(1)}) custom-call(s32[8]{0:T(128)S(1)} %compare_select_fusion.4.where_ref, bf16[32,40,128]{2,1,0:T(8,128)(2,1)S(1)} %all-to-all-done.x_ref, bf16[384,256]{1,0:T(8,128)(2,1)S(1)} %constant_dynamic-update-slice_fusion.refs_0_, bf16[384,256]{1,0:T(8,128)(2,1)S(1)} %collective-permute-done.3.refs_1_, ...), custom_call_target="tpu_custom_call" | custom-call | tf_op jit(solution)/shard_map/row_partials/pallas_call | solution.py:367
  41.5 22.9 %all_to_all.15.z_ref = bf16[32,40,128]{2,1,0:T(8,128)(2,1)S(1)} all-to-all(bf16[32,40,128]{2,1,0:T(8,128)(2,1)S(1)} %get-tuple-element.19), channel_id=1, replica_groups=mesh['seq_0'=4,'seq_1'=8,'seq_2'=2,'seq_3'=2,'head'=4] {'seq_0','seq_1'}, dimensions={0} | all-to-all | bytes 655360 | tf_op jit(solution)/shard_map/all_to_all | solution.py:295
  64.4 1.2 row_merge.1
  65.6 4.9 %all-to-all-start.2 = ((bf16[32,24,128]{2,1,0:T(8,128)(2,1)}), bf16[32,24,128]{2,1,0:T(8,128)(2,1)S(1)}, u32[]{:S(2)}, u32[]{:S(2)}) async-start(bf16[32,24,128]{2,1,0:T(8,128)(2,1)} %row_merge.1), calls=%async_computation.2 | async-start | bytes 393216 | tf_op jit(solution)/shard_map/all_to_all | solution.py:295
  70.6 0.0 copy-done
  70.6 3.6 %collective-permute-start.7 = (bf16[32,2048]{1,0:T(8,128)(2,1)S(1)}, bf16[32,2048]{1,0:T(8,128)(2,1)S(1)}, u32[]{:S(2)}, u32[]{:S(2)}) collective-permute-start(bf16[32,2048]{1,0:T(8,128)(2,1)S(1)} %copy-done), channel_id=1, source_target_pairs={{0,8},{4,12},{8,0},{12,4},{1,9},{5,13},{9,1},{13,5},{2,10},{6,14},... | collective-permute-start | bytes 393224 | tf_op jit(solution)/shard_map/ppermute | solution.py:304
  74.3 1.9 %collective-permute-start.6 = (bf16[32,2048]{1,0:T(8,128)(2,1)S(1)}, bf16[32,2048]{1,0:T(8,128)(2,1)S(1)}, u32[]{:S(2)}, u32[]{:S(2)}) collective-permute-start(bf16[32,2048]{1,0:T(8,128)(2,1)S(1)} %copy-done), channel_id=1, source_target_pairs={{0,4},{4,0},{8,12},{12,8},{1,5},{5,1},{9,13},{13,9},{2,6},{6,2},{1... | collective-permute-start | bytes 393224 | tf_op jit(solution)/shard_map/ppermute | solution.py:304
  76.2 1.3 collective-permute-done.7.refs_6_
  77.5 1.9 %collective-permute-start.8 = (bf16[32,2048]{1,0:T(8,128)(2,1)S(1)}, bf16[32,2048]{1,0:T(8,128)(2,1)S(1)}, u32[]{:S(2)}, u32[]{:S(2)}) collective-permute-start(bf16[32,2048]{1,0:T(8,128)(2,1)S(1)} %collective-permute-done.7.refs_6_), channel_id=1, source_target_pairs={{0,4},{4,0},{8,12},{12,8},{1,5},{5,1},{9,13},{13,9},{2,6},{6,2},{1... | collective-permute-start | bytes 393224 | tf_op jit(solution)/shard_map/ppermute | solution.py:304
  79.4 0.0 collective-permute-done.6.refs_5_
  79.4 1.3 collective-permute-done.8.refs_7_
  80.7 0.9 all-to-all-done.2.u_ref
  81.6 4.3 %slot_gradients.1 = (f32[2,416,256]{2,1,0:T(8,128)S(1)}, f32[2,416,256]{2,1,0:T(8,128)}) custom-call(s32[8]{0:T(128)S(1)} %compare_select_fusion.4.where_ref, f32[8]{0:T(128)S(1)} %get-tuple-element.18.place_ref, bf16[32,40,128]{2,1,0:T(8,128)(2,1)S(1)} %all-to-all-done.x_ref, bf16[32,24,128]{2,1,0:T(8,128)(2,1)S(1)} %all-to-all-done.2.u_ref, ...), custom_call_target="tpu_custom_call" | custom-call | tf_op jit(solution)/shard_map/slot_gradients/pallas_call | solution.py:397
  86.0 1.9 %collective-permute-start.9 = (f32[2,416,256]{2,1,0:T(8,128)}, f32[2,416,256]{2,1,0:T(8,128)S(1)}, u32[]{:S(2)}, u32[]{:S(2)}) collective-permute-start(f32[2,416,256]{2,1,0:T(8,128)} %get-tuple-element.21), channel_id=1, source_target_pairs={{0,4},{4,0},{8,12},{12,8},{1,5},{5,1},{9,13},{13,9},{2,6},{6,2},{1... | collective-permute-start | bytes 2555912 | tf_op jit(solution)/shard_map/ppermute | solution.py:304
  87.9 1.3 broadcast_select_fusion
  89.2 0.1 constant_dynamic-slice_fusion
  89.3 6.1 %collective-permute-start.13 = (bf16[1024,128]{1,0:T(8,128)(2,1)S(1)}, bf16[1024,128]{1,0:T(8,128)(2,1)S(1)}, u32[]{:S(2)}, u32[]{:S(2)}) collective-permute-start(bf16[1024,128]{1,0:T(8,128)(2,1)S(1)} %get-tuple-element.34), channel_id=1, source_target_pairs={{0,1},{1,2},{2,3},{3,0},{4,5},{5,6},{6,7},{7,4},{8,9},{9,10},{10,1... | collective-permute-start | bytes 786440 | tf_op jit(solution)/shard_map/ppermute | solution.py:300
  95.4 6.1 %collective-permute-start.14 = (bf16[1024,128]{1,0:T(8,128)(2,1)S(1)}, bf16[1024,128]{1,0:T(8,128)(2,1)S(1)}, u32[]{:S(2)}, u32[]{:S(2)}) collective-permute-start(bf16[1024,128]{1,0:T(8,128)(2,1)S(1)} %get-tuple-element.33), channel_id=1, source_target_pairs={{0,3},{1,0},{2,1},{3,2},{4,7},{5,4},{6,5},{7,6},{8,11},{9,8},{10,9... | collective-permute-start | bytes 786440 | tf_op jit(solution)/shard_map/ppermute | solution.py:300
  101.6 6.0 %collective-permute-start.18 = (bf16[1024,128]{1,0:T(8,128)(2,1)S(1)}, bf16[1024,128]{1,0:T(8,128)(2,1)S(1)}, u32[]{:S(2)}, u32[]{:S(2)}) collective-permute-start(bf16[1024,128]{1,0:T(8,128)(2,1)S(1)} %get-tuple-element.32), channel_id=1, source_target_pairs={{0,2},{1,3},{2,0},{3,1},{4,6},{5,7},{6,4},{7,5},{8,10},{9,11},{10,... | collective-permute-start | bytes 786440 | tf_op jit(solution)/shard_map/ppermute | solution.py:300
  107.6 2.7 %collective-permute-done.13.refs_5_ = bf16[1024,128]{1,0:T(8,128)(2,1)S(1)} collective-permute-done((bf16[1024,128]{1,0:T(8,128)(2,1)S(1)}, bf16[1024,128]{1,0:T(8,128)(2,1)S(1)}, u32[]{:S(2)}, u32[]{:S(2)}) %collective-permute-start.13) | collective-permute-done | bytes 262176 | tf_op jit(solution)/shard_map/ppermute | solution.py:300
  110.2 1.9 %collective-permute-start.15 = (bf16[1024,128]{1,0:T(8,128)(2,1)S(1)}, bf16[1024,128]{1,0:T(8,128)(2,1)S(1)}, u32[]{:S(2)}, u32[]{:S(2)}) collective-permute-start(bf16[1024,128]{1,0:T(8,128)(2,1)S(1)} %collective-permute-done.13.refs_5_), channel_id=1, source_target_pairs={{0,4},{4,0},{8,12},{12,8},{1,5},{5,1},{9,13},{13,9},{2,6},{6,2},{1... | collective-permute-start | bytes 786440 | tf_op jit(solution)/shard_map/ppermute | solution.py:304
  112.1 0.0 collective-permute-done.9.other_ref
  112.2 0.1 core_sums.1
  112.3 5.6 %collective-permute-start.10 = (bf16[448,256]{1,0:T(8,128)(2,1)S(1)}, bf16[448,256]{1,0:T(8,128)(2,1)S(1)}, u32[]{:S(2)}, u32[]{:S(2)}) collective-permute-start(bf16[448,256]{1,0:T(8,128)(2,1)S(1)} %get-tuple-element.23), channel_id=1, source_target_pairs={{0,8},{4,12},{8,0},{12,4},{1,9},{5,13},{9,1},{13,5},{2,10},{6,14},... | collective-permute-start | bytes 688136 | tf_op jit(solution)/shard_map/ppermute | solution.py:304
  117.8 0.0 collective-permute-done.14.refs_6_
  117.8 2.1 %collective-permute-start.16 = (bf16[1024,128]{1,0:T(8,128)(2,1)S(1)}, bf16[1024,128]{1,0:T(8,128)(2,1)S(1)}, u32[]{:S(2)}, u32[]{:S(2)}) collective-permute-start(bf16[1024,128]{1,0:T(8,128)(2,1)S(1)} %collective-permute-done.14.refs_6_), channel_id=1, source_target_pairs={{0,4},{4,0},{8,12},{12,8},{1,5},{5,1},{9,13},{13,9},{2,6},{6,2},{1... | collective-permute-start | bytes 786440 | tf_op jit(solution)/shard_map/ppermute | solution.py:304
  120.0 8.9 %collective-permute-done.18.refs_5_ = bf16[1024,128]{1,0:T(8,128)(2,1)S(1)} collective-permute-done((bf16[1024,128]{1,0:T(8,128)(2,1)S(1)}, bf16[1024,128]{1,0:T(8,128)(2,1)S(1)}, u32[]{:S(2)}, u32[]{:S(2)}) %collective-permute-start.18) | collective-permute-done | bytes 262176 | tf_op jit(solution)/shard_map/ppermute | solution.py:300
  128.9 1.9 %collective-permute-start.19 = (bf16[1024,128]{1,0:T(8,128)(2,1)S(1)}, bf16[1024,128]{1,0:T(8,128)(2,1)S(1)}, u32[]{:S(2)}, u32[]{:S(2)}) collective-permute-start(bf16[1024,128]{1,0:T(8,128)(2,1)S(1)} %collective-permute-done.18.refs_5_), channel_id=1, source_target_pairs={{0,4},{4,0},{8,12},{12,8},{1,5},{5,1},{9,13},{13,9},{2,6},{6,2},{1... | collective-permute-start | bytes 786440 | tf_op jit(solution)/shard_map/ppermute | solution.py:304
  130.8 0.0 collective-permute-done.10.other_ref
  130.8 1.3 slot_sums.1
  132.2 6.2 %collective-permute-start.11 = (bf16[416,256]{1,0:T(8,128)(2,1)S(1)}, bf16[416,256]{1,0:T(8,128)(2,1)S(1)}, u32[]{:S(2)}, u32[]{:S(2)}) collective-permute-start(bf16[416,256]{1,0:T(8,128)(2,1)S(1)} %get-tuple-element.26.refs_0_), channel_id=1, source_target_pairs={{0,1},{1,2},{2,3},{3,0},{4,5},{5,6},{6,7},{7,4},{8,9},{9,10},{10,1... | collective-permute-start | bytes 638984 | tf_op jit(solution)/shard_map/ppermute | solution.py:300
  138.4 1.9 %collective-permute-start.12 = (bf16[416,256]{1,0:T(8,128)(2,1)S(1)}, bf16[416,256]{1,0:T(8,128)(2,1)S(1)}, u32[]{:S(2)}, u32[]{:S(2)}) collective-permute-start(bf16[416,256]{1,0:T(8,128)(2,1)S(1)} %get-tuple-element.27), channel_id=1, source_target_pairs={{0,3},{1,0},{2,1},{3,2},{4,7},{5,4},{6,5},{7,6},{8,11},{9,8},{10,9... | collective-permute-start | bytes 638984 | tf_op jit(solution)/shard_map/ppermute | solution.py:300
  140.4 0.0 collective-permute-done.15.refs_7_
  140.4 10.0 %collective-permute-start.17 = (bf16[416,256]{1,0:T(8,128)(2,1)S(1)}, bf16[416,256]{1,0:T(8,128)(2,1)S(1)}, u32[]{:S(2)}, u32[]{:S(2)}) collective-permute-start(bf16[416,256]{1,0:T(8,128)(2,1)S(1)} %get-tuple-element.29), channel_id=1, source_target_pairs={{0,2},{1,3},{2,0},{3,1},{4,6},{5,7},{6,4},{7,5},{8,10},{9,11},{10,... | collective-permute-start | bytes 638984 | tf_op jit(solution)/shard_map/ppermute | solution.py:300
  150.4 1.1 constant_dynamic-slice_fusion.3
  151.5 0.0 collective-permute-done.16.refs_8_
  151.5 0.0 collective-permute-done.11.refs_3_.refs_2_
  151.5 4.1 %collective-permute-done.12.refs_4_.refs_3_ = bf16[416,256]{1,0:T(8,128)(2,1)S(1)} collective-permute-done((bf16[416,256]{1,0:T(8,128)(2,1)S(1)}, bf16[416,256]{1,0:T(8,128)(2,1)S(1)}, u32[]{:S(2)}, u32[]{:S(2)}) %collective-permute-start.12) | collective-permute-done | bytes 213024 | tf_op jit(solution)/shard_map/ppermute | solution.py:300
  155.6 1.3 input_first.1.refs_0_
  156.9 0.0 collective-permute-done.19.refs_6_
  157.0 8.8 %collective-permute-done.17.refs_4_ = bf16[416,256]{1,0:T(8,128)(2,1)S(1)} collective-permute-done((bf16[416,256]{1,0:T(8,128)(2,1)S(1)}, bf16[416,256]{1,0:T(8,128)(2,1)S(1)}, u32[]{:S(2)}, u32[]{:S(2)}) %collective-permute-start.17) | collective-permute-done | bytes 213024 | tf_op jit(solution)/shard_map/ppermute | solution.py:300
  165.7 1.8 %input_gradient.1 = (bf16[384,1024]{1,0:T(8,128)(2,1)}, bf16[32,32]{1,0:T(8,128)(2,1)}) custom-call(s32[8]{0:T(128)S(1)} %compare_select_fusion.4.where_ref, f32[384,1024]{1,0:T(8,128)S(1)} %input_first.1.refs_0_, f32[32,128]{1,0:T(8,128)S(1)} %get-tuple-element.28.refs_1_, bf16[416,256]{1,0:T(8,128)(2,1)S(1)} %collective-permute-done.11.refs_3_.refs_2_, ...), custom_call_target="tpu_custom_call" | custom-call | tf_op jit(solution)/shard_map/input_gradient/pallas_call | solution.py:440
  (1 shorter events, 0.0 us)
Async XLA Ops:
  0.6 11.5 %collective-permute-start = (s32[1]{0:T(128)}, s32[1]{0:T(128)}, u32[]{:S(2)}, u32[]{:S(2)}) collective-permute-start(s32[1]{0:T(128)} %param.13), channel_id=1, source_target_pairs={{0,4},{4,0},{8,12},{12,8},{1,5},{5,1},{9,13},{13,9},{2,6},{6,2},{1... | collective-permute-start | bytes 20 | tf_op jit(solution)/shard_map/ppermute | solution.py:304
  2.6 9.6 %collective-permute-start.1 = (s32[1]{0:T(128)}, s32[1]{0:T(128)}, u32[]{:S(2)}, u32[]{:S(2)}) collective-permute-start(s32[1]{0:T(128)} %param.13), channel_id=1, source_target_pairs={{0,8},{4,12},{8,0},{12,4},{1,9},{5,13},{9,1},{13,5},{2,10},{6,14},... | collective-permute-start | bytes 20 | tf_op jit(solution)/shard_map/ppermute | solution.py:304
  9.5 5.0 %collective-permute-start.2 = (s32[1]{0:T(128)}, s32[1]{0:T(128)}, u32[]{:S(2)}, u32[]{:S(2)}) collective-permute-start(s32[1]{0:T(128)} %param.13), channel_id=1, source_target_pairs={{0,12},{4,8},{8,4},{12,0},{1,13},{5,9},{9,5},{13,1},{2,14},{6,10},... | collective-permute-start | bytes 20 | tf_op jit(solution)/shard_map/ppermute | solution.py:304
  17.8 19.3 %all-to-all-start = ((bf16[32,40,128]{2,1,0:T(8,128)(2,1)}), bf16[32,40,128]{2,1,0:T(8,128)(2,1)S(1)}, u32[]{:S(2)}, u32[]{:S(2)}) async-start(bf16[32,40,128]{2,1,0:T(8,128)(2,1)} %row_pack.1), calls=%async_computation | async-start | bytes 655360 | tf_op jit(solution)/shard_map/all_to_all | solution.py:295
  23.0 47.6 %copy-start = (bf16[32,2048]{1,0:T(8,128)(2,1)S(1)}, bf16[32,2048]{1,0:T(8,128)(2,1)}, u32[]{:S(2)}) copy-start(bf16[32,2048]{1,0:T(8,128)(2,1)} %refs_4_.3) | copy-start | bytes 393220
  24.9 8.9 %collective-permute-start.4 = (bf16[384,256]{1,0:T(8,128)(2,1)S(1)}, bf16[384,256]{1,0:T(8,128)(2,1)S(1)}, u32[]{:S(2)}, u32[]{:S(2)}) collective-permute-start(bf16[384,256]{1,0:T(8,128)(2,1)S(1)} %constant_dynamic-update-slice_fusion.refs_0_), channel_id=1, source_target_pairs={{0,8},{4,12},{8,0},{12,4},{1,9},{5,13},{9,1},{13,5},{2,10},{6,14},... | collective-permute-start | bytes 589832 | tf_op jit(solution)/shard_map/ppermute | solution.py:304
  28.6 7.7 %collective-permute-start.3 = (bf16[384,256]{1,0:T(8,128)(2,1)S(1)}, bf16[384,256]{1,0:T(8,128)(2,1)S(1)}, u32[]{:S(2)}, u32[]{:S(2)}) collective-permute-start(bf16[384,256]{1,0:T(8,128)(2,1)S(1)} %constant_dynamic-update-slice_fusion.refs_0_), channel_id=1, source_target_pairs={{0,4},{4,0},{8,12},{12,8},{1,5},{5,1},{9,13},{13,9},{2,6},{6,2},{1... | collective-permute-start | bytes 589832 | tf_op jit(solution)/shard_map/ppermute | solution.py:304
  33.7 3.3 %collective-permute-start.5 = (bf16[384,256]{1,0:T(8,128)(2,1)S(1)}, bf16[384,256]{1,0:T(8,128)(2,1)S(1)}, u32[]{:S(2)}, u32[]{:S(2)}) collective-permute-start(bf16[384,256]{1,0:T(8,128)(2,1)S(1)} %collective-permute-done.4.refs_2_), channel_id=1, source_target_pairs={{0,4},{4,0},{8,12},{12,8},{1,5},{5,1},{9,13},{13,9},{2,6},{6,2},{1... | collective-permute-start | bytes 589832 | tf_op jit(solution)/shard_map/ppermute | solution.py:304
  65.6 16.0 %all-to-all-start.2 = ((bf16[32,24,128]{2,1,0:T(8,128)(2,1)}), bf16[32,24,128]{2,1,0:T(8,128)(2,1)S(1)}, u32[]{:S(2)}, u32[]{:S(2)}) async-start(bf16[32,24,128]{2,1,0:T(8,128)(2,1)} %row_merge.1), calls=%async_computation.2 | async-start | bytes 393216 | tf_op jit(solution)/shard_map/all_to_all | solution.py:295
  70.6 6.9 %collective-permute-start.7 = (bf16[32,2048]{1,0:T(8,128)(2,1)S(1)}, bf16[32,2048]{1,0:T(8,128)(2,1)S(1)}, u32[]{:S(2)}, u32[]{:S(2)}) collective-permute-start(bf16[32,2048]{1,0:T(8,128)(2,1)S(1)} %copy-done), channel_id=1, source_target_pairs={{0,8},{4,12},{8,0},{12,4},{1,9},{5,13},{9,1},{13,5},{2,10},{6,14},... | collective-permute-start | bytes 393224 | tf_op jit(solution)/shard_map/ppermute | solution.py:304
  74.3 5.1 %collective-permute-start.6 = (bf16[32,2048]{1,0:T(8,128)(2,1)S(1)}, bf16[32,2048]{1,0:T(8,128)(2,1)S(1)}, u32[]{:S(2)}, u32[]{:S(2)}) collective-permute-start(bf16[32,2048]{1,0:T(8,128)(2,1)S(1)} %copy-done), channel_id=1, source_target_pairs={{0,4},{4,0},{8,12},{12,8},{1,5},{5,1},{9,13},{13,9},{2,6},{6,2},{1... | collective-permute-start | bytes 393224 | tf_op jit(solution)/shard_map/ppermute | solution.py:304
  77.5 3.2 %collective-permute-start.8 = (bf16[32,2048]{1,0:T(8,128)(2,1)S(1)}, bf16[32,2048]{1,0:T(8,128)(2,1)S(1)}, u32[]{:S(2)}, u32[]{:S(2)}) collective-permute-start(bf16[32,2048]{1,0:T(8,128)(2,1)S(1)} %collective-permute-done.7.refs_6_), channel_id=1, source_target_pairs={{0,4},{4,0},{8,12},{12,8},{1,5},{5,1},{9,13},{13,9},{2,6},{6,2},{1... | collective-permute-start | bytes 393224 | tf_op jit(solution)/shard_map/ppermute | solution.py:304
  86.0 26.2 %collective-permute-start.9 = (f32[2,416,256]{2,1,0:T(8,128)}, f32[2,416,256]{2,1,0:T(8,128)S(1)}, u32[]{:S(2)}, u32[]{:S(2)}) collective-permute-start(f32[2,416,256]{2,1,0:T(8,128)} %get-tuple-element.21), channel_id=1, source_target_pairs={{0,4},{4,0},{8,12},{12,8},{1,5},{5,1},{9,13},{13,9},{2,6},{6,2},{1... | collective-permute-start | bytes 2555912 | tf_op jit(solution)/shard_map/ppermute | solution.py:304
  89.3 20.9 %collective-permute-start.13 = (bf16[1024,128]{1,0:T(8,128)(2,1)S(1)}, bf16[1024,128]{1,0:T(8,128)(2,1)S(1)}, u32[]{:S(2)}, u32[]{:S(2)}) collective-permute-start(bf16[1024,128]{1,0:T(8,128)(2,1)S(1)} %get-tuple-element.34), channel_id=1, source_target_pairs={{0,1},{1,2},{2,3},{3,0},{4,5},{5,6},{6,7},{7,4},{8,9},{9,10},{10,1... | collective-permute-start | bytes 786440 | tf_op jit(solution)/shard_map/ppermute | solution.py:300
  95.4 22.4 %collective-permute-start.14 = (bf16[1024,128]{1,0:T(8,128)(2,1)S(1)}, bf16[1024,128]{1,0:T(8,128)(2,1)S(1)}, u32[]{:S(2)}, u32[]{:S(2)}) collective-permute-start(bf16[1024,128]{1,0:T(8,128)(2,1)S(1)} %get-tuple-element.33), channel_id=1, source_target_pairs={{0,3},{1,0},{2,1},{3,2},{4,7},{5,4},{6,5},{7,6},{8,11},{9,8},{10,9... | collective-permute-start | bytes 786440 | tf_op jit(solution)/shard_map/ppermute | solution.py:300
  101.6 27.4 %collective-permute-start.18 = (bf16[1024,128]{1,0:T(8,128)(2,1)S(1)}, bf16[1024,128]{1,0:T(8,128)(2,1)S(1)}, u32[]{:S(2)}, u32[]{:S(2)}) collective-permute-start(bf16[1024,128]{1,0:T(8,128)(2,1)S(1)} %get-tuple-element.32), channel_id=1, source_target_pairs={{0,2},{1,3},{2,0},{3,1},{4,6},{5,7},{6,4},{7,5},{8,10},{9,11},{10,... | collective-permute-start | bytes 786440 | tf_op jit(solution)/shard_map/ppermute | solution.py:300
  110.2 30.1 %collective-permute-start.15 = (bf16[1024,128]{1,0:T(8,128)(2,1)S(1)}, bf16[1024,128]{1,0:T(8,128)(2,1)S(1)}, u32[]{:S(2)}, u32[]{:S(2)}) collective-permute-start(bf16[1024,128]{1,0:T(8,128)(2,1)S(1)} %collective-permute-done.13.refs_5_), channel_id=1, source_target_pairs={{0,4},{4,0},{8,12},{12,8},{1,5},{5,1},{9,13},{13,9},{2,6},{6,2},{1... | collective-permute-start | bytes 786440 | tf_op jit(solution)/shard_map/ppermute | solution.py:304
  112.3 18.6 %collective-permute-start.10 = (bf16[448,256]{1,0:T(8,128)(2,1)S(1)}, bf16[448,256]{1,0:T(8,128)(2,1)S(1)}, u32[]{:S(2)}, u32[]{:S(2)}) collective-permute-start(bf16[448,256]{1,0:T(8,128)(2,1)S(1)} %get-tuple-element.23), channel_id=1, source_target_pairs={{0,8},{4,12},{8,0},{12,4},{1,9},{5,13},{9,1},{13,5},{2,10},{6,14},... | collective-permute-start | bytes 688136 | tf_op jit(solution)/shard_map/ppermute | solution.py:304
  117.8 33.6 %collective-permute-start.16 = (bf16[1024,128]{1,0:T(8,128)(2,1)S(1)}, bf16[1024,128]{1,0:T(8,128)(2,1)S(1)}, u32[]{:S(2)}, u32[]{:S(2)}) collective-permute-start(bf16[1024,128]{1,0:T(8,128)(2,1)S(1)} %collective-permute-done.14.refs_6_), channel_id=1, source_target_pairs={{0,4},{4,0},{8,12},{12,8},{1,5},{5,1},{9,13},{13,9},{2,6},{6,2},{1... | collective-permute-start | bytes 786440 | tf_op jit(solution)/shard_map/ppermute | solution.py:304
  128.9 28.0 %collective-permute-start.19 = (bf16[1024,128]{1,0:T(8,128)(2,1)S(1)}, bf16[1024,128]{1,0:T(8,128)(2,1)S(1)}, u32[]{:S(2)}, u32[]{:S(2)}) collective-permute-start(bf16[1024,128]{1,0:T(8,128)(2,1)S(1)} %collective-permute-done.18.refs_5_), channel_id=1, source_target_pairs={{0,4},{4,0},{8,12},{12,8},{1,5},{5,1},{9,13},{13,9},{2,6},{6,2},{1... | collective-permute-start | bytes 786440 | tf_op jit(solution)/shard_map/ppermute | solution.py:304
  132.2 19.3 %collective-permute-start.11 = (bf16[416,256]{1,0:T(8,128)(2,1)S(1)}, bf16[416,256]{1,0:T(8,128)(2,1)S(1)}, u32[]{:S(2)}, u32[]{:S(2)}) collective-permute-start(bf16[416,256]{1,0:T(8,128)(2,1)S(1)} %get-tuple-element.26.refs_0_), channel_id=1, source_target_pairs={{0,1},{1,2},{2,3},{3,0},{4,5},{5,6},{6,7},{7,4},{8,9},{9,10},{10,1... | collective-permute-start | bytes 638984 | tf_op jit(solution)/shard_map/ppermute | solution.py:300
  138.4 17.2 %collective-permute-start.12 = (bf16[416,256]{1,0:T(8,128)(2,1)S(1)}, bf16[416,256]{1,0:T(8,128)(2,1)S(1)}, u32[]{:S(2)}, u32[]{:S(2)}) collective-permute-start(bf16[416,256]{1,0:T(8,128)(2,1)S(1)} %get-tuple-element.27), channel_id=1, source_target_pairs={{0,3},{1,0},{2,1},{3,2},{4,7},{5,4},{6,5},{7,6},{8,11},{9,8},{10,9... | collective-permute-start | bytes 638984 | tf_op jit(solution)/shard_map/ppermute | solution.py:300
  140.4 25.4 %collective-permute-start.17 = (bf16[416,256]{1,0:T(8,128)(2,1)S(1)}, bf16[416,256]{1,0:T(8,128)(2,1)S(1)}, u32[]{:S(2)}, u32[]{:S(2)}) collective-permute-start(bf16[416,256]{1,0:T(8,128)(2,1)S(1)} %get-tuple-element.29), channel_id=1, source_target_pairs={{0,2},{1,3},{2,0},{3,1},{4,6},{5,7},{6,4},{7,5},{8,10},{9,11},{10,... | collective-permute-start | bytes 638984 | tf_op jit(solution)/shard_map/ppermute | solution.py:300

commit v7 on v5

--- a/solution.py
+++ b/solution.py
@@ -195,68 +195,65 @@
         ref[half:, :features] = both[:, first * features : (first + 1) * features]
 
 
-def finish_kernel(groups, features, where_ref, own_ref, other_ref, k_ref, v_ref, span_ref, *out_refs):
+def folded(value):
+    high = value.astype(BF16).astype(F32)
+    wide = high + pltpu.roll((value - high).astype(BF16).astype(F32), 32, 1)
+    count = value.shape[0] // 4
+    a, b, c, d = [wide[k * count : (k + 1) * count] for k in range(4)]
+    both = [a + pltpu.roll(b, 64, 1), c + pltpu.roll(d, 64, 1)]
+    return jnp.concatenate(both, axis=1).astype(BF16)
+
+
+def unfolded(block):
+    wide = block.astype(F32)
+    left, right = wide[:, :128], wide[:, 128:]
+    rows = [left, pltpu.roll(left, 64, 1), right, pltpu.roll(right, 64, 1)]
+    rows = jnp.concatenate(rows, axis=0)
+    return rows + pltpu.roll(rows, 96, 1)
+
+
+def finish_kernel(groups, features, where_ref, own_ref, other_ref, k_ref, v_ref, send_ref):
     half = k_ref.shape[0]
-    per = span_ref.shape[0] // 2
+    per = (own_ref.shape[0] - half) // groups
     sums = (own_ref[:half, :] + other_ref[:half, :]).astype(BF16)
     k_ref[...] = sums[:, :HEAD_WIDTH]
     v_ref[...] = sums[:, HEAD_WIDTH:]
     is_first = where_ref[1] == 0
     lane = lax.broadcasted_iota(jnp.int32, (2 * per, 128), 1)
-
-    def block_rows(target):
-        start = half + per * target
-        if per % 8 == 0:
-            start = pl.multiple_of(start, 8)
-        part = pl.ds(start, per)
+    for target in range(groups):
+        part = slice(half + per * target, half + per * (target + 1))
         mine, theirs = own_ref[part, :128], other_ref[part, :128]
         even = jnp.where(is_first, mine, theirs)
         odd = jnp.where(is_first, theirs, mine)
-        return jnp.where(lane < features, jnp.concatenate([even, odd], axis=0), 0.0)
-
+        lines = jnp.where(lane < features, jnp.concatenate([even, odd], axis=0), 0.0)
+        send_ref[target, :half, :] = sums
+        send_ref[target, half:, :] = folded(lines)
+
+
+def input_kernel(groups, sharers, where_ref, arrived_ref, own_k_ref, own_v_ref, *refs):
+    here, there, refs = refs[:sharers], refs[sharers : 2 * sharers], refs[2 * sharers :]
+    out_ref, block_ref, turn_ref = refs
+    half = out_ref.shape[0]
+    is_first = where_ref[1] == 0
     mine = where_ref[4]
-    span_ref[...] = block_rows(mine)
-    for k, ref in enumerate(out_refs, 1):
-        high, middle, low = three_parts(block_rows(lax.rem(mine + k, groups)))
-        wide = high + pltpu.roll(middle, features, 1) + pltpu.roll(low, 2 * features, 1)
-        ref[:half, :] = sums
-        ref[half:, :] = jnp.concatenate([wide, jnp.zeros_like(wide)], axis=1).astype(BF16)
-
-
-def input_kernel(others, sharers, first, more, where_ref, *refs):
-    is_first = where_ref[1] == 0
-    if first:
-        own_ref, own_k_ref, own_v_ref = refs[:3]
-    else:
-        total_ref, span_ref, *spans = refs[: 2 + more]
-    refs = refs[3:] if first else refs[2 + more :]
-    arrived, refs = refs[: len(others)], refs[len(others) :]
-    here, there, refs = refs[:sharers], refs[sharers : 2 * sharers], refs[2 * sharers :]
-    out_ref = refs[0]
-    half = out_ref.shape[0]
-    left = [own_ref[:half, :]] if first else []
-    for ref in arrived:
-        keys, values = ref[:half, :HEAD_WIDTH], ref[:half, HEAD_WIDTH:]
+    left = [arrived_ref[mine, :half, :]]
+    span = unfolded(arrived_ref[0, half:, :])
+    for k in range(1, groups):
+        both = arrived_ref[lax.rem(mine - k + groups, groups), :half, :]
+        keys, values = both[:, :HEAD_WIDTH], both[:, HEAD_WIDTH:]
         left += [jnp.where(is_first, keys, values), jnp.where(is_first, values, keys)]
+        span += unfolded(arrived_ref[k, half:, :])
     left = jnp.concatenate(left, axis=1)
     share = out_ref.shape[1] // sharers
     for k, (near_ref, far_ref) in enumerate(zip(here, there)):
         start = lax.rem(where_ref[5] - k + sharers, sharers) * share
         part = pl.ds(pl.multiple_of(start, share), share)
-        right = [own_k_ref[part, :], own_v_ref[part, :]] if first else []
-        for other in others:
-            lines = slice((other - 1) * share, other * share)
+        right = [own_k_ref[part, :], own_v_ref[part, :]]
+        for other in range(groups - 1):
+            lines = slice(other * share, (other + 1) * share)
             right += [near_ref[lines, :], far_ref[lines, :]]
-        term = rows_dot(left, jnp.concatenate(right, axis=1))
-        out_ref[:, part] = term if first else (total_ref[:, part] + term).astype(BF16)
-    if first:
-        return
-    block_ref, turn_ref = refs[1:3]
+        out_ref[:, part] = rows_dot(left, jnp.concatenate(right, axis=1)).astype(BF16)
     rows, features = block_ref.shape
-    span = span_ref[...]
-    for ref in (*spans, *arrived):
-        wide = ref[half:, :128].astype(F32)
-        span += wide + pltpu.roll(wide, 128 - features, 1) + pltpu.roll(wide, 128 - 2 * features, 1)
     turn_ref[pl.ds(0, rows // 2, stride=2), :] = span[: rows // 2]
     turn_ref[pl.ds(1, rows // 2, stride=2), :] = span[rows // 2 :]
     block_ref[...] = turn_ref[:, :features].astype(BF16)
@@ -365,44 +362,32 @@
     )(where, place, x, u, keys, values, both_query)
     other_sums = shifted(other_part, CORE, 1)
     per = rows // groups
-    saved_key_gradient, saved_value_gradient, own_span, *leaving = pl.pallas_call(
+    saved_key_gradient, saved_value_gradient, leaving = pl.pallas_call(
         functools.partial(finish_kernel, groups, width),
         out_shape=(
             jax.ShapeDtypeStruct((block, HEAD_WIDTH), BF16),
             jax.ShapeDtypeStruct((block, HEAD_WIDTH), BF16),
-            jax.ShapeDtypeStruct((2 * per, 128), F32),
-        )
-        + (jax.ShapeDtypeStruct((block + 2 * per, 2 * HEAD_WIDTH), BF16),) * (groups - 1),
+            jax.ShapeDtypeStruct((groups, block + per // 2, 2 * HEAD_WIDTH), BF16),
+        ),
         in_specs=[SMEM, VMEM, VMEM],
-        out_specs=(VMEM,) * (2 + groups),
+        out_specs=(VMEM, VMEM, VMEM),
         name="slot_sums",
         compiler_params=PARAMS,
     )(where, own_part, other_sums)
 
-    pieces = {}
-    for k, piece in enumerate(leaving, 1):
-        pieces[k] = shifted(piece, "head", k)
-    early = [k for k in pieces if k != 2]
-    total = pl.pallas_call(
-        functools.partial(input_kernel, early, sharers, True, 0),
-        out_shape=jax.ShapeDtypeStruct((block, features), F32),
-        in_specs=[SMEM] + [VMEM] * (3 + len(early) + 2 * sharers),
-        out_specs=VMEM,
-        name="input_first",
-        compiler_params=PARAMS,
-    )(where, leaving[0], *own_weights, *[pieces[k] for k in early], *near, *there)
+    pieces = exchanged(leaving, "head")
     cached_input_gradient, grad_span_input = pl.pallas_call(
-        functools.partial(input_kernel, [2], sharers, False, len(early)),
+        functools.partial(input_kernel, groups, sharers),
         out_shape=(
             jax.ShapeDtypeStruct((block, features), BF16),
             jax.ShapeDtypeStruct((2 * per, width), BF16),
         ),
-        in_specs=[SMEM] + [VMEM] * (3 + len(early) + 2 * sharers),
+        in_specs=[SMEM] + [VMEM] * (3 + 2 * sharers),
         out_specs=(VMEM, VMEM),
         scratch_shapes=[pltpu.VMEM((2 * per, 128), F32)],
         name="input_gradient",
         compiler_params=PARAMS,
-    )(where, total, own_span, *[pieces[k] for k in early], pieces[2], *near, *there)
+    )(where, pieces, *own_weights, *near, *there)
     return (saved_key_gradient, saved_value_gradient, cached_input_gradient, grad_span_input)
 
 

time: 156 us -> 162 us (1.038)
  blocking collectives: 0 us -> 25.5 us
  starting transfers between devices: 91 us -> 78.9 us
  waiting for transfers between devices: 42 us -> 36.2 us
    all_to_all x0 -> x1, blocking collectives: none -> 25.5 us  [exchanged(): return lax.all_to_all(value, axes, split_axis=0, concat_axis=0, tiled=True)]
    ppermute x17 -> x14, starting transfers between devices: 68.8 us -> 55.1 us  [shifted(): lax.ppermute(value, axis, [(k, (k + by) % count) for k in range(count)])]
    all_to_all x3, waiting for transfers between devices: 33.1 us -> 23.1 us  [exchanged(): return lax.all_to_all(value, axes, split_axis=0, concat_axis=0, tiled=True)]
    ppermute x17 -> x14, waiting for transfers between devices: 8.85 us -> 13 us  [shifted(): lax.ppermute(value, axis, [(k, (k + by) % count) for k in range(count)])]
    all_to_all x3, starting transfers between devices: 22.2 us -> 23.8 us  [exchanged(): return lax.all_to_all(value, axes, split_axis=0, concat_axis=0, tiled=True)]
  transfers between devices with their start and end apart: 20 -> 17, of which waited for: 7 -> 9; matrix products, arithmetic and copies ran while one was open for 2% -> 2% of each run, Pallas kernels for 4% -> 0%
where the time goes in v7:
time: 162 us; the launch traced here: 161 us
  starting transfers between devices  78.9 us (49%)
  waiting for transfers between devices  36.2 us (22%)
  blocking collectives  25.5 us (16%)
  Pallas kernels  14.7 us (9%)
  between operations  2.21 us (1%)
  local copies, waits for them, and re-layouts  2.05 us (1%)
    ppermute x14, starting transfers between devices, shifted(): lax.ppermute(value, axis, [(k, (k + by) % count) for k in range(count)])  55.1 us
    all_to_all x1, blocking collectives, exchanged(): return lax.all_to_all(value, axes, split_axis=0, concat_axis=0, tiled=True)  25.5 us
    all_to_all x3, starting transfers between devices, exchanged(): return lax.all_to_all(value, axes, split_axis=0, concat_axis=0, tiled=True)  23.8 us
    all_to_all x3, waiting for transfers between devices, exchanged(): return lax.all_to_all(value, axes, split_axis=0, concat_axis=0, tiled=True)  23.1 us
    ppermute x14, waiting for transfers between devices, shifted(): lax.ppermute(value, axis, [(k, (k + by) % count) for k in range(count)])  13 us
    pallas_call x1, Pallas kernels, local(): pl.pallas_call(functools.partial(first_kernel, heads, group), out_shape=(...  3.68 us
  transfers between devices with their start and end apart: 17, of which 9 were waited for; matrix products, arithmetic and copies ran while one was open for 2% of the time, Pallas kernels for 0%

profile of v7, /device:TPU:1, one launch (start us, length us, event | category | flops | bytes accessed | tf_op | source)
XLA Modules:
  0.0 160.9 jit_solution(3555907395882087869)
XLA Ops:
  0.6 8.7 %collective-permute-start = (s32[1]{0:T(128)}, s32[1]{0:T(128)}, u32[]{:S(2)}, u32[]{:S(2)}) collective-permute-start(s32[1]{0:T(128)} %param.13), channel_id=1, source_target_pairs={{0,4},{4,0},{1,5},{5,1},{2,6},{6,2},{3,7},{7,3},{8,12},{12,8},{9,1... | collective-permute-start | bytes 20 | tf_op jit(solution)/shard_map/ppermute | solution.py:268
  10.0 0.3 collective-permute-done.other_ref
  10.3 2.3 %row_pack.1 = bf16[64,40,128]{2,1,0:T(8,128)(2,1)} custom-call(s32[1]{0:T(128)S(6)} %copy.15.own_ref, s32[1]{0:T(128)} %collective-permute-done.other_ref, bf16[1,2048]{1,0:T(2,128)(2,1)} %q_ref.1, bf16[1,2048]{1,0:T(2,128)(2,1)} %g_ref.1), custom_call_target="tpu_custom_call" | custom-call | tf_op jit(solution)/shard_map/row_pack/pallas_call | solution.py:293
  12.6 0.0 copy-start.1
  12.6 0.0 copy-start.2
  12.6 6.9 %all-to-all-start = ((bf16[64,40,128]{2,1,0:T(8,128)(2,1)}), bf16[64,40,128]{2,1,0:T(8,128)(2,1)S(1)}, u32[]{:S(2)}, u32[]{:S(2)}) async-start(bf16[64,40,128]{2,1,0:T(8,128)(2,1)} %row_pack.1), calls=%async_computation | async-start | bytes 1310720 | tf_op jit(solution)/shard_map/all_to_all | solution.py:263
  19.5 0.0 copy-done.1
  19.5 0.0 copy-done.2
  19.6 2.5 %collective-permute-start.1 = (bf16[384,256]{1,0:T(8,128)(2,1)S(1)}, bf16[384,256]{1,0:T(8,128)(2,1)S(1)}, u32[]{:S(2)}, u32[]{:S(2)}) collective-permute-start(bf16[384,256]{1,0:T(8,128)(2,1)S(1)} %pad_maximum_fusion.1), channel_id=1, source_target_pairs={{0,4},{4,0},{1,5},{5,1},{2,6},{6,2},{3,7},{7,3},{8,12},{12,8},{9,1... | collective-permute-start | bytes 589832 | tf_op jit(solution)/shard_map/ppermute | solution.py:268
  22.7 0.4 collective-permute-done.1
  23.2 14.9 %all-to-all-done.x_ref = bf16[64,40,128]{2,1,0:T(8,128)(2,1)S(1)} async-done(((bf16[64,40,128]{2,1,0:T(8,128)(2,1)}), bf16[64,40,128]{2,1,0:T(8,128)(2,1)S(1)}, u32[]{:S(2)}, u32[]{:S(2)}) %all-to-all-start) | async-done | bytes 655392 | tf_op jit(solution)/shard_map/all_to_all | solution.py:263
  38.1 3.7 %row_partials.1 = (bf16[64,40,128]{2,1,0:T(8,128)(2,1)S(1)}, f32[4]{0:T(128)S(1)}) custom-call(s32[8]{0:T(128)S(1)} %compare_select_fusion.4.where_ref, bf16[64,40,128]{2,1,0:T(8,128)(2,1)S(1)} %all-to-all-done.x_ref, bf16[768,128]{1,0:T(8,128)(2,1)S(1)} %get-tuple-element.27.k_ref, bf16[768,128]{1,0:T(8,128)(2,1)S(1)} %get-tuple-element.28.v_ref), custom_call_target="tpu_custom_call" | custom-call | tf_op jit(solution)/shard_map/row_partials/pallas_call | solution.py:333
  41.8 25.5 %all_to_all.20.z_ref = bf16[64,40,128]{2,1,0:T(8,128)(2,1)S(1)} all-to-all(bf16[64,40,128]{2,1,0:T(8,128)(2,1)S(1)} %get-tuple-element.14), channel_id=1, replica_groups=mesh['seq_0'=4,'seq_1'=8,'seq_2'=2,'seq_3'=2,'head'=4] {'seq_0','seq_1',..., dimensions={0} | all-to-all | bytes 1310720 | tf_op jit(solution)/shard_map/all_to_all | solution.py:263
  67.3 1.5 row_merge.1
  68.9 0.0 copy-start.3
  68.9 7.8 %all-to-all-start.2 = ((bf16[64,24,128]{2,1,0:T(8,128)(2,1)}), bf16[64,24,128]{2,1,0:T(8,128)(2,1)S(1)}, u32[]{:S(2)}, u32[]{:S(2)}) async-start(bf16[64,24,128]{2,1,0:T(8,128)(2,1)} %row_merge.1), calls=%async_computation.2 | async-start | bytes 786432 | tf_op jit(solution)/shard_map/all_to_all | solution.py:263
  76.7 0.0 copy-done.3
  76.7 3.4 %collective-permute-start.2 = (bf16[32,2048]{1,0:T(8,128)(2,1)S(1)}, bf16[32,2048]{1,0:T(8,128)(2,1)S(1)}, u32[]{:S(2)}, u32[]{:S(2)}) collective-permute-start(bf16[32,2048]{1,0:T(8,128)(2,1)S(1)} %copy-done.3), channel_id=1, source_target_pairs={{0,4},{4,0},{1,5},{5,1},{2,6},{6,2},{3,7},{7,3},{8,12},{12,8},{9,1... | collective-permute-start | bytes 393224 | tf_op jit(solution)/shard_map/ppermute | solution.py:268
  80.2 1.0 collective-permute-done.2
  81.1 8.2 %all-to-all-done.2.u_ref = bf16[64,24,128]{2,1,0:T(8,128)(2,1)S(1)} async-done(((bf16[64,24,128]{2,1,0:T(8,128)(2,1)}), bf16[64,24,128]{2,1,0:T(8,128)(2,1)S(1)}, u32[]{:S(2)}, u32[]{:S(2)}) %all-to-all-start.2) | async-done | bytes 393248 | tf_op jit(solution)/shard_map/all_to_all | solution.py:263
  89.4 3.1 %slot_gradients.1 = (f32[448,256]{1,0:T(8,128)S(1)}, f32[448,256]{1,0:T(8,128)S(1)}) custom-call(s32[8]{0:T(128)S(1)} %compare_select_fusion.4.where_ref, f32[4]{0:T(128)S(1)} %get-tuple-element.13.place_ref, bf16[64,40,128]{2,1,0:T(8,128)(2,1)S(1)} %all-to-all-done.x_ref, bf16[64,24,128]{2,1,0:T(8,128)(2,1)S(1)} %all-to-all-done.2.u_ref, ...), custom_call_target="tpu_custom_call" | custom-call | tf_op jit(solution)/shard_map/slot_gradients/pallas_call | solution.py:355
  92.5 5.2 %collective-permute-start.3 = (f32[448,256]{1,0:T(8,128)S(1)}, f32[448,256]{1,0:T(8,128)S(1)}, u32[]{:S(2)}, u32[]{:S(2)}) collective-permute-start(f32[448,256]{1,0:T(8,128)S(1)} %get-tuple-element.16), channel_id=1, source_target_pairs={{0,4},{4,0},{1,5},{5,1},{2,6},{6,2},{3,7},{7,3},{8,12},{12,8},{9,1... | collective-permute-start | bytes 1376264 | tf_op jit(solution)/shard_map/ppermute | solution.py:268
  97.7 1.4 collective-permute-done.3.other_ref
  99.1 0.0 copy-start
  99.1 1.6 %slot_sums.1 = (bf16[384,128]{1,0:T(8,128)(2,1)}, bf16[384,128]{1,0:T(8,128)(2,1)}, bf16[4,392,256]{2,1,0:T(8,128)(2,1)}) custom-call(s32[8]{0:T(128)S(1)} %compare_select_fusion.4.where_ref, f32[448,256]{1,0:T(8,128)S(1)} %get-tuple-element.15.own_ref, f32[448,256]{1,0:T(8,128)S(1)} %collective-permute-done.3.other_ref), custom_call_target="tpu_custom_call" | custom-call | tf_op jit(solution)/shard_map/slot_sums/pallas_call | solution.py:365
  100.8 9.1 %all-to-all-start.3 = ((bf16[4,392,256]{2,1,0:T(8,128)(2,1)}), bf16[4,392,256]{2,1,0:T(8,128)(2,1)S(1)}, u32[]{:S(2)}, u32[]{:S(2)}) async-start(bf16[4,392,256]{2,1,0:T(8,128)(2,1)} %get-tuple-element.19), calls=%async_computation.3 | async-start | bytes 1605632 | tf_op jit(solution)/shard_map/all_to_all | solution.py:263
  109.9 0.0 copy-done
  109.9 1.2 broadcast_select_fusion
  111.1 0.9 constant_dynamic-slice_fusion
  112.0 4.3 %collective-permute-start.4 = (bf16[256,128]{1,0:T(8,128)(2,1)S(1)}, bf16[256,128]{1,0:T(8,128)(2,1)S(1)}, u32[]{:S(2)}, u32[]{:S(2)}) collective-permute-start(bf16[256,128]{1,0:T(8,128)(2,1)S(1)} %get-tuple-element.24), channel_id=1, source_target_pairs={{0,1},{1,2},{2,3},{3,0},{4,5},{5,6},{6,7},{7,4},{8,9},{9,10},{10,1... | collective-permute-start | bytes 196616 | tf_op jit(solution)/shard_map/ppermute | solution.py:268
  116.3 3.1 %collective-permute-start.6 = (bf16[256,128]{1,0:T(8,128)(2,1)S(1)}, bf16[256,128]{1,0:T(8,128)(2,1)S(1)}, u32[]{:S(2)}, u32[]{:S(2)}) collective-permute-start(bf16[256,128]{1,0:T(8,128)(2,1)S(1)} %get-tuple-element.22), channel_id=1, source_target_pairs={{0,3},{1,0},{2,1},{3,2},{4,7},{5,4},{6,5},{7,6},{8,11},{9,8},{10,9... | collective-permute-start | bytes 196616 | tf_op jit(solution)/shard_map/ppermute | solution.py:268
  119.4 7.3 %collective-permute-start.5 = (bf16[256,128]{1,0:T(8,128)(2,1)S(1)}, bf16[256,128]{1,0:T(8,128)(2,1)S(1)}, u32[]{:S(2)}, u32[]{:S(2)}) collective-permute-start(bf16[256,128]{1,0:T(8,128)(2,1)S(1)} %get-tuple-element.23), channel_id=1, source_target_pairs={{0,2},{1,3},{2,0},{3,1},{4,6},{5,7},{6,4},{7,5},{8,10},{9,11},{10,... | collective-permute-start | bytes 196616 | tf_op jit(solution)/shard_map/ppermute | solution.py:268
  126.7 7.5 %collective-permute-done.4 = bf16[256,128]{1,0:T(8,128)(2,1)S(1)} collective-permute-done((bf16[256,128]{1,0:T(8,128)(2,1)S(1)}, bf16[256,128]{1,0:T(8,128)(2,1)S(1)}, u32[]{:S(2)}, u32[]{:S(2)}) %collective-permute-start.4) | collective-permute-done | bytes 65568 | tf_op jit(solution)/shard_map/ppermute | solution.py:268
  134.2 2.1 %collective-permute-done.5 = bf16[256,128]{1,0:T(8,128)(2,1)S(1)} collective-permute-done((bf16[256,128]{1,0:T(8,128)(2,1)S(1)}, bf16[256,128]{1,0:T(8,128)(2,1)S(1)}, u32[]{:S(2)}, u32[]{:S(2)}) %collective-permute-start.5) | collective-permute-done | bytes 65568 | tf_op jit(solution)/shard_map/ppermute | solution.py:268
  136.4 0.0 collective-permute-done.6
  136.4 2.6 %collective-permute-start.9 = (bf16[768,128]{1,0:T(8,128)(2,1)S(1)}, bf16[768,128]{1,0:T(8,128)(2,1)S(1)}, u32[]{:S(2)}, u32[]{:S(2)}) collective-permute-start(bf16[768,128]{1,0:T(8,128)(2,1)S(1)} %constant_dynamic-update-slice_fusion.refs_0_), channel_id=1, source_target_pairs={{0,384},{128,0},{256,128},{384,256},{1,385},{129,1},{257,129},{385... | collective-permute-start | bytes 589832 | tf_op jit(solution)/shard_map/ppermute | solution.py:268
  139.0 3.5 %collective-permute-start.8 = (bf16[768,128]{1,0:T(8,128)(2,1)S(1)}, bf16[768,128]{1,0:T(8,128)(2,1)S(1)}, u32[]{:S(2)}, u32[]{:S(2)}) collective-permute-start(bf16[768,128]{1,0:T(8,128)(2,1)S(1)} %constant_dynamic-update-slice_fusion.refs_0_), channel_id=1, source_target_pairs={{0,256},{128,384},{256,0},{384,128},{1,257},{129,385},{257,1},{385... | collective-permute-start | bytes 589832 | tf_op jit(solution)/shard_map/ppermute | solution.py:268
  142.5 1.9 %collective-permute-start.7 = (bf16[768,128]{1,0:T(8,128)(2,1)S(1)}, bf16[768,128]{1,0:T(8,128)(2,1)S(1)}, u32[]{:S(2)}, u32[]{:S(2)}) collective-permute-start(bf16[768,128]{1,0:T(8,128)(2,1)S(1)} %constant_dynamic-update-slice_fusion.refs_0_), channel_id=1, source_target_pairs={{0,128},{128,256},{256,384},{384,0},{1,129},{129,257},{257,385},{3... | collective-permute-start | bytes 589832 | tf_op jit(solution)/shard_map/ppermute | solution.py:268
  144.4 5.6 %collective-permute-start.10 = (bf16[768,128]{1,0:T(8,128)(2,1)S(1)}, bf16[768,128]{1,0:T(8,128)(2,1)S(1)}, u32[]{:S(2)}, u32[]{:S(2)}) collective-permute-start(bf16[768,128]{1,0:T(8,128)(2,1)S(1)} %constant_dynamic-update-slice_fusion.refs_0_), channel_id=1, source_target_pairs={{0,4},{4,0},{1,5},{5,1},{2,6},{6,2},{3,7},{7,3},{8,12},{12,8},{9,1... | collective-permute-start | bytes 589832 | tf_op jit(solution)/shard_map/ppermute | solution.py:268
  150.1 0.0 collective-permute-done.9.refs_3_
  150.1 1.9 %collective-permute-start.13 = (bf16[768,128]{1,0:T(8,128)(2,1)S(1)}, bf16[768,128]{1,0:T(8,128)(2,1)S(1)}, u32[]{:S(2)}, u32[]{:S(2)}) collective-permute-start(bf16[768,128]{1,0:T(8,128)(2,1)S(1)} %collective-permute-done.9.refs_3_), channel_id=1, source_target_pairs={{0,4},{4,0},{1,5},{5,1},{2,6},{6,2},{3,7},{7,3},{8,12},{12,8},{9,1... | collective-permute-start | bytes 589832 | tf_op jit(solution)/shard_map/ppermute | solution.py:268
  152.0 0.0 collective-permute-done.8.refs_2_
  152.0 3.0 %collective-permute-start.12 = (bf16[768,128]{1,0:T(8,128)(2,1)S(1)}, bf16[768,128]{1,0:T(8,128)(2,1)S(1)}, u32[]{:S(2)}, u32[]{:S(2)}) collective-permute-start(bf16[768,128]{1,0:T(8,128)(2,1)S(1)} %collective-permute-done.8.refs_2_), channel_id=1, source_target_pairs={{0,4},{4,0},{1,5},{5,1},{2,6},{6,2},{3,7},{7,3},{8,12},{12,8},{9,1... | collective-permute-start | bytes 589832 | tf_op jit(solution)/shard_map/ppermute | solution.py:268
  155.1 0.0 collective-permute-done.7.refs_1_
  155.1 1.9 %collective-permute-start.11 = (bf16[768,128]{1,0:T(8,128)(2,1)S(1)}, bf16[768,128]{1,0:T(8,128)(2,1)S(1)}, u32[]{:S(2)}, u32[]{:S(2)}) collective-permute-start(bf16[768,128]{1,0:T(8,128)(2,1)S(1)} %collective-permute-done.7.refs_1_), channel_id=1, source_target_pairs={{0,4},{4,0},{1,5},{5,1},{2,6},{6,2},{3,7},{7,3},{8,12},{12,8},{9,1... | collective-permute-start | bytes 589832 | tf_op jit(solution)/shard_map/ppermute | solution.py:268
  157.0 1.1 constant_dynamic-slice_fusion.3
  158.1 0.0 collective-permute-done.10.refs_4_
  158.1 0.0 collective-permute-done.13.refs_7_
  158.1 0.0 collective-permute-done.12.refs_6_
  158.1 0.3 collective-permute-done.11.refs_5_
  158.4 0.0 all-to-all-done.3.arrived_ref
  158.4 2.5 %input_gradient.1 = (bf16[384,1024]{1,0:T(8,128)(2,1)}, bf16[32,32]{1,0:T(8,128)(2,1)}) custom-call(s32[8]{0:T(128)S(1)} %compare_select_fusion.4.where_ref, bf16[4,392,256]{2,1,0:T(8,128)(2,1)S(1)} %all-to-all-done.3.arrived_ref, bf16[1024,128]{1,0:T(8,128)(2,1)S(1)} %get-tuple-element.30.own_k_ref, bf16[1024,128]{1,0:T(8,128)(2,1)S(1)} %get-tuple-element.29.own_v_ref, ...), custom_call_target="tpu_custom_call" | custom-call | tf_op jit(solution)/shard_map/input_gradient/pallas_call | solution.py:379
  (8 shorter events, 0.1 us)
Async XLA Ops:
  0.6 9.7 %collective-permute-start = (s32[1]{0:T(128)}, s32[1]{0:T(128)}, u32[]{:S(2)}, u32[]{:S(2)}) collective-permute-start(s32[1]{0:T(128)} %param.13), channel_id=1, source_target_pairs={{0,4},{4,0},{1,5},{5,1},{2,6},{6,2},{3,7},{7,3},{8,12},{12,8},{9,1... | collective-permute-start | bytes 20 | tf_op jit(solution)/shard_map/ppermute | solution.py:268
  12.6 6.9 %copy-start.1 = (bf16[384,128]{1,0:T(8,128)(2,1)S(1)}, bf16[384,128]{1,0:T(8,128)(2,1)}, u32[]{:S(2)}) copy-start(bf16[384,128]{1,0:T(8,128)(2,1)} %param.12) | copy-start | bytes 294916
  12.6 6.9 %copy-start.2 = (bf16[384,128]{1,0:T(8,128)(2,1)S(1)}, bf16[384,128]{1,0:T(8,128)(2,1)}, u32[]{:S(2)}) copy-start(bf16[384,128]{1,0:T(8,128)(2,1)} %param.11) | copy-start | bytes 294916
  12.6 25.5 %all-to-all-start = ((bf16[64,40,128]{2,1,0:T(8,128)(2,1)}), bf16[64,40,128]{2,1,0:T(8,128)(2,1)S(1)}, u32[]{:S(2)}, u32[]{:S(2)}) async-start(bf16[64,40,128]{2,1,0:T(8,128)(2,1)} %row_pack.1), calls=%async_computation | async-start | bytes 1310720 | tf_op jit(solution)/shard_map/all_to_all | solution.py:263
  19.6 3.6 %collective-permute-start.1 = (bf16[384,256]{1,0:T(8,128)(2,1)S(1)}, bf16[384,256]{1,0:T(8,128)(2,1)S(1)}, u32[]{:S(2)}, u32[]{:S(2)}) collective-permute-start(bf16[384,256]{1,0:T(8,128)(2,1)S(1)} %pad_maximum_fusion.1), channel_id=1, source_target_pairs={{0,4},{4,0},{1,5},{5,1},{2,6},{6,2},{3,7},{7,3},{8,12},{12,8},{9,1... | collective-permute-start | bytes 589832 | tf_op jit(solution)/shard_map/ppermute | solution.py:268
  68.9 7.8 %copy-start.3 = (bf16[32,2048]{1,0:T(8,128)(2,1)S(1)}, bf16[32,2048]{1,0:T(8,128)(2,1)}, u32[]{:S(2)}) copy-start(bf16[32,2048]{1,0:T(8,128)(2,1)} %param.15) | copy-start | bytes 393220
  68.9 20.5 %all-to-all-start.2 = ((bf16[64,24,128]{2,1,0:T(8,128)(2,1)}), bf16[64,24,128]{2,1,0:T(8,128)(2,1)S(1)}, u32[]{:S(2)}, u32[]{:S(2)}) async-start(bf16[64,24,128]{2,1,0:T(8,128)(2,1)} %row_merge.1), calls=%async_computation.2 | async-start | bytes 786432 | tf_op jit(solution)/shard_map/all_to_all | solution.py:263
  76.7 4.4 %collective-permute-start.2 = (bf16[32,2048]{1,0:T(8,128)(2,1)S(1)}, bf16[32,2048]{1,0:T(8,128)(2,1)S(1)}, u32[]{:S(2)}, u32[]{:S(2)}) collective-permute-start(bf16[32,2048]{1,0:T(8,128)(2,1)S(1)} %copy-done.3), channel_id=1, source_target_pairs={{0,4},{4,0},{1,5},{5,1},{2,6},{6,2},{3,7},{7,3},{8,12},{12,8},{9,1... | collective-permute-start | bytes 393224 | tf_op jit(solution)/shard_map/ppermute | solution.py:268
  92.5 6.6 %collective-permute-start.3 = (f32[448,256]{1,0:T(8,128)S(1)}, f32[448,256]{1,0:T(8,128)S(1)}, u32[]{:S(2)}, u32[]{:S(2)}) collective-permute-start(f32[448,256]{1,0:T(8,128)S(1)} %get-tuple-element.16), channel_id=1, source_target_pairs={{0,4},{4,0},{1,5},{5,1},{2,6},{6,2},{3,7},{7,3},{8,12},{12,8},{9,1... | collective-permute-start | bytes 1376264 | tf_op jit(solution)/shard_map/ppermute | solution.py:268
  99.1 10.8 %copy-start = (bf16[4096,128]{1,0:T(8,128)(2,1)S(1)}, bf16[4096,128]{1,0:T(8,128)(2,1)}, u32[]{:S(2)}) copy-start(bf16[4096,128]{1,0:T(8,128)(2,1)} %param.17) | copy-start | bytes 3145732
  100.8 57.6 %all-to-all-start.3 = ((bf16[4,392,256]{2,1,0:T(8,128)(2,1)}), bf16[4,392,256]{2,1,0:T(8,128)(2,1)S(1)}, u32[]{:S(2)}, u32[]{:S(2)}) async-start(bf16[4,392,256]{2,1,0:T(8,128)(2,1)} %get-tuple-element.19), calls=%async_computation.3 | async-start | bytes 1605632 | tf_op jit(solution)/shard_map/all_to_all | solution.py:263
  112.0 22.2 %collective-permute-start.4 = (bf16[256,128]{1,0:T(8,128)(2,1)S(1)}, bf16[256,128]{1,0:T(8,128)(2,1)S(1)}, u32[]{:S(2)}, u32[]{:S(2)}) collective-permute-start(bf16[256,128]{1,0:T(8,128)(2,1)S(1)} %get-tuple-element.24), channel_id=1, source_target_pairs={{0,1},{1,2},{2,3},{3,0},{4,5},{5,6},{6,7},{7,4},{8,9},{9,10},{10,1... | collective-permute-start | bytes 196616 | tf_op jit(solution)/shard_map/ppermute | solution.py:268
  116.3 20.1 %collective-permute-start.6 = (bf16[256,128]{1,0:T(8,128)(2,1)S(1)}, bf16[256,128]{1,0:T(8,128)(2,1)S(1)}, u32[]{:S(2)}, u32[]{:S(2)}) collective-permute-start(bf16[256,128]{1,0:T(8,128)(2,1)S(1)} %get-tuple-element.22), channel_id=1, source_target_pairs={{0,3},{1,0},{2,1},{3,2},{4,7},{5,4},{6,5},{7,6},{8,11},{9,8},{10,9... | collective-permute-start | bytes 196616 | tf_op jit(solution)/shard_map/ppermute | solution.py:268
  119.4 17.0 %collective-permute-start.5 = (bf16[256,128]{1,0:T(8,128)(2,1)S(1)}, bf16[256,128]{1,0:T(8,128)(2,1)S(1)}, u32[]{:S(2)}, u32[]{:S(2)}) collective-permute-start(bf16[256,128]{1,0:T(8,128)(2,1)S(1)} %get-tuple-element.23), channel_id=1, source_target_pairs={{0,2},{1,3},{2,0},{3,1},{4,6},{5,7},{6,4},{7,5},{8,10},{9,11},{10,... | collective-permute-start | bytes 196616 | tf_op jit(solution)/shard_map/ppermute | solution.py:268
  136.4 13.6 %collective-permute-start.9 = (bf16[768,128]{1,0:T(8,128)(2,1)S(1)}, bf16[768,128]{1,0:T(8,128)(2,1)S(1)}, u32[]{:S(2)}, u32[]{:S(2)}) collective-permute-start(bf16[768,128]{1,0:T(8,128)(2,1)S(1)} %constant_dynamic-update-slice_fusion.refs_0_), channel_id=1, source_target_pairs={{0,384},{128,0},{256,128},{384,256},{1,385},{129,1},{257,129},{385... | collective-permute-start | bytes 589832 | tf_op jit(solution)/shard_map/ppermute | solution.py:268
  139.0 13.0 %collective-permute-start.8 = (bf16[768,128]{1,0:T(8,128)(2,1)S(1)}, bf16[768,128]{1,0:T(8,128)(2,1)S(1)}, u32[]{:S(2)}, u32[]{:S(2)}) collective-permute-start(bf16[768,128]{1,0:T(8,128)(2,1)S(1)} %constant_dynamic-update-slice_fusion.refs_0_), channel_id=1, source_target_pairs={{0,256},{128,384},{256,0},{384,128},{1,257},{129,385},{257,1},{385... | collective-permute-start | bytes 589832 | tf_op jit(solution)/shard_map/ppermute | solution.py:268
  142.5 12.6 %collective-permute-start.7 = (bf16[768,128]{1,0:T(8,128)(2,1)S(1)}, bf16[768,128]{1,0:T(8,128)(2,1)S(1)}, u32[]{:S(2)}, u32[]{:S(2)}) collective-permute-start(bf16[768,128]{1,0:T(8,128)(2,1)S(1)} %constant_dynamic-update-slice_fusion.refs_0_), channel_id=1, source_target_pairs={{0,128},{128,256},{256,384},{384,0},{1,129},{129,257},{257,385},{3... | collective-permute-start | bytes 589832 | tf_op jit(solution)/shard_map/ppermute | solution.py:268
  144.4 13.7 %collective-permute-start.10 = (bf16[768,128]{1,0:T(8,128)(2,1)S(1)}, bf16[768,128]{1,0:T(8,128)(2,1)S(1)}, u32[]{:S(2)}, u32[]{:S(2)}) collective-permute-start(bf16[768,128]{1,0:T(8,128)(2,1)S(1)} %constant_dynamic-update-slice_fusion.refs_0_), channel_id=1, source_target_pairs={{0,4},{4,0},{1,5},{5,1},{2,6},{6,2},{3,7},{7,3},{8,12},{12,8},{9,1... | collective-permute-start | bytes 589832 | tf_op jit(solution)/shard_map/ppermute | solution.py:268
  150.1 8.0 %collective-permute-start.13 = (bf16[768,128]{1,0:T(8,128)(2,1)S(1)}, bf16[768,128]{1,0:T(8,128)(2,1)S(1)}, u32[]{:S(2)}, u32[]{:S(2)}) collective-permute-start(bf16[768,128]{1,0:T(8,128)(2,1)S(1)} %collective-permute-done.9.refs_3_), channel_id=1, source_target_pairs={{0,4},{4,0},{1,5},{5,1},{2,6},{6,2},{3,7},{7,3},{8,12},{12,8},{9,1... | collective-permute-start | bytes 589832 | tf_op jit(solution)/shard_map/ppermute | solution.py:268
  152.0 6.1 %collective-permute-start.12 = (bf16[768,128]{1,0:T(8,128)(2,1)S(1)}, bf16[768,128]{1,0:T(8,128)(2,1)S(1)}, u32[]{:S(2)}, u32[]{:S(2)}) collective-permute-start(bf16[768,128]{1,0:T(8,128)(2,1)S(1)} %collective-permute-done.8.refs_2_), channel_id=1, source_target_pairs={{0,4},{4,0},{1,5},{5,1},{2,6},{6,2},{3,7},{7,3},{8,12},{12,8},{9,1... | collective-permute-start | bytes 589832 | tf_op jit(solution)/shard_map/ppermute | solution.py:268
  155.1 3.3 %collective-permute-start.11 = (bf16[768,128]{1,0:T(8,128)(2,1)S(1)}, bf16[768,128]{1,0:T(8,128)(2,1)S(1)}, u32[]{:S(2)}, u32[]{:S(2)}) collective-permute-start(bf16[768,128]{1,0:T(8,128)(2,1)S(1)} %collective-permute-done.7.refs_1_), channel_id=1, source_target_pairs={{0,4},{4,0},{1,5},{5,1},{2,6},{6,2},{3,7},{7,3},{8,12},{12,8},{9,1... | collective-permute-start | bytes 589832 | tf_op jit(solution)/shard_map/ppermute | solution.py:268

commit v8 on v7

--- a/solution.py
+++ b/solution.py
@@ -51,18 +51,28 @@
     return wide + pltpu.roll(wide, 112, axis) + pltpu.roll(wide, 96, axis)
 
 
-def pack_kernel(heads, own_ref, other_ref, q_ref, g_ref, row_ref):
+def pack_kernel(heads, q_ref, g_ref, row_ref):
+    lines = []
+    for ref in (q_ref, g_ref):
+        wide = ref[...].astype(F32)
+        lines += [wide[:, h * HEAD_WIDTH : (h + 1) * HEAD_WIDTH] for h in range(heads)]
+    lines.append(jnp.zeros((row_ref.shape[1] - 2 * heads, HEAD_WIDTH), F32))
+    row = jnp.concatenate(lines, axis=0).astype(BF16)
+    for k in range(row_ref.shape[0]):
+        row_ref[k] = row
+
+
+def length_kernel(own_ref, other_ref, row_ref, out_ref, held_ref, sem):
     lane = lax.broadcasted_iota(jnp.int32, (8, 128), 1)
     own, other = own_ref[0], other_ref[0]
     numbers = jnp.where(lane == 0, own // 16, 0) + jnp.where(lane == 1, own % 16, 0)
     numbers += jnp.where(lane == 2, other // 16, 0) + jnp.where(lane == 3, other % 16, 0)
-    lines = []
-    for ref in (q_ref, g_ref):
-        wide = ref[...].astype(F32)
-        lines += [wide[:, h * HEAD_WIDTH : (h + 1) * HEAD_WIDTH] for h in range(heads)]
-    row = jnp.concatenate([*lines, numbers.astype(F32)], axis=0).astype(BF16)
-    for k in range(row_ref.shape[0]):
-        row_ref[k] = row
+    numbers = numbers.astype(F32).astype(BF16)
+    for k in range(held_ref.shape[0]):
+        held_ref[k] = numbers
+    copy = pltpu.make_async_copy(held_ref, out_ref.at[:, out_ref.shape[1] - 8 :, :], sem)
+    copy.start()
+    copy.wait()
 
 
 def first_kernel(heads, group, where_ref, x_ref, k_ref, v_ref, y_ref, place_ref):
@@ -290,13 +300,23 @@
     group = min(16, rows)
 
     other_length = shifted(lengths, CORE, 1)
-    row = pl.pallas_call(
+    pack_call = pl.pallas_call(
         functools.partial(pack_kernel, heads),
         out_shape=jax.ShapeDtypeStruct((rows, lines, HEAD_WIDTH), BF16),
-        in_specs=[SMEM, SMEM, VMEM, VMEM],
+        in_specs=[VMEM, VMEM],
         out_specs=VMEM,
         name="row_pack",
-    )(lengths, other_length, queries, grad_output)
+    )
+    row = pack_call(queries, grad_output)
+    row = pl.pallas_call(
+        length_kernel,
+        out_shape=jax.ShapeDtypeStruct(row.shape, BF16),
+        in_specs=[SMEM, SMEM, pl.BlockSpec(memory_space=pl.ANY)],
+        out_specs=pl.BlockSpec(memory_space=pl.ANY),
+        scratch_shapes=[pltpu.VMEM((rows, 8, HEAD_WIDTH), BF16), pltpu.SemaphoreType.DMA],
+        input_output_aliases={2: 0},
+        name="row_lengths",
+    )(lengths, other_length, row)
     x = exchanged(row, FAR)
 
     cache = jnp.concatenate([key_cache, saved_value_rows], axis=1)

time: 162 us -> 162 us (level)
  transfers between devices with their start and end apart: 17 -> 17, of which waited for: 9 -> 8; matrix products, arithmetic and copies ran while one was open for 2% -> 2% of each run, Pallas kernels for 0% -> 1%
where the time goes in v8:
time: 162 us; the launch traced here: 161 us
  starting transfers between devices  78.1 us (48%)
  waiting for transfers between devices  37.1 us (23%)
  blocking collectives  25.2 us (16%)
  Pallas kernels  15.4 us (10%)
  between operations  2.23 us (1%)
  local copies, waits for them, and re-layouts  2.05 us (1%)
    ppermute x14, starting transfers between devices, shifted(): lax.ppermute(value, axis, [(k, (k + by) % count) for k in range(count)])  54.4 us
    all_to_all x1, blocking collectives, exchanged(): return lax.all_to_all(value, axes, split_axis=0, concat_axis=0, tiled=True)  25.2 us
    all_to_all x3, waiting for transfers between devices, exchanged(): return lax.all_to_all(value, axes, split_axis=0, concat_axis=0, tiled=True)  24.5 us
    all_to_all x3, starting transfers between devices, exchanged(): return lax.all_to_all(value, axes, split_axis=0, concat_axis=0, tiled=True)  23.7 us
    ppermute x14, waiting for transfers between devices, shifted(): lax.ppermute(value, axis, [(k, (k + by) % count) for k in range(count)])  12.6 us
    pallas_call x1, Pallas kernels, local(): pl.pallas_call(functools.partial(first_kernel, heads, group), out_shape=(...  3.67 us
  transfers between devices with their start and end apart: 17, of which 8 were waited for; matrix products, arithmetic and copies ran while one was open for 2% of the time, Pallas kernels for 1%

profile of v8, /device:TPU:1, one launch (start us, length us, event | category | flops | bytes accessed | tf_op | source)
XLA Modules:
  0.0 161.3 jit_solution(12506988665160025751)
XLA Ops:
  0.6 8.7 %collective-permute-start = (s32[1]{0:T(128)}, s32[1]{0:T(128)}, u32[]{:S(2)}, u32[]{:S(2)}) collective-permute-start(s32[1]{0:T(128)} %param.13), channel_id=1, source_target_pairs={{0,4},{4,0},{1,5},{5,1},{2,6},{6,2},{3,7},{7,3},{8,12},{12,8},{9,1... | collective-permute-start | bytes 20 | tf_op jit(solution)/shard_map/ppermute | solution.py:278
  10.0 1.6 row_pack.1.row_ref
  11.6 0.0 collective-permute-done.other_ref
  11.6 1.4 row_lengths.1
  13.0 0.0 copy-start.1
  13.0 0.0 copy-start.2
  13.1 6.9 %all-to-all-start = ((bf16[64,40,128]{2,1,0:T(8,128)(2,1)}), bf16[64,40,128]{2,1,0:T(8,128)(2,1)S(1)}, u32[]{:S(2)}, u32[]{:S(2)}) async-start(bf16[64,40,128]{2,1,0:T(8,128)(2,1)} %row_lengths.1), calls=%async_computation | async-start | bytes 1310720 | tf_op jit(solution)/shard_map/all_to_all | solution.py:273
  20.0 0.0 copy-done.1
  20.0 0.0 copy-done.2
  20.0 2.2 %collective-permute-start.1 = (bf16[384,256]{1,0:T(8,128)(2,1)S(1)}, bf16[384,256]{1,0:T(8,128)(2,1)S(1)}, u32[]{:S(2)}, u32[]{:S(2)}) collective-permute-start(bf16[384,256]{1,0:T(8,128)(2,1)S(1)} %pad_maximum_fusion.1), channel_id=1, source_target_pairs={{0,4},{4,0},{1,5},{5,1},{2,6},{6,2},{3,7},{7,3},{8,12},{12,8},{9,1... | collective-permute-start | bytes 589832 | tf_op jit(solution)/shard_map/ppermute | solution.py:278
  22.9 0.5 collective-permute-done.1
  23.4 15.8 %all-to-all-done.x_ref = bf16[64,40,128]{2,1,0:T(8,128)(2,1)S(1)} async-done(((bf16[64,40,128]{2,1,0:T(8,128)(2,1)}), bf16[64,40,128]{2,1,0:T(8,128)(2,1)S(1)}, u32[]{:S(2)}, u32[]{:S(2)}) %all-to-all-start) | async-done | bytes 655392 | tf_op jit(solution)/shard_map/all_to_all | solution.py:273
  39.2 3.7 %row_partials.1 = (bf16[64,40,128]{2,1,0:T(8,128)(2,1)S(1)}, f32[4]{0:T(128)S(1)}) custom-call(s32[8]{0:T(128)S(1)} %compare_select_fusion.4.where_ref, bf16[64,40,128]{2,1,0:T(8,128)(2,1)S(1)} %all-to-all-done.x_ref, bf16[768,128]{1,0:T(8,128)(2,1)S(1)} %get-tuple-element.27.k_ref, bf16[768,128]{1,0:T(8,128)(2,1)S(1)} %get-tuple-element.28.v_ref), custom_call_target="tpu_custom_call" | custom-call | tf_op jit(solution)/shard_map/row_partials/pallas_call | solution.py:353
  42.9 25.2 %all_to_all.20.z_ref = bf16[64,40,128]{2,1,0:T(8,128)(2,1)S(1)} all-to-all(bf16[64,40,128]{2,1,0:T(8,128)(2,1)S(1)} %get-tuple-element.14), channel_id=1, replica_groups=mesh['seq_0'=4,'seq_1'=8,'seq_2'=2,'seq_3'=2,'head'=4] {'seq_0','seq_1',..., dimensions={0} | all-to-all | bytes 1310720 | tf_op jit(solution)/shard_map/all_to_all | solution.py:273
  68.1 1.5 row_merge.1
  69.6 0.0 copy-start.3
  69.6 7.7 %all-to-all-start.2 = ((bf16[64,24,128]{2,1,0:T(8,128)(2,1)}), bf16[64,24,128]{2,1,0:T(8,128)(2,1)S(1)}, u32[]{:S(2)}, u32[]{:S(2)}) async-start(bf16[64,24,128]{2,1,0:T(8,128)(2,1)} %row_merge.1), calls=%async_computation.2 | async-start | bytes 786432 | tf_op jit(solution)/shard_map/all_to_all | solution.py:273
  77.3 0.0 copy-done.3
  77.3 3.4 %collective-permute-start.2 = (bf16[32,2048]{1,0:T(8,128)(2,1)S(1)}, bf16[32,2048]{1,0:T(8,128)(2,1)S(1)}, u32[]{:S(2)}, u32[]{:S(2)}) collective-permute-start(bf16[32,2048]{1,0:T(8,128)(2,1)S(1)} %copy-done.3), channel_id=1, source_target_pairs={{0,4},{4,0},{1,5},{5,1},{2,6},{6,2},{3,7},{7,3},{8,12},{12,8},{9,1... | collective-permute-start | bytes 393224 | tf_op jit(solution)/shard_map/ppermute | solution.py:278
  80.7 1.0 collective-permute-done.2
  81.7 8.7 %all-to-all-done.2.u_ref = bf16[64,24,128]{2,1,0:T(8,128)(2,1)S(1)} async-done(((bf16[64,24,128]{2,1,0:T(8,128)(2,1)}), bf16[64,24,128]{2,1,0:T(8,128)(2,1)S(1)}, u32[]{:S(2)}, u32[]{:S(2)}) %all-to-all-start.2) | async-done | bytes 393248 | tf_op jit(solution)/shard_map/all_to_all | solution.py:273
  90.3 3.1 %slot_gradients.1 = (f32[448,256]{1,0:T(8,128)S(1)}, f32[448,256]{1,0:T(8,128)S(1)}) custom-call(s32[8]{0:T(128)S(1)} %compare_select_fusion.4.where_ref, f32[4]{0:T(128)S(1)} %get-tuple-element.13.place_ref, bf16[64,40,128]{2,1,0:T(8,128)(2,1)S(1)} %all-to-all-done.x_ref, bf16[64,24,128]{2,1,0:T(8,128)(2,1)S(1)} %all-to-all-done.2.u_ref, ...), custom_call_target="tpu_custom_call" | custom-call | tf_op jit(solution)/shard_map/slot_gradients/pallas_call | solution.py:375
  93.5 4.8 %collective-permute-start.3 = (f32[448,256]{1,0:T(8,128)S(1)}, f32[448,256]{1,0:T(8,128)S(1)}, u32[]{:S(2)}, u32[]{:S(2)}) collective-permute-start(f32[448,256]{1,0:T(8,128)S(1)} %get-tuple-element.16), channel_id=1, source_target_pairs={{0,4},{4,0},{1,5},{5,1},{2,6},{6,2},{3,7},{7,3},{8,12},{12,8},{9,1... | collective-permute-start | bytes 1376264 | tf_op jit(solution)/shard_map/ppermute | solution.py:278
  98.3 1.4 collective-permute-done.3.other_ref
  99.8 0.0 copy-start
  99.8 1.6 %slot_sums.1 = (bf16[384,128]{1,0:T(8,128)(2,1)}, bf16[384,128]{1,0:T(8,128)(2,1)}, bf16[4,392,256]{2,1,0:T(8,128)(2,1)}) custom-call(s32[8]{0:T(128)S(1)} %compare_select_fusion.4.where_ref, f32[448,256]{1,0:T(8,128)S(1)} %get-tuple-element.15.own_ref, f32[448,256]{1,0:T(8,128)S(1)} %collective-permute-done.3.other_ref), custom_call_target="tpu_custom_call" | custom-call | tf_op jit(solution)/shard_map/slot_sums/pallas_call | solution.py:385
  101.4 9.1 %all-to-all-start.3 = ((bf16[4,392,256]{2,1,0:T(8,128)(2,1)}), bf16[4,392,256]{2,1,0:T(8,128)(2,1)S(1)}, u32[]{:S(2)}, u32[]{:S(2)}) async-start(bf16[4,392,256]{2,1,0:T(8,128)(2,1)} %get-tuple-element.19), calls=%async_computation.3 | async-start | bytes 1605632 | tf_op jit(solution)/shard_map/all_to_all | solution.py:273
  110.5 0.0 copy-done
  110.5 1.2 broadcast_select_fusion
  111.7 0.9 constant_dynamic-slice_fusion
  112.6 4.3 %collective-permute-start.4 = (bf16[256,128]{1,0:T(8,128)(2,1)S(1)}, bf16[256,128]{1,0:T(8,128)(2,1)S(1)}, u32[]{:S(2)}, u32[]{:S(2)}) collective-permute-start(bf16[256,128]{1,0:T(8,128)(2,1)S(1)} %get-tuple-element.24), channel_id=1, source_target_pairs={{0,1},{1,2},{2,3},{3,0},{4,5},{5,6},{6,7},{7,4},{8,9},{9,10},{10,1... | collective-permute-start | bytes 196616 | tf_op jit(solution)/shard_map/ppermute | solution.py:278
  116.9 3.1 %collective-permute-start.6 = (bf16[256,128]{1,0:T(8,128)(2,1)S(1)}, bf16[256,128]{1,0:T(8,128)(2,1)S(1)}, u32[]{:S(2)}, u32[]{:S(2)}) collective-permute-start(bf16[256,128]{1,0:T(8,128)(2,1)S(1)} %get-tuple-element.22), channel_id=1, source_target_pairs={{0,3},{1,0},{2,1},{3,2},{4,7},{5,4},{6,5},{7,6},{8,11},{9,8},{10,9... | collective-permute-start | bytes 196616 | tf_op jit(solution)/shard_map/ppermute | solution.py:278
  120.0 7.3 %collective-permute-start.5 = (bf16[256,128]{1,0:T(8,128)(2,1)S(1)}, bf16[256,128]{1,0:T(8,128)(2,1)S(1)}, u32[]{:S(2)}, u32[]{:S(2)}) collective-permute-start(bf16[256,128]{1,0:T(8,128)(2,1)S(1)} %get-tuple-element.23), channel_id=1, source_target_pairs={{0,2},{1,3},{2,0},{3,1},{4,6},{5,7},{6,4},{7,5},{8,10},{9,11},{10,... | collective-permute-start | bytes 196616 | tf_op jit(solution)/shard_map/ppermute | solution.py:278
  127.3 7.7 %collective-permute-done.4 = bf16[256,128]{1,0:T(8,128)(2,1)S(1)} collective-permute-done((bf16[256,128]{1,0:T(8,128)(2,1)S(1)}, bf16[256,128]{1,0:T(8,128)(2,1)S(1)}, u32[]{:S(2)}, u32[]{:S(2)}) %collective-permute-start.4) | collective-permute-done | bytes 65568 | tf_op jit(solution)/shard_map/ppermute | solution.py:278
  135.1 1.8 %collective-permute-done.5 = bf16[256,128]{1,0:T(8,128)(2,1)S(1)} collective-permute-done((bf16[256,128]{1,0:T(8,128)(2,1)S(1)}, bf16[256,128]{1,0:T(8,128)(2,1)S(1)}, u32[]{:S(2)}, u32[]{:S(2)}) %collective-permute-start.5) | collective-permute-done | bytes 65568 | tf_op jit(solution)/shard_map/ppermute | solution.py:278
  136.9 0.0 collective-permute-done.6
  136.9 2.7 %collective-permute-start.9 = (bf16[768,128]{1,0:T(8,128)(2,1)S(1)}, bf16[768,128]{1,0:T(8,128)(2,1)S(1)}, u32[]{:S(2)}, u32[]{:S(2)}) collective-permute-start(bf16[768,128]{1,0:T(8,128)(2,1)S(1)} %constant_dynamic-update-slice_fusion.refs_0_), channel_id=1, source_target_pairs={{0,384},{128,0},{256,128},{384,256},{1,385},{129,1},{257,129},{385... | collective-permute-start | bytes 589832 | tf_op jit(solution)/shard_map/ppermute | solution.py:278
  139.6 3.5 %collective-permute-start.8 = (bf16[768,128]{1,0:T(8,128)(2,1)S(1)}, bf16[768,128]{1,0:T(8,128)(2,1)S(1)}, u32[]{:S(2)}, u32[]{:S(2)}) collective-permute-start(bf16[768,128]{1,0:T(8,128)(2,1)S(1)} %constant_dynamic-update-slice_fusion.refs_0_), channel_id=1, source_target_pairs={{0,256},{128,384},{256,0},{384,128},{1,257},{129,385},{257,1},{385... | collective-permute-start | bytes 589832 | tf_op jit(solution)/shard_map/ppermute | solution.py:278
  143.1 1.9 %collective-permute-start.7 = (bf16[768,128]{1,0:T(8,128)(2,1)S(1)}, bf16[768,128]{1,0:T(8,128)(2,1)S(1)}, u32[]{:S(2)}, u32[]{:S(2)}) collective-permute-start(bf16[768,128]{1,0:T(8,128)(2,1)S(1)} %constant_dynamic-update-slice_fusion.refs_0_), channel_id=1, source_target_pairs={{0,128},{128,256},{256,384},{384,0},{1,129},{129,257},{257,385},{3... | collective-permute-start | bytes 589832 | tf_op jit(solution)/shard_map/ppermute | solution.py:278
  145.0 5.7 %collective-permute-start.10 = (bf16[768,128]{1,0:T(8,128)(2,1)S(1)}, bf16[768,128]{1,0:T(8,128)(2,1)S(1)}, u32[]{:S(2)}, u32[]{:S(2)}) collective-permute-start(bf16[768,128]{1,0:T(8,128)(2,1)S(1)} %constant_dynamic-update-slice_fusion.refs_0_), channel_id=1, source_target_pairs={{0,4},{4,0},{1,5},{5,1},{2,6},{6,2},{3,7},{7,3},{8,12},{12,8},{9,1... | collective-permute-start | bytes 589832 | tf_op jit(solution)/shard_map/ppermute | solution.py:278
  150.7 0.0 collective-permute-done.9.refs_3_
  150.7 1.9 %collective-permute-start.13 = (bf16[768,128]{1,0:T(8,128)(2,1)S(1)}, bf16[768,128]{1,0:T(8,128)(2,1)S(1)}, u32[]{:S(2)}, u32[]{:S(2)}) collective-permute-start(bf16[768,128]{1,0:T(8,128)(2,1)S(1)} %collective-permute-done.9.refs_3_), channel_id=1, source_target_pairs={{0,4},{4,0},{1,5},{5,1},{2,6},{6,2},{3,7},{7,3},{8,12},{12,8},{9,1... | collective-permute-start | bytes 589832 | tf_op jit(solution)/shard_map/ppermute | solution.py:278
  152.6 0.0 collective-permute-done.8.refs_2_
  152.6 2.9 %collective-permute-start.12 = (bf16[768,128]{1,0:T(8,128)(2,1)S(1)}, bf16[768,128]{1,0:T(8,128)(2,1)S(1)}, u32[]{:S(2)}, u32[]{:S(2)}) collective-permute-start(bf16[768,128]{1,0:T(8,128)(2,1)S(1)} %collective-permute-done.8.refs_2_), channel_id=1, source_target_pairs={{0,4},{4,0},{1,5},{5,1},{2,6},{6,2},{3,7},{7,3},{8,12},{12,8},{9,1... | collective-permute-start | bytes 589832 | tf_op jit(solution)/shard_map/ppermute | solution.py:278
  155.5 0.0 collective-permute-done.7.refs_1_
  155.6 2.0 %collective-permute-start.11 = (bf16[768,128]{1,0:T(8,128)(2,1)S(1)}, bf16[768,128]{1,0:T(8,128)(2,1)S(1)}, u32[]{:S(2)}, u32[]{:S(2)}) collective-permute-start(bf16[768,128]{1,0:T(8,128)(2,1)S(1)} %collective-permute-done.7.refs_1_), channel_id=1, source_target_pairs={{0,4},{4,0},{1,5},{5,1},{2,6},{6,2},{3,7},{7,3},{8,12},{12,8},{9,1... | collective-permute-start | bytes 589832 | tf_op jit(solution)/shard_map/ppermute | solution.py:278
  157.6 1.1 constant_dynamic-slice_fusion.3
  158.6 0.0 collective-permute-done.10.refs_4_
  158.7 0.0 collective-permute-done.13.refs_7_
  158.7 0.0 collective-permute-done.12.refs_6_
  158.7 0.2 collective-permute-done.11.refs_5_
  158.9 0.0 all-to-all-done.3.arrived_ref
  158.9 2.4 %input_gradient.1 = (bf16[384,1024]{1,0:T(8,128)(2,1)}, bf16[32,32]{1,0:T(8,128)(2,1)}) custom-call(s32[8]{0:T(128)S(1)} %compare_select_fusion.4.where_ref, bf16[4,392,256]{2,1,0:T(8,128)(2,1)S(1)} %all-to-all-done.3.arrived_ref, bf16[1024,128]{1,0:T(8,128)(2,1)S(1)} %get-tuple-element.30.own_k_ref, bf16[1024,128]{1,0:T(8,128)(2,1)S(1)} %get-tuple-element.29.own_v_ref, ...), custom_call_target="tpu_custom_call" | custom-call | tf_op jit(solution)/shard_map/input_gradient/pallas_call | solution.py:399
  (8 shorter events, 0.1 us)
Async XLA Ops:
  0.6 11.0 %collective-permute-start = (s32[1]{0:T(128)}, s32[1]{0:T(128)}, u32[]{:S(2)}, u32[]{:S(2)}) collective-permute-start(s32[1]{0:T(128)} %param.13), channel_id=1, source_target_pairs={{0,4},{4,0},{1,5},{5,1},{2,6},{6,2},{3,7},{7,3},{8,12},{12,8},{9,1... | collective-permute-start | bytes 20 | tf_op jit(solution)/shard_map/ppermute | solution.py:278
  13.0 6.9 %copy-start.1 = (bf16[384,128]{1,0:T(8,128)(2,1)S(1)}, bf16[384,128]{1,0:T(8,128)(2,1)}, u32[]{:S(2)}) copy-start(bf16[384,128]{1,0:T(8,128)(2,1)} %param.12) | copy-start | bytes 294916
  13.0 6.9 %copy-start.2 = (bf16[384,128]{1,0:T(8,128)(2,1)S(1)}, bf16[384,128]{1,0:T(8,128)(2,1)}, u32[]{:S(2)}) copy-start(bf16[384,128]{1,0:T(8,128)(2,1)} %param.11) | copy-start | bytes 294916
  13.1 26.1 %all-to-all-start = ((bf16[64,40,128]{2,1,0:T(8,128)(2,1)}), bf16[64,40,128]{2,1,0:T(8,128)(2,1)S(1)}, u32[]{:S(2)}, u32[]{:S(2)}) async-start(bf16[64,40,128]{2,1,0:T(8,128)(2,1)} %row_lengths.1), calls=%async_computation | async-start | bytes 1310720 | tf_op jit(solution)/shard_map/all_to_all | solution.py:273
  20.0 3.3 %collective-permute-start.1 = (bf16[384,256]{1,0:T(8,128)(2,1)S(1)}, bf16[384,256]{1,0:T(8,128)(2,1)S(1)}, u32[]{:S(2)}, u32[]{:S(2)}) collective-permute-start(bf16[384,256]{1,0:T(8,128)(2,1)S(1)} %pad_maximum_fusion.1), channel_id=1, source_target_pairs={{0,4},{4,0},{1,5},{5,1},{2,6},{6,2},{3,7},{7,3},{8,12},{12,8},{9,1... | collective-permute-start | bytes 589832 | tf_op jit(solution)/shard_map/ppermute | solution.py:278
  69.6 7.7 %copy-start.3 = (bf16[32,2048]{1,0:T(8,128)(2,1)S(1)}, bf16[32,2048]{1,0:T(8,128)(2,1)}, u32[]{:S(2)}) copy-start(bf16[32,2048]{1,0:T(8,128)(2,1)} %param.15) | copy-start | bytes 393220
  69.6 20.7 %all-to-all-start.2 = ((bf16[64,24,128]{2,1,0:T(8,128)(2,1)}), bf16[64,24,128]{2,1,0:T(8,128)(2,1)S(1)}, u32[]{:S(2)}, u32[]{:S(2)}) async-start(bf16[64,24,128]{2,1,0:T(8,128)(2,1)} %row_merge.1), calls=%async_computation.2 | async-start | bytes 786432 | tf_op jit(solution)/shard_map/all_to_all | solution.py:273
  77.3 4.3 %collective-permute-start.2 = (bf16[32,2048]{1,0:T(8,128)(2,1)S(1)}, bf16[32,2048]{1,0:T(8,128)(2,1)S(1)}, u32[]{:S(2)}, u32[]{:S(2)}) collective-permute-start(bf16[32,2048]{1,0:T(8,128)(2,1)S(1)} %copy-done.3), channel_id=1, source_target_pairs={{0,4},{4,0},{1,5},{5,1},{2,6},{6,2},{3,7},{7,3},{8,12},{12,8},{9,1... | collective-permute-start | bytes 393224 | tf_op jit(solution)/shard_map/ppermute | solution.py:278
  93.5 6.3 %collective-permute-start.3 = (f32[448,256]{1,0:T(8,128)S(1)}, f32[448,256]{1,0:T(8,128)S(1)}, u32[]{:S(2)}, u32[]{:S(2)}) collective-permute-start(f32[448,256]{1,0:T(8,128)S(1)} %get-tuple-element.16), channel_id=1, source_target_pairs={{0,4},{4,0},{1,5},{5,1},{2,6},{6,2},{3,7},{7,3},{8,12},{12,8},{9,1... | collective-permute-start | bytes 1376264 | tf_op jit(solution)/shard_map/ppermute | solution.py:278
  99.8 10.8 %copy-start = (bf16[4096,128]{1,0:T(8,128)(2,1)S(1)}, bf16[4096,128]{1,0:T(8,128)(2,1)}, u32[]{:S(2)}) copy-start(bf16[4096,128]{1,0:T(8,128)(2,1)} %param.17) | copy-start | bytes 3145732
  101.4 57.5 %all-to-all-start.3 = ((bf16[4,392,256]{2,1,0:T(8,128)(2,1)}), bf16[4,392,256]{2,1,0:T(8,128)(2,1)S(1)}, u32[]{:S(2)}, u32[]{:S(2)}) async-start(bf16[4,392,256]{2,1,0:T(8,128)(2,1)} %get-tuple-element.19), calls=%async_computation.3 | async-start | bytes 1605632 | tf_op jit(solution)/shard_map/all_to_all | solution.py:273
  112.6 22.4 %collective-permute-start.4 = (bf16[256,128]{1,0:T(8,128)(2,1)S(1)}, bf16[256,128]{1,0:T(8,128)(2,1)S(1)}, u32[]{:S(2)}, u32[]{:S(2)}) collective-permute-start(bf16[256,128]{1,0:T(8,128)(2,1)S(1)} %get-tuple-element.24), channel_id=1, source_target_pairs={{0,1},{1,2},{2,3},{3,0},{4,5},{5,6},{6,7},{7,4},{8,9},{9,10},{10,1... | collective-permute-start | bytes 196616 | tf_op jit(solution)/shard_map/ppermute | solution.py:278
  116.9 20.0 %collective-permute-start.6 = (bf16[256,128]{1,0:T(8,128)(2,1)S(1)}, bf16[256,128]{1,0:T(8,128)(2,1)S(1)}, u32[]{:S(2)}, u32[]{:S(2)}) collective-permute-start(bf16[256,128]{1,0:T(8,128)(2,1)S(1)} %get-tuple-element.22), channel_id=1, source_target_pairs={{0,3},{1,0},{2,1},{3,2},{4,7},{5,4},{6,5},{7,6},{8,11},{9,8},{10,9... | collective-permute-start | bytes 196616 | tf_op jit(solution)/shard_map/ppermute | solution.py:278
  120.0 16.9 %collective-permute-start.5 = (bf16[256,128]{1,0:T(8,128)(2,1)S(1)}, bf16[256,128]{1,0:T(8,128)(2,1)S(1)}, u32[]{:S(2)}, u32[]{:S(2)}) collective-permute-start(bf16[256,128]{1,0:T(8,128)(2,1)S(1)} %get-tuple-element.23), channel_id=1, source_target_pairs={{0,2},{1,3},{2,0},{3,1},{4,6},{5,7},{6,4},{7,5},{8,10},{9,11},{10,... | collective-permute-start | bytes 196616 | tf_op jit(solution)/shard_map/ppermute | solution.py:278
  136.9 13.7 %collective-permute-start.9 = (bf16[768,128]{1,0:T(8,128)(2,1)S(1)}, bf16[768,128]{1,0:T(8,128)(2,1)S(1)}, u32[]{:S(2)}, u32[]{:S(2)}) collective-permute-start(bf16[768,128]{1,0:T(8,128)(2,1)S(1)} %constant_dynamic-update-slice_fusion.refs_0_), channel_id=1, source_target_pairs={{0,384},{128,0},{256,128},{384,256},{1,385},{129,1},{257,129},{385... | collective-permute-start | bytes 589832 | tf_op jit(solution)/shard_map/ppermute | solution.py:278
  139.6 13.0 %collective-permute-start.8 = (bf16[768,128]{1,0:T(8,128)(2,1)S(1)}, bf16[768,128]{1,0:T(8,128)(2,1)S(1)}, u32[]{:S(2)}, u32[]{:S(2)}) collective-permute-start(bf16[768,128]{1,0:T(8,128)(2,1)S(1)} %constant_dynamic-update-slice_fusion.refs_0_), channel_id=1, source_target_pairs={{0,256},{128,384},{256,0},{384,128},{1,257},{129,385},{257,1},{385... | collective-permute-start | bytes 589832 | tf_op jit(solution)/shard_map/ppermute | solution.py:278
  143.1 12.5 %collective-permute-start.7 = (bf16[768,128]{1,0:T(8,128)(2,1)S(1)}, bf16[768,128]{1,0:T(8,128)(2,1)S(1)}, u32[]{:S(2)}, u32[]{:S(2)}) collective-permute-start(bf16[768,128]{1,0:T(8,128)(2,1)S(1)} %constant_dynamic-update-slice_fusion.refs_0_), channel_id=1, source_target_pairs={{0,128},{128,256},{256,384},{384,0},{1,129},{129,257},{257,385},{3... | collective-permute-start | bytes 589832 | tf_op jit(solution)/shard_map/ppermute | solution.py:278
  145.0 13.6 %collective-permute-start.10 = (bf16[768,128]{1,0:T(8,128)(2,1)S(1)}, bf16[768,128]{1,0:T(8,128)(2,1)S(1)}, u32[]{:S(2)}, u32[]{:S(2)}) collective-permute-start(bf16[768,128]{1,0:T(8,128)(2,1)S(1)} %constant_dynamic-update-slice_fusion.refs_0_), channel_id=1, source_target_pairs={{0,4},{4,0},{1,5},{5,1},{2,6},{6,2},{3,7},{7,3},{8,12},{12,8},{9,1... | collective-permute-start | bytes 589832 | tf_op jit(solution)/shard_map/ppermute | solution.py:278
  150.7 8.0 %collective-permute-start.13 = (bf16[768,128]{1,0:T(8,128)(2,1)S(1)}, bf16[768,128]{1,0:T(8,128)(2,1)S(1)}, u32[]{:S(2)}, u32[]{:S(2)}) collective-permute-start(bf16[768,128]{1,0:T(8,128)(2,1)S(1)} %collective-permute-done.9.refs_3_), channel_id=1, source_target_pairs={{0,4},{4,0},{1,5},{5,1},{2,6},{6,2},{3,7},{7,3},{8,12},{12,8},{9,1... | collective-permute-start | bytes 589832 | tf_op jit(solution)/shard_map/ppermute | solution.py:278
  152.6 6.0 %collective-permute-start.12 = (bf16[768,128]{1,0:T(8,128)(2,1)S(1)}, bf16[768,128]{1,0:T(8,128)(2,1)S(1)}, u32[]{:S(2)}, u32[]{:S(2)}) collective-permute-start(bf16[768,128]{1,0:T(8,128)(2,1)S(1)} %collective-permute-done.8.refs_2_), channel_id=1, source_target_pairs={{0,4},{4,0},{1,5},{5,1},{2,6},{6,2},{3,7},{7,3},{8,12},{12,8},{9,1... | collective-permute-start | bytes 589832 | tf_op jit(solution)/shard_map/ppermute | solution.py:278
  155.6 3.3 %collective-permute-start.11 = (bf16[768,128]{1,0:T(8,128)(2,1)S(1)}, bf16[768,128]{1,0:T(8,128)(2,1)S(1)}, u32[]{:S(2)}, u32[]{:S(2)}) collective-permute-start(bf16[768,128]{1,0:T(8,128)(2,1)S(1)} %collective-permute-done.7.refs_1_), channel_id=1, source_target_pairs={{0,4},{4,0},{1,5},{5,1},{2,6},{6,2},{3,7},{7,3},{8,12},{12,8},{9,1... | collective-permute-start | bytes 589832 | tf_op jit(solution)/shard_map/ppermute | solution.py:278
